TPU v7x, 32 devices: a whole 2x2x4 slice. The times are simulated.
32 devices in a mesh: row: 8 (over z, y), col: 4 (over x, core).
Axes of the slice: x: 2, y: 2, z: 4, core: 2. Of those that a mesh axis runs over, the one named last changes fastest.
Arguments:
- tokens: bfloat16 [6272, 2048], P('row', 'col'), may hold values from -6 to 6
- first_gain: float32 [1024], P('col'), may hold values from 0.1 to 1.9
- first_shift: float32 [1024], P('col'), may hold values from -1.5 to 1.5
- inward_weight: bfloat16 [1024, 3, 1024], P('row', None, 'col'), may hold values from -0.25 to 0.25
- attention_bias: float32 [2, 1024], P(None, 'col'), may hold values from -2.5 to 2.5
- output_weight: bfloat16 [1024, 1024], P('col', 'row'), may hold values from -2 to 2
- output_bias: float32 [1024], P('col'), may hold values from -2.5 to 2.5
- second_gain: float32 [1024], P('col'), may hold values from 0.1 to 1.9
- second_shift: float32 [1024], P('col'), may hold values from -1.5 to 1.5
- expand_weight: bfloat16 [1024, 4096], P('row', 'col'), may hold values from -0.1875 to 0.1875
- expand_bias: float32 [4096], P('col'), may hold values from -2.5 to 2.5
- reduce_weight: bfloat16 [4096, 1024], P('col', 'row'), may hold values from -0.125 to 0.125
- reduce_bias: float32 [1024], P('col'), may hold values from -2.5 to 2.5
- cotangent: bfloat16 [6272, 2048], P('row', 'col'), may hold values from -6 to 6
Outputs:
- layer_output: bfloat16 [6272, 2048], P('row', 'col')
- tokens_grad: float32 [6272, 2048], P('row', 'col')
- first_gain_grad: float32 [1024], P('col')
- first_shift_grad: float32 [1024], P('col')
- inward_grad: float32 [1024, 3, 1024], P('row', None, 'col')
- attention_bias_grad: float32 [2, 1024], P(None, 'col')
- output_grad: float32 [1024, 1024], P('col', 'row')
- output_bias_grad: float32 [1024], P('col')
- second_gain_grad: float32 [1024], P('col')
- second_shift_grad: float32 [1024], P('col')
- expand_grad: float32 [1024, 4096], P('row', 'col')
- expand_bias_grad: float32 [4096], P('col')
- reduce_grad: float32 [4096, 1024], P('col', 'row')
- reduce_bias_grad: float32 [1024], P('col')
All inputs are finite; a program needn't handle non-finite values.
Results may differ from a plain program's by a relative error of at most 0.015.
The roundings to bfloat16 on the way count: a program that leaves them out, or rounds other values in their place, can miss the bound.
Values may be sent and summed in bfloat16 or wider, within the bound.
A program may use at most 192 MiB of HBM per device.

v0:
```python
import jax
import jax.numpy as jnp
from jax import lax
from jax.sharding import PartitionSpec as P

HEAD_DIM = 64
SEQ = 1568


EPSILON = 1e-06
CONTRACT_ROWS = (((0,), (0,)), ((), ()))
CONTRACT_COLS = (((1,), (1,)), ((), ()))


def norm_forward(values, gain, shift, full_width):
    row_total = lax.psum(jnp.sum(values, axis=1), "col")
    centred = values - (row_total / full_width)[:, None]
    row_square = lax.psum(jnp.sum(centred * centred, axis=1), "col")
    inverse = lax.rsqrt(row_square / full_width + EPSILON)
    unit_rows = centred * inverse[:, None]
    return (unit_rows, inverse, unit_rows * gain + shift)


def norm_backward(incoming, unit_rows, inverse, gain, full_width):
    scaled = incoming * gain
    plain_sum, cross_sum = lax.psum(
        (jnp.sum(scaled, axis=1), jnp.sum(scaled * unit_rows, axis=1)), "col"
    )
    result = inverse[:, None] * (
        scaled - (plain_sum / full_width)[:, None] - unit_rows * (cross_sum / full_width)[:, None]
    )
    return (result, jnp.sum(incoming * unit_rows, axis=0), jnp.sum(incoming, axis=0))


def spread_features(values):
    return lax.all_gather(values, "col", axis=1, tiled=True)


def sum_partials(values):
    return lax.psum_scatter(values, "col", scatter_dimension=1, tiled=True)


def spread_grads(values):
    return lax.all_gather(values, "col", axis=1, tiled=True)


def sum_grad_partials(values):
    return lax.psum_scatter(values, "col", scatter_dimension=1, tiled=True)


def fetch_weights(inward_weight, output_weight, expand_weight, reduce_weight):
    return (
        lax.all_gather(inward_weight, "row", axis=0, tiled=True),
        lax.all_gather(output_weight, "row", axis=1, tiled=True),
        lax.all_gather(expand_weight, "row", axis=0, tiled=True),
        lax.all_gather(reduce_weight, "row", axis=1, tiled=True),
    )


def attend_clip(queries, key_rows, value_rows, score_scale):
    seq_len = queries.shape[0]
    blocks = queries.reshape((2, seq_len // 2) + queries.shape[1:])

    def one_block(query_part):
        scores = (
            jnp.einsum("qhd,khd->hqk", query_part, key_rows, preferred_element_type=jnp.float32)
            * score_scale
        )
        row_peak = jnp.max(scores, axis=-1, keepdims=True)
        exponent = jnp.exp(scores - row_peak)
        row_sum = jnp.sum(exponent, axis=-1, keepdims=True)
        prob_low = (exponent / row_sum).astype(jnp.bfloat16)
        mixed_rows = jnp.einsum(
            "hqk,khd->qhd", prob_low, value_rows, preferred_element_type=jnp.float32
        )
        return (mixed_rows, (row_peak + jnp.log(row_sum))[..., 0])

    mixed_rows, logsum = lax.map(one_block, blocks)
    return (mixed_rows.reshape(queries.shape), logsum)


def attend_clip_back(queries, key_rows, value_rows, logsum, grad_out, score_scale):
    seq_len = queries.shape[0]
    block_shape = (2, seq_len // 2) + queries.shape[1:]

    def step_block(carry, pieces):
        key_acc, value_acc = carry
        query_part, grad_part, log_part = pieces
        scores = (
            jnp.einsum("qhd,khd->hqk", query_part, key_rows, preferred_element_type=jnp.float32)
            * score_scale
        )
        probs = jnp.exp(scores - log_part[..., None])
        grad_probs = jnp.einsum(
            "qhd,khd->hqk", grad_part, value_rows, preferred_element_type=jnp.float32
        )
        inner_sum = jnp.sum(probs * grad_probs, axis=-1, keepdims=True)
        grad_scores = (probs * (grad_probs - inner_sum)).astype(jnp.bfloat16)
        query_grad = (
            jnp.einsum("hqk,khd->qhd", grad_scores, key_rows, preferred_element_type=jnp.float32)
            * score_scale
        )
        key_acc = key_acc + jnp.einsum(
            "hqk,qhd->khd", grad_scores, query_part, preferred_element_type=jnp.float32
        )
        value_acc = value_acc + jnp.einsum(
            "hqk,qhd->khd",
            probs.astype(jnp.bfloat16),
            grad_part,
            preferred_element_type=jnp.float32,
        )
        return ((key_acc, value_acc), query_grad)

    zero_acc = jnp.zeros(key_rows.shape, jnp.float32)
    (key_acc, value_acc), query_grads = lax.scan(
        step_block,
        (zero_acc, zero_acc),
        (queries.reshape(block_shape), grad_out.reshape(block_shape), logsum),
    )
    return (query_grads.reshape(queries.shape), key_acc * score_scale, value_acc)


def forward_pass(
    tokens,
    first_gain,
    first_shift,
    attention_bias,
    output_bias,
    second_gain,
    second_shift,
    expand_bias,
    reduce_bias,
    gathered,
):
    inward_all, output_rows, expand_all, reduce_rows = gathered
    full_width = inward_all.shape[0]
    local_width = inward_all.shape[2]
    row_count = tokens.shape[0]
    clip_shape = (row_count // SEQ, SEQ, local_width // HEAD_DIM, HEAD_DIM)
    score_scale = HEAD_DIM ** (-0.5)
    source = tokens.astype(jnp.float32)
    unit_one, inverse_one, normed_one = norm_forward(source, first_gain, first_shift, full_width)
    normed_all = spread_features(normed_one.astype(jnp.bfloat16))
    projected = jnp.dot(
        normed_all,
        inward_all.reshape(full_width, 3 * local_width),
        preferred_element_type=jnp.float32,
    )
    projected = projected.reshape(row_count, 3, local_width)
    queries = (projected[:, 0] + attention_bias[0]).astype(jnp.bfloat16)
    key_rows = projected[:, 1].astype(jnp.bfloat16)
    value_rows = (projected[:, 2] + attention_bias[1]).astype(jnp.bfloat16)
    mixed_rows, logsum = lax.map(
        lambda clip_parts: attend_clip(clip_parts[0], clip_parts[1], clip_parts[2], score_scale),
        (queries.reshape(clip_shape), key_rows.reshape(clip_shape), value_rows.reshape(clip_shape)),
    )
    mixed_low = mixed_rows.reshape(row_count, local_width).astype(jnp.bfloat16)
    hidden_state = (
        source
        + sum_partials(jnp.dot(mixed_low, output_rows, preferred_element_type=jnp.float32))
        + output_bias
    )
    unit_two, inverse_two, normed_two = norm_forward(
        hidden_state, second_gain, second_shift, full_width
    )
    normed_all_two = spread_features(normed_two.astype(jnp.bfloat16))
    expanded = jnp.dot(normed_all_two, expand_all, preferred_element_type=jnp.float32) + expand_bias
    activated = jax.nn.gelu(expanded, approximate=False).astype(jnp.bfloat16)
    output_value = (
        hidden_state
        + sum_partials(jnp.dot(activated, reduce_rows, preferred_element_type=jnp.float32))
        + reduce_bias
    )
    saved_state = (
        unit_one,
        inverse_one,
        normed_all,
        queries,
        key_rows,
        value_rows,
        logsum,
        mixed_low,
        unit_two,
        inverse_two,
        normed_all_two,
        expanded,
        activated,
    )
    return (output_value, saved_state)


def per_device(
    tokens,
    first_gain,
    first_shift,
    inward_weight,
    attention_bias,
    output_weight,
    output_bias,
    second_gain,
    second_shift,
    expand_weight,
    expand_bias,
    reduce_weight,
    reduce_bias,
    cotangent,
):
    packed_width = tokens.shape[1]
    tokens = tokens.reshape(-1, packed_width // 2)
    cotangent = cotangent.reshape(-1, packed_width // 2)
    gathered = fetch_weights(inward_weight, output_weight, expand_weight, reduce_weight)
    output_value, saved_state = forward_pass(
        tokens,
        first_gain,
        first_shift,
        attention_bias,
        output_bias,
        second_gain,
        second_shift,
        expand_bias,
        reduce_bias,
        gathered,
    )
    gathered = fetch_weights(inward_weight, output_weight, expand_weight, reduce_weight)
    unused_value, saved_state = forward_pass(
        tokens,
        first_gain,
        first_shift,
        attention_bias,
        output_bias,
        second_gain,
        second_shift,
        expand_bias,
        reduce_bias,
        gathered,
    )
    inward_all, output_rows, expand_all, reduce_rows = gathered
    (
        unit_one,
        inverse_one,
        normed_all,
        queries,
        key_rows,
        value_rows,
        logsum,
        mixed_low,
        unit_two,
        inverse_two,
        normed_all_two,
        expanded,
        activated,
    ) = saved_state
    full_width = inward_all.shape[0]
    local_width = inward_all.shape[2]
    row_count = tokens.shape[0]
    clip_shape = (row_count // SEQ, SEQ, local_width // HEAD_DIM, HEAD_DIM)
    score_scale = HEAD_DIM ** (-0.5)
    grad_rows = cotangent.astype(jnp.float32)
    grad_all = spread_grads(cotangent)
    grad_act = lax.dot_general(
        grad_all, reduce_rows, CONTRACT_COLS, preferred_element_type=jnp.float32
    )
    reduce_grad = lax.dot_general(
        activated, grad_all, CONTRACT_ROWS, preferred_element_type=jnp.float32
    )
    reduce_bias_grad = jnp.sum(grad_rows, axis=0)
    gelu_value, gelu_back = jax.vjp(
        lambda inner_value: jax.nn.gelu(inner_value, approximate=False), expanded
    )
    grad_expanded = gelu_back(grad_act)[0].astype(jnp.bfloat16)
    expand_grad = lax.dot_general(
        normed_all_two, grad_expanded, CONTRACT_ROWS, preferred_element_type=jnp.float32
    )
    expand_bias_grad = jnp.sum(grad_expanded.astype(jnp.float32), axis=0)
    grad_normed_two = sum_grad_partials(
        lax.dot_general(
            grad_expanded, expand_all, CONTRACT_COLS, preferred_element_type=jnp.float32
        )
    )
    back_two, second_gain_grad, second_shift_grad = norm_backward(
        grad_normed_two, unit_two, inverse_two, second_gain, full_width
    )
    grad_hidden = grad_rows + back_two
    grad_hidden_low = grad_hidden.astype(jnp.bfloat16)
    grad_hidden_all = spread_grads(grad_hidden_low)
    output_grad = lax.dot_general(
        mixed_low, grad_hidden_all, CONTRACT_ROWS, preferred_element_type=jnp.float32
    )
    output_bias_grad = jnp.sum(grad_hidden_low.astype(jnp.float32), axis=0)
    grad_mixed = lax.dot_general(
        grad_hidden_all, output_rows, CONTRACT_COLS, preferred_element_type=jnp.float32
    ).astype(jnp.bfloat16)
    query_grads, key_grads, value_grads = lax.map(
        lambda clip_parts: attend_clip_back(
            clip_parts[0], clip_parts[1], clip_parts[2], clip_parts[3], clip_parts[4], score_scale
        ),
        (
            queries.reshape(clip_shape),
            key_rows.reshape(clip_shape),
            value_rows.reshape(clip_shape),
            logsum,
            grad_mixed.reshape(clip_shape),
        ),
    )
    stacked = jnp.stack(
        [
            query_grads.reshape(row_count, local_width),
            key_grads.reshape(row_count, local_width),
            value_grads.reshape(row_count, local_width),
        ],
        axis=1,
    ).astype(jnp.bfloat16)
    attention_bias_grad = jnp.stack(
        [
            jnp.sum(stacked[:, 0].astype(jnp.float32), axis=0),
            jnp.sum(stacked[:, 2].astype(jnp.float32), axis=0),
        ]
    )
    flat_grads = stacked.reshape(row_count, 3 * local_width)
    inward_grad = lax.dot_general(
        normed_all, flat_grads, CONTRACT_ROWS, preferred_element_type=jnp.float32
    ).reshape(full_width, 3, local_width)
    grad_normed_one = sum_grad_partials(
        lax.dot_general(
            flat_grads,
            inward_all.reshape(full_width, 3 * local_width),
            CONTRACT_COLS,
            preferred_element_type=jnp.float32,
        )
    )
    back_one, first_gain_grad, first_shift_grad = norm_backward(
        grad_normed_one, unit_one, inverse_one, first_gain, full_width
    )
    tokens_grad = grad_hidden + back_one
    inward_grad, output_grad, expand_grad, reduce_grad = (
        lax.psum_scatter(
            inward_grad.astype(jnp.bfloat16), "row", scatter_dimension=0, tiled=True
        ).astype(jnp.float32),
        lax.psum_scatter(
            output_grad.astype(jnp.bfloat16), "row", scatter_dimension=1, tiled=True
        ).astype(jnp.float32),
        lax.psum_scatter(
            expand_grad.astype(jnp.bfloat16), "row", scatter_dimension=0, tiled=True
        ).astype(jnp.float32),
        lax.psum_scatter(
            reduce_grad.astype(jnp.bfloat16), "row", scatter_dimension=1, tiled=True
        ).astype(jnp.float32),
    )
    (
        first_gain_grad,
        first_shift_grad,
        attention_bias_grad,
        output_bias_grad,
        second_gain_grad,
        second_shift_grad,
        expand_bias_grad,
        reduce_bias_grad,
    ) = lax.psum(
        (
            first_gain_grad,
            first_shift_grad,
            attention_bias_grad,
            output_bias_grad,
            second_gain_grad,
            second_shift_grad,
            expand_bias_grad,
            reduce_bias_grad,
        ),
        "row",
    )
    return (
        output_value.astype(jnp.bfloat16).reshape(-1, packed_width),
        tokens_grad.reshape(-1, packed_width),
        first_gain_grad,
        first_shift_grad,
        inward_grad,
        attention_bias_grad,
        output_grad,
        output_bias_grad,
        second_gain_grad,
        second_shift_grad,
        expand_grad,
        expand_bias_grad,
        reduce_grad,
        reduce_bias_grad,
    )


def solution(mesh):
    in_specs = (
        P("row", "col"),
        P("col"),
        P("col"),
        P("row", None, "col"),
        P(None, "col"),
        P("col", "row"),
        P("col"),
        P("col"),
        P("col"),
        P("row", "col"),
        P("col"),
        P("col", "row"),
        P("col"),
        P("row", "col"),
    )
    out_specs = (
        P("row", "col"),
        P("row", "col"),
        P("col"),
        P("col"),
        P("row", None, "col"),
        P(None, "col"),
        P("col", "row"),
        P("col"),
        P("col"),
        P("col"),
        P("row", "col"),
        P("col"),
        P("col", "row"),
        P("col"),
    )
    return jax.shard_map(
        per_device, mesh=mesh, in_specs=in_specs, out_specs=out_specs, check_vma=False
    )
```

profile of v0, /device:TPU:0, one launch (start us, length us, event | category | flops | bytes accessed | tf_op | source)
XLA Modules:
  0.0 1172.6 jit_solution(17945256681787545454)
XLA Ops:
  27.5 32.0 %all_gather.34 = bf16[256,1024]{1,0:T(8,128)(2,1)} all-gather(bf16[256,128]{1,0:T(8,128)(2,1)S(1)} %copy-done.18), channel_id=1, replica_groups=mesh['row'=8,'col'=4] {'row'}, dimensions={1}, use_global_device_ids=true | all-gather | bytes 589824 | tf_op jit(solution)/shard_map/all_gather | solution.py:54
  63.6 29.1 %all-gather.9.cloned.1.call-done = bf16[1568,1024]{1,0:T(8,128)(2,1)} async-done(((bf16[1568,256]{1,0:T(8,128)(2,1)}), bf16[1568,1024]{1,0:T(8,128)(2,1)}) %all-gather.9.cloned.1.call-update) | async-done | bytes 3211280 | tf_op jit(solution)/shard_map/all_gather | solution.py:36
  109.3 34.2 %while.64 = (s32[]{:T(128)}, bf16[2,784,4,64]{1,3,2,0:T(8,128)(2,1)S(1)}, bf16[2,784,4,64]{1,3,2,0:T(8,128)(2,1)}, bf16[1568,4,64]{0,2,1:T(8,128)(2,1)}, bf16[1568,4,64]{0,2,1:T(8,128)(2,1)}, /*index=5*/s32[]{:T(128)}) while((s32[]{:T(128)}, bf16[2,784,4,64]{1,3,2,0:T(8,128)(2,1)S(1)}, bf16[2,784,4,64]{1,3,2,0:T(8,128)(2,1)}, ...), condition=%wide.region_7.0_spmd, body=%wide.region_4.7_spmd.sunk | while | flops 1922650112 | bytes 4304209 | solution.py:78
  149.9 30.1 %while.65 = (s32[]{:T(128)}, bf16[2,784,4,64]{1,3,2,0:T(8,128)(2,1)}, f32[2,4,784]{2,1,0:T(4,128)S(1)}, bf16[2,784,4,64]{1,3,2,0:T(8,128)(2,1)}, bf16[1568,4,64]...) while((s32[]{:T(128)}, bf16[2,784,4,64]{1,3,2,0:T(8,128)(2,1)}, ...), condition=%wide.region_17.18_spmd, body=%wide.region_14.17_spmd.sunk | while | flops 1303067648 | bytes 62078304 | solution.py:78
  188.6 19.6 %reduce-scatter.14.cloned.1.call-done = f32[1568,256]{1,0:T(8,128)} async-done(((f32[1568,1024]{1,0:T(8,128)}), f32[1568,256]{1,0:T(8,128)}) %reduce-scatter.14.cloned.1.call-update) | async-done | bytes 1605648 | tf_op jit(solution)/shard_map/reduce_scatter | solution.py:40
  208.2 61.8 %reduce-scatter.18.cloned.1.call-done = f32[1568,256]{1,0:T(8,128)} async-done(((f32[1568,1024]{1,0:T(8,128)}), f32[1568,256]{1,0:T(8,128)}) %reduce-scatter.18.cloned.1.call-update) | async-done | bytes 1605648 | tf_op jit(solution)/shard_map/reduce_scatter | solution.py:40
  291.0 30.4 %all-gather.15.cloned.1.call-done = bf16[1024,1024]{1,0:T(8,128)(2,1)} async-done(((bf16[128,1024]{1,0:T(8,128)(2,1)}), bf16[1024,1024]{1,0:T(8,128)(2,1)}) %all-gather.15.cloned.1.call-update) | async-done | bytes 2097168 | tf_op jit(solution)/shard_map/all_gather | solution.py:55
  321.3 29.8 %all-gather.19.cloned.1.call-done = bf16[1568,1024]{1,0:T(8,128)(2,1)} async-done(((bf16[1568,256]{1,0:T(8,128)(2,1)}), bf16[1568,1024]{1,0:T(8,128)(2,1)}) %all-gather.19.cloned.1.call-update) | async-done | bytes 3211280 | tf_op jit(solution)/shard_map/all_gather | solution.py:36
  359.8 44.5 %all-gather.17.cloned.1.call-done = bf16[1024,1024]{1,0:T(8,128)(2,1)} async-done(((bf16[1024,128]{1,0:T(8,128)(2,1)}), bf16[1024,1024]{1,0:T(8,128)(2,1)}) %all-gather.17.cloned.1.call-update) | async-done | bytes 2097168 | tf_op jit(solution)/shard_map/all_gather | solution.py:56
  404.3 29.1 %all-gather.21.cloned.1.call-done = bf16[1568,1024]{1,0:T(8,128)(2,1)} async-done(((bf16[1568,256]{1,0:T(8,128)(2,1)}), bf16[1568,1024]{1,0:T(8,128)(2,1)}) %all-gather.21.cloned.1.call-update) | async-done | bytes 3211280 | tf_op jit(solution)/shard_map/all_gather | solution.py:44
  433.4 22.4 %convert_reduce_fusion = (f32[1024]{0:T(1024)}, bf16[1568,1024]{1,0:T(8,128)(2,1)S(1)}, f32[1568,1024]{1,0:T(8,128)}) fusion(f32[1568,1024]{1,0:T(8,128)} %fusion.142, f32[1024]{0:T(1024)S(1)} %copy-done.34, bf16[1568,1024]{1,0:T(8,128)(2,1)} %all-gather.21.cloned.1.call-done, bf16[1024,1024]{1,0:T(8,128)(2,1)} %all-gather.17.cloned.1.call-done), kind=kOutput, calls=%fused_computation.69 | convolution fusion | flops 3408755712 | bytes 21372928 | tf_op jit(solution)/shard_map/dot_general | solution.py:260
  463.2 59.1 %reduce-scatter.20.cloned.1.call-done = f32[1568,256]{1,0:T(8,128)} async-done(((f32[1568,1024]{1,0:T(8,128)}), f32[1568,256]{1,0:T(8,128)}) %reduce-scatter.20.cloned.1.call-update) | async-done | bytes 1605648 | tf_op jit(solution)/shard_map/reduce_scatter | solution.py:48
  539.5 31.0 %all-gather.23.cloned.1.call-done = bf16[1568,1024]{1,0:T(8,128)(2,1)} async-done(((bf16[1568,256]{1,0:T(8,128)(2,1)}), bf16[1568,1024]{1,0:T(8,128)(2,1)}) %all-gather.23.cloned.1.call-update) | async-done | bytes 3211280 | tf_op jit(solution)/shard_map/all_gather | solution.py:44
  578.2 129.4 %while.66 = (s32[]{:T(128)}, f32[1568,4,64]{0,2,1:T(8,128)}, f32[1568,4,64]{0,2,1:T(8,128)}, bf16[2,784,4,64]{1,3,2,0:T(8,128)(2,1)}, bf16[2,784,4,64]{1,3,2,0:T...) while((s32[]{:T(128)}, f32[1568,4,64]{0,2,1:T(8,128)}, ...), condition=%wide.region_30.31_spmd.clone, body=%wide.region_28.30_spmd.clone.sunk | while | flops 3188179968 | bytes 291960320 | solution.py:115
  603.2 18.2 %multiply_convert_fusion.6 = bf16[4,784,1568]{2,1,0:T(8,128)(2,1)} fusion(f32[4,784,1568]{2,1,0:T(8,128)} %get-tuple-element.495, f32[4,784,1568]{2,1,0:T(8,128)} %fusion.222, f32[4,784]{1,0:T(4,128)S(1)} %get-tuple-element.496), kind=kLoop, calls=%fused_computation.36.clone.1 | loop fusion | flops 14751744 | bytes 49185024 | tf_op jit(solution)/shard_map/while/body/eval_jaxpr/while/body/eval_jaxpr/convert_element_type | solution.py:98
  667.6 18.2 %multiply_convert_fusion.6 = bf16[4,784,1568]{2,1,0:T(8,128)(2,1)} fusion(f32[4,784,1568]{2,1,0:T(8,128)} %get-tuple-element.495, f32[4,784,1568]{2,1,0:T(8,128)} %fusion.222, f32[4,784]{1,0:T(4,128)S(1)} %get-tuple-element.496), kind=kLoop, calls=%fused_computation.36.clone.1 | loop fusion | flops 14751744 | bytes 49185024 | tf_op jit(solution)/shard_map/while/body/eval_jaxpr/while/body/eval_jaxpr/convert_element_type | solution.py:98
  726.2 57.5 %reduce-scatter.22.cloned.1.call-done = f32[1568,256]{1,0:T(8,128)} async-done(((f32[1568,1024]{1,0:T(8,128)}), f32[1568,256]{1,0:T(8,128)}) %reduce-scatter.22.cloned.1.call-update) | async-done | bytes 1605648 | tf_op jit(solution)/shard_map/reduce_scatter | solution.py:48
  835.6 23.6 %fusion.94 = f32[1568,1024]{1,0:T(8,128)} fusion(bf16[1024,1024]{1,0:T(8,128)(2,1)} %all-gather.17.cloned.1.call-done, bf16[1568,1024]{1,0:T(8,128)(2,1)} %all-gather.13.cloned.1.call-done, bf16[1024,1024]{1,0:T(8,128)(2,1)} %all-gather.15.cloned.1.call-done, f32[1024]{0:T(1024)S(1)} %copy-done.35), kind=kOutput, calls=%fused_computation.110 | convolution fusion | flops 6682640384 | bytes 13832192 | tf_op jit(solution)/shard_map/dot_general | solution.py:171
  859.2 40.4 %reduce-scatter.30.cloned.1.call-done = bf16[128,1024]{1,0:T(8,128)(2,1)} async-done(((bf16[1024,1024]{1,0:T(8,128)(2,1)}), bf16[128,1024]{1,0:T(8,128)(2,1)}) %reduce-scatter.30.cloned.1.call-update) | async-done | bytes 262160
  901.6 68.0 %reduce-scatter.26.cloned.1.call-done = bf16[128,1024]{1,0:T(8,128)(2,1)} async-done(((bf16[1024,1024]{1,0:T(8,128)(2,1)}), bf16[128,1024]{1,0:T(8,128)(2,1)}) %reduce-scatter.26.cloned.1.call-update) | async-done | bytes 262160 | tf_op jit(solution)/shard_map/reduce_scatter | solution.py:342
  973.0 60.7 %reduce-scatter.28.cloned.1.call-done = bf16[128,256]{1,0:T(8,128)(2,1)} async-done(((bf16[1024,256]{1,0:T(8,128)(2,1)}), bf16[128,256]{1,0:T(8,128)(2,1)}) %reduce-scatter.28.cloned.1.call-update) | async-done | bytes 65552
  1035.3 67.2 %reduce-scatter.24.cloned.1.call-done = bf16[128,3,256]{2,0,1:T(8,128)(2,1)} async-done(((bf16[1024,3,256]{2,0,1:T(8,128)(2,1)}), bf16[128,3,256]{2,0,1:T(8,128)(2,1)}) %reduce-scatter.24.cloned.1.call-update) | async-done | bytes 196624 | tf_op jit(solution)/shard_map/reduce_scatter | solution.py:336
  1110.3 35.2 %all-reduce = (f32[256]{0:T(256)}, f32[256]{0:T(256)}, f32[2,256]{1,0:T(2,128)}, f32[256]{0:T(256)}, f32[256]{0:T(256)}, /*index=5*/f32[256]{0:T(256)}, f32[1024]{0:T(1024)}, f32[256]{0:T(256)}) all-reduce(f32[256]{0:T(256)S(1)} %get-tuple-element.281, f32[256]{0:T(256)S(1)} %get-tuple-element.288, ...), channel_id=1, replica_groups=mesh['row'=8,'col'=4] {'row'}, use_global_device_ids=true, to_apply=%region_37.38 | all-reduce | flops 3072 | bytes 24576 | tf_op jit(solution)/shard_map/psum | solution.py:358
  1145.5 17.6 %reduce-scatter.16.cloned.1.call-done = f32[1568,256]{1,0:T(8,128)} async-done(((f32[1568,1024]{1,0:T(8,128)}), f32[1568,256]{1,0:T(8,128)}) %reduce-scatter.16.cloned.1.call-update) | async-done | bytes 1605648 | tf_op jit(solution)/shard_map/reduce_scatter | solution.py:40
  (226 shorter events, 361.8 us)
Async XLA Ops:
  7.2 54.7 %all-gather.11.cloned.1.call-start = ((), (), s32[]{:S(2)}) async-start(), calls=%async_computation.10 | async-start | bytes 1769472 | tf_op jit(solution)/shard_map/all_gather | solution.py:53
  7.9 84.8 %all-gather.9.cloned.1.call-start = ((), (), s32[]{:S(2)}) async-start(), calls=%async_computation.9 | async-start | bytes 4014080 | tf_op jit(solution)/shard_map/all_gather | solution.py:36
  27.2 180.9 %reduce-scatter.14.cloned.1.call-start = ((), (), s32[]{:S(2)}) async-start(), calls=%async_computation.11 | async-start | bytes 8028160 | tf_op jit(solution)/shard_map/reduce_scatter | solution.py:40
  148.8 121.2 %reduce-scatter.18.cloned.1.call-start = ((), (), s32[]{:S(2)}) async-start(), calls=%async_computation.16 | async-start | bytes 8028160 | tf_op jit(solution)/shard_map/reduce_scatter | solution.py:40
  187.9 133.4 %all-gather.15.cloned.1.call-start = ((), (), s32[]{:S(2)}) async-start(), calls=%async_computation.13 | async-start | bytes 2359296 | tf_op jit(solution)/shard_map/all_gather | solution.py:55
  188.5 162.6 %all-gather.19.cloned.1.call-start = ((), (), s32[]{:S(2)}) async-start(), calls=%async_computation.17 | async-start | bytes 4014080 | tf_op jit(solution)/shard_map/all_gather | solution.py:36
  288.0 116.3 %all-gather.17.cloned.1.call-start = ((), (), s32[]{:S(2)}) async-start(), calls=%async_computation.14 | async-start | bytes 2359296 | tf_op jit(solution)/shard_map/all_gather | solution.py:56
  288.7 144.6 %all-gather.21.cloned.1.call-start = ((), (), s32[]{:S(2)}) async-start(), calls=%async_computation.18 | async-start | bytes 4014080 | tf_op jit(solution)/shard_map/all_gather | solution.py:44
  290.9 142.5 %copy-start.34 = (f32[1024]{0:T(1024)S(1)}, f32[1024]{0:T(1024)}, u32[]{:S(2)}) copy-start(f32[1024]{0:T(1024)} %param.30) | copy-start | bytes 12292
  290.9 231.4 %reduce-scatter.20.cloned.1.call-start = ((), (), s32[]{:S(2)}) async-start(), calls=%async_computation.19 | async-start | bytes 8028160 | tf_op jit(solution)/shard_map/reduce_scatter | solution.py:48
  463.0 107.6 %all-gather.23.cloned.1.call-start = ((), (), s32[]{:S(2)}) async-start(), calls=%async_computation.20 | async-start | bytes 4014080 | tf_op jit(solution)/shard_map/all_gather | solution.py:44
  539.5 244.3 %reduce-scatter.22.cloned.1.call-start = ((), (), s32[]{:S(2)}) async-start(), calls=%async_computation.21 | async-start | bytes 8028160 | tf_op jit(solution)/shard_map/reduce_scatter | solution.py:48
  724.4 111.2 %all-gather.13.cloned.1.call-start = ((), (), s32[]{:S(2)}) async-start(), calls=%async_computation.12 | async-start | bytes 4014080 | tf_op jit(solution)/shard_map/all_gather | solution.py:36
  797.8 101.7 %reduce-scatter.30.cloned.1.call-start = ((), (), s32[]{:S(2)}) async-start(), calls=%async_computation.25 | async-start | bytes 2359296
  813.3 156.2 %reduce-scatter.26.cloned.1.call-start = ((), (), s32[]{:S(2)}) async-start(), calls=%async_computation.23 | async-start | bytes 2359296 | tf_op jit(solution)/shard_map/reduce_scatter | solution.py:342
  822.1 211.5 %reduce-scatter.28.cloned.1.call-start = ((), (), s32[]{:S(2)}) async-start(), calls=%async_computation.24 | async-start | bytes 589824
  828.3 274.1 %reduce-scatter.24.cloned.1.call-start = ((), (), s32[]{:S(2)}) async-start(), calls=%async_computation.22 | async-start | bytes 1769472 | tf_op jit(solution)/shard_map/reduce_scatter | solution.py:336
  835.3 327.8 %reduce-scatter.16.cloned.1.call-start = ((), (), s32[]{:S(2)}) async-start(), calls=%async_computation.15 | async-start | bytes 8028160 | tf_op jit(solution)/shard_map/reduce_scatter | solution.py:40
  901.5 208.8 %copy-start.25 = (f32[256]{0:T(256)S(1)}, f32[256]{0:T(256)}, u32[]{:S(2)}) copy-start(f32[256]{0:T(256)} %get-tuple-element.279) | copy-start | bytes 3076
  901.5 208.8 %copy-start.26 = (f32[256]{0:T(256)S(1)}, f32[256]{0:T(256)}, u32[]{:S(2)}) copy-start(f32[256]{0:T(256)} %get-tuple-element.287) | copy-start | bytes 3076
  901.5 208.8 %copy-start.27 = (f32[256]{0:T(256)S(1)}, f32[256]{0:T(256)}, u32[]{:S(2)}) copy-start(f32[256]{0:T(256)} %get-tuple-element.348) | copy-start | bytes 3076
  901.5 208.8 %copy-start.28 = (f32[256]{0:T(256)S(1)}, f32[256]{0:T(256)}, u32[]{:S(2)}) copy-start(f32[256]{0:T(256)} %get-tuple-element.363) | copy-start | bytes 3076
  901.5 208.8 %copy-start.29 = (f32[1024]{0:T(1024)S(1)}, f32[1024]{0:T(1024)}, u32[]{:S(2)}) copy-start(f32[1024]{0:T(1024)} %get-tuple-element.345) | copy-start | bytes 12292
  901.5 261.6 %copy-start.32 = (f32[256]{0:T(256)S(1)}, f32[256]{0:T(256)}, u32[]{:S(2)}) copy-start(f32[256]{0:T(256)} %param.32) | copy-start | bytes 3076
  (34 other events, 1336.4 us)
Sparse Core Ops, SparseCore 0:
  10.2 51.6 all-gather.10
  64.0 28.6 all-gather.8
  148.9 59.2 reduce-scatter.13
  210.8 59.2 reduce-scatter.17
  272.0 49.2 all-gather.14
  323.3 27.7 all-gather.18
  353.2 51.0 all-gather.16
  405.8 27.4 all-gather.20
  463.1 59.2 reduce-scatter.19
  539.6 30.9 all-gather.22
  724.5 59.2 reduce-scatter.21
  798.0 30.3 all-gather.12
  831.9 67.6 reduce-scatter.29
  902.9 66.5 reduce-scatter.25
  972.7 60.8 reduce-scatter.27
  1037.9 64.4 reduce-scatter.23
  1104.9 58.2 reduce-scatter.15
where the time goes:
time: 1180 us; the launch traced here: 1170 us
  waiting for transfers between devices  650 us (55%)
  matrix products  250 us (21%)
  blocking collectives  114 us (10%)
  other arithmetic  79.1 us (7%)
  local copies, waits for them, and re-layouts  61.6 us (5%)
  between operations  14.8 us (1%)
    reduce_scatter x2, waiting for transfers between devices, sum_grad_partials(): return lax.psum_scatter(values, 'col', scatter_dimension=1, tiled=True)  117 us
    unnamed x19, waiting for transfers between devices  103 us
    reduce_scatter x3, waiting for transfers between devices, sum_partials(): return lax.psum_scatter(values, 'col', scatter_dimension=1, tiled=True)  99.1 us
    reduce_scatter x1, waiting for transfers between devices, per_device(): lax.psum_scatter(expand_grad.astype(jnp.bfloat16), 'row', scatter_dimensi...  68 us
    reduce_scatter x1, waiting for transfers between devices, per_device(): lax.psum_scatter(inward_grad.astype(jnp.bfloat16), 'row', scatter_dimensi...  67.2 us
    all_gather x2, waiting for transfers between devices, spread_grads(): return lax.all_gather(values, 'col', axis=1, tiled=True)  60.1 us
    all_gather x3, waiting for transfers between devices, spread_features(): return lax.all_gather(values, 'col', axis=1, tiled=True)  58.9 us
    all_gather x1, waiting for transfers between devices, fetch_weights(): lax.all_gather(reduce_weight, 'row', axis=1, tiled=True)  44.5 us
  transfers between devices with their start and end apart: 17, of which 16 were waited for; matrix products, arithmetic and copies ran while one was open for 12% of the time, Pallas kernels for 0%

commit v1 on v0

--- a/solution.py
+++ b/solution.py
@@ -1,13 +1,954 @@
+import functools
 import jax
 import jax.numpy as jnp
 from jax import lax
+from jax.experimental import pallas as pl
+from jax.experimental.pallas import tpu as pltpu
 from jax.sharding import PartitionSpec as P
 
 HEAD_DIM = 64
 SEQ = 1568
-
-
 EPSILON = 1e-06
+CHUNKS = 7
+F32 = jnp.float32
+BF16 = jnp.bfloat16
+MESH = pl.DeviceIdType.MESH
+LOG2E = 1.4426950408889634
+NT_DIMS = (((1,), (1,)), ((), ()))
+TN_DIMS = (((0,), (0,)), ((), ()))
+
+
+def remote(src, dst, send, recv, row, col):
+    return pltpu.make_async_remote_copy(
+        src_ref=src, dst_ref=dst, send_sem=send, recv_sem=recv,
+        device_id=(row, col), device_id_type=MESH,
+    )
+
+
+def aligned(index, size):
+    return pl.ds(pl.multiple_of(index * size, size), size)
+
+
+def row_norm(values):
+    mean = jnp.mean(values, axis=1, keepdims=True)
+    centred = values - mean
+    inverse = lax.rsqrt(jnp.mean(centred * centred, axis=1, keepdims=True) + EPSILON)
+    return centred * inverse, mean, inverse
+
+
+def weight_blocks(ref, kind, row):
+    if kind == "rows":
+        return ref.at[aligned(row, 128), :]
+    return ref.at[:, aligned(row, 128)]
+
+
+WEIGHT_KINDS = ("rows", "cols", "rows", "cols")
+
+
+def forward_kernel(
+    tok, cot, vec, attn_bias, exp_bias, win_s, wo_s, we_s, wr_s,
+    tok_o, cot_o, q_o, qt_o, k_o, kt_o, v_o, mixf_o, lse_o, hid_o, unit_o, inv_o,
+    norm_o, act_o, slope_o, win_o, wo_o, we_o, wr_o, vec_o, one_o, stat_o,
+    tok_all, cot_all, norm_one, q, qt, k, kt, v, vt, mixed, mixf, lse, hid, unit, inv, norm_two, act, slope,
+    win, wo, we, wr, vecs, stat, scores, sb, rb, xb, xr,
+    local_sem, wz_send, wz_recv, wy_send, wy_recv, vec_send, vec_recv,
+    tx_send, tx_recv, tc_send, tc_recv, cx_send, cx_recv, cc_send, cc_recv,
+    h1_send, h1_recv, h2_send, h2_recv, h3_send, h3_recv,
+):
+    r, c = lax.axis_index("row"), lax.axis_index("col")
+    z, y = r // 2, r % 2
+    xx, core = c // 2, c % 2
+    c_x, c_core, c_far = (c + 2) % 4, c + 1 - 2 * core, (c + 2) % 4 + 1 - 2 * core
+    r_y = r + 1 - 2 * y
+    z_peers = [((z + step) % 4) * 2 + y for step in (1, 2, 3)]
+    half = tok.shape[0] // CHUNKS
+    chunk = 2 * half
+    width = vec.shape[1]
+    scale = LOG2E * HEAD_DIM ** (-0.5)
+
+    barrier = pltpu.get_barrier_semaphore()
+    for col in (c_x, c_core, c_far):
+        pl.semaphore_signal(barrier, inc=1, device_id=(r, col), device_id_type=MESH)
+    for row in (r_y, *z_peers):
+        pl.semaphore_signal(barrier, inc=1, device_id=(row, c), device_id_type=MESH)
+
+    own = aligned(c, width)
+    for i in range(CHUNKS):
+        for s in range(2):
+            rows = pl.ds(i * half, half)
+            tok_all[i, s * half : (s + 1) * half, own] = tok[rows, s * width : (s + 1) * width]
+            cot_all[i, s * half : (s + 1) * half, own] = cot[rows, s * width : (s + 1) * width]
+    vecs[:, own] = vec[...]
+    shards = (win_s, wo_s, we_s, wr_s)
+    fulls = (win, wo, we, wr)
+    for w in range(4):
+        weight_blocks(fulls[w], WEIGHT_KINDS[w], r)[...] = shards[w][...]
+    pl.semaphore_wait(barrier, 7)
+
+    def z_send(w, step):
+        block = weight_blocks(fulls[w], WEIGHT_KINDS[w], r)
+        return remote(shards[w], block, wz_send.at[w, step], wz_recv.at[w, step], z_peers[step], c)
+
+    def z_arrival(w, step):
+        source = ((z + 4 - (step + 1)) % 4) * 2 + y
+        block = weight_blocks(fulls[w], WEIGHT_KINDS[w], source)
+        return remote(block, block, wz_send.at[w, step], wz_recv.at[w, step], source, c), source
+
+    def y_send(w, slot, row):
+        block = weight_blocks(fulls[w], WEIGHT_KINDS[w], row)
+        return remote(block, block, wy_send.at[w, slot], wy_recv.at[w, slot], r_y, c)
+
+    def start_weight(w):
+        for step in range(3):
+            z_send(w, step).start()
+        y_send(w, 3, r).start()
+
+    def forward_weight(w):
+        for step in (0, 2, 1):
+            arrival, source = z_arrival(w, step)
+            arrival.wait_recv()
+            y_send(w, step, source).start()
+
+    def finish_weight(w):
+        for step in range(3):
+            z_send(w, step).wait_send()
+            source = ((z + 4 - (step + 1)) % 4) * 2 + y
+            y_send(w, step, source).wait_send()
+            pair = source + 1 - 2 * y
+            y_send(w, step, pair).wait_recv()
+        y_send(w, 3, r).wait_send()
+        y_send(w, 3, r_y).wait_recv()
+
+    def x_copy(ref, send, recv, i, col):
+        block = ref.at[i, :, aligned(col, width)]
+        return remote(block, block, send.at[i], recv.at[i], r, c_x)
+
+    def core_copy(ref, send, recv, i, slot, col):
+        block = ref.at[i, :, aligned(col, width)]
+        return remote(block, block, send.at[i, slot], recv.at[i, slot], r, c_core)
+
+    def vec_copy(slot, target, col):
+        block = vecs.at[:, aligned(col, width)]
+        return remote(block, block, vec_send.at[slot], vec_recv.at[slot], r, target)
+
+    for i in range(CHUNKS):
+        x_copy(tok_all, tx_send, tx_recv, i, c).start()
+        core_copy(tok_all, tc_send, tc_recv, i, 0, c).start()
+    for slot, target in enumerate((c_x, c_core, c_far)):
+        vec_copy(slot, target, c).start()
+    start_weight(0)
+    start_weight(1)
+    for slot, target in enumerate((c_x, c_core, c_far)):
+        vec_copy(slot, target, c).wait_send()
+        vec_copy(slot, target, target).wait_recv()
+
+    def keep(index, i, src, dst):
+        return pltpu.make_async_copy(src, dst, local_sem.at[index, i])
+
+    def kept(i, stage):
+        if stage == 0:
+            pairs = ((tok_all, tok_o), (q, q_o), (qt, qt_o), (k, k_o), (kt, kt_o), (v, v_o), (norm_one, one_o), (stat, stat_o))
+            base = 0
+        elif stage == 1:
+            pairs = ((mixf, mixf_o), (lse, lse_o))
+            base = 8
+        elif stage == 2:
+            pairs = ((unit, unit_o), (inv, inv_o), (norm_two, norm_o), (act, act_o), (slope, slope_o))
+            base = 10
+        else:
+            pairs = ((cot_all, cot_o),)
+            base = 15
+        return [keep(base + n, i, a.at[i], b.at[i]) for n, (a, b) in enumerate(pairs)]
+
+    def keep_hid(i):
+        return keep(16, i, hid.at[i, :, own], hid_o.at[i])
+
+    lane_ids = lax.broadcasted_iota(jnp.int32, (chunk // 7, 128), 1)
+
+    @pl.loop(0, CHUNKS)
+    def _(i):
+        x_copy(tok_all, tx_send, tx_recv, i, c_x).wait_recv()
+        core_copy(tok_all, tc_send, tc_recv, i, 1, c_x).start()
+        core_copy(tok_all, tc_send, tc_recv, i, 0, c_core).wait_recv()
+        core_copy(tok_all, tc_send, tc_recv, i, 1, c_far).wait_recv()
+        for part in range(7):
+            rows = pl.ds(part * (chunk // 7), chunk // 7)
+            units, mean, inverse = row_norm(tok_all[i, rows, :].astype(F32))
+            stat[i, rows, :] = jnp.where(lane_ids < 64, mean, inverse)
+            norm_one[i, rows, :] = (units * vecs[0:1, :] + vecs[1:2, :]).astype(BF16)
+
+    forward_weight(0)
+    start_weight(2)
+    forward_weight(1)
+    finish_weight(0)
+
+    @pl.loop(0, CHUNKS)
+    def _(i):
+        part = jnp.dot(norm_one[i], win[:, 0:width], preferred_element_type=F32)
+        part = (part + attn_bias[0:1, :]).astype(BF16)
+        q[i] = part
+        qt[i] = part.T
+        part = jnp.dot(norm_one[i], win[:, width : 2 * width], preferred_element_type=F32).astype(BF16)
+        k[i] = part
+        kt[i] = part.T
+        part = jnp.dot(norm_one[i], win[:, 2 * width : 3 * width], preferred_element_type=F32)
+        part = (part + attn_bias[1:2, :]).astype(BF16)
+        v[i] = part
+        vt[i] = part.T
+        for copy in kept(i, 0):
+            copy.start()
+
+    finish_weight(1)
+
+    def attend(i):
+        row_ids = lax.broadcasted_iota(jnp.int32, (128, chunk), 0)
+
+        @pl.loop(0, width // 128)
+        def _(pair):
+            lanes = aligned(pair, 128)
+            peaks = []
+            for h in range(2):
+                query = qt[i, lanes, :]
+                query = jnp.where(row_ids // HEAD_DIM == h, query, jnp.zeros_like(query))
+                peak = jnp.full((1, chunk), -jnp.inf, F32)
+                for j in range(CHUNKS):
+                    block = jnp.dot(k[j, :, lanes], query, preferred_element_type=F32)
+                    scores[h, j] = block
+                    peak = jnp.maximum(peak, jnp.max(block, axis=0, keepdims=True))
+                peaks.append(peak * scale)
+            outs = []
+            for h in range(2):
+                total = jnp.zeros((1, chunk), F32)
+                acc = jnp.zeros((HEAD_DIM, chunk), F32)
+                rows = pl.ds(pl.multiple_of(pair * 128 + h * HEAD_DIM, HEAD_DIM), HEAD_DIM)
+                for j in range(CHUNKS):
+                    weights = jnp.exp2(scores[h, j] * scale - peaks[h])
+                    total = total + jnp.sum(weights, axis=0, keepdims=True)
+                    acc = acc + jnp.dot(vt[j, rows, :], weights.astype(BF16), preferred_element_type=F32)
+                outs.append(acc / total)
+                lse[i, pl.ds(pair * 2 + h, 1), :] = peaks[h] + jnp.log2(total)
+            out = jnp.concatenate(outs, axis=0).T
+            mixf[i, :, lanes] = out
+            mixed[i, :, lanes] = out.astype(BF16)
+
+    def h1(i):
+        slot = i % 2
+        return remote(sb.at[slot, 1 - core], rb.at[i], h1_send.at[i], h1_recv.at[i], r, c_core)
+
+    def h2(i):
+        return remote(xb.at[i % 2], xr.at[i], h2_send.at[i], h2_recv.at[i], r, c_x)
+
+    def h3(i, x, side):
+        block = hid.at[i, :, aligned(x * 2 + side, width)]
+        return remote(block, block, h3_send.at[i, x], h3_recv.at[i, x], r, c_core)
+
+    @pl.loop(0, CHUNKS + 2)
+    def _(i):
+        @pl.when(i < CHUNKS)
+        def _():
+            x_copy(cot_all, cx_send, cx_recv, i, c).start()
+            core_copy(cot_all, cc_send, cc_recv, i, 0, c).start()
+            attend(i)
+            for copy in kept(i, 1):
+                copy.start()
+            partial = jnp.dot(mixed[i], wo[...], preferred_element_type=F32)
+            for x in range(2):
+                for side in range(2):
+                    block = x * 2 + side
+                    sb[i % 2, side, x] = partial[:, block * width : (block + 1) * width].astype(BF16)
+            h1(i).start()
+
+        @pl.when(i == 1)
+        def _():
+            forward_weight(2)
+            start_weight(3)
+
+        @pl.when(i == 2)
+        def _():
+            finish_weight(2)
+
+        @pl.when(i == 5)
+        def _():
+            forward_weight(3)
+
+        @pl.when(i >= 2)
+        def _():
+            t = i - 2
+            for x in range(2):
+                h3(t, x, core).wait_send()
+                h3(t, x, 1 - core).wait_recv()
+            for part in range(7):
+                rows = pl.ds(part * (chunk // 7), chunk // 7)
+                units, _, inverse = row_norm(hid[t, rows, :])
+                unit[t, rows, :] = units.astype(BF16)
+                inv[t, rows, :] = jnp.broadcast_to(inverse, (chunk // 7, 128))
+                norm_two[t, rows, :] = (units * vecs[3:4, :] + vecs[4:5, :]).astype(BF16)
+            for n in range(we.shape[1] // 256):
+                lanes = slice(n * 256, (n + 1) * 256)
+                expanded = jnp.dot(norm_two[t], we[:, lanes], preferred_element_type=F32) + exp_bias[:, lanes]
+                gate = 0.5 + 0.5 * lax.erf(expanded * (0.5 ** 0.5))
+                act[t, :, lanes] = (expanded * gate).astype(BF16)
+                bell = jnp.exp2(expanded * expanded * (-0.5 * LOG2E)) * 0.3989422804014327
+                slope[t, :, lanes] = (gate + expanded * bell).astype(BF16)
+            for copy in kept(t, 2):
+                copy.start()
+            keep_hid(t).start()
+
+        @pl.when(i < CHUNKS)
+        def _():
+            h1(i).wait()
+            for x in range(2):
+                xb[i % 2, x] = (sb[i % 2, core, x].astype(F32) + rb[i, x].astype(F32)).astype(BF16)
+            h2(i).start()
+
+        @pl.when((i >= 1) & (i <= CHUNKS))
+        def _():
+            t = i - 1
+            x_copy(cot_all, cx_send, cx_recv, t, c_x).wait_recv()
+            core_copy(cot_all, cc_send, cc_recv, t, 1, c_x).start()
+            h2(t).wait()
+            for x in range(2):
+                lanes = aligned(x * 2 + core, width)
+                total = xb[t % 2, x].astype(F32) + xr[t, x].astype(F32)
+                hid[t, :, lanes] = tok_all[t, :, lanes].astype(F32) + total + vecs[2:3, lanes]
+            for x in range(2):
+                h3(t, x, core).start()
+
+    @pl.loop(0, CHUNKS)
+    def _(i):
+        x_copy(tok_all, tx_send, tx_recv, i, c).wait_send()
+        x_copy(cot_all, cx_send, cx_recv, i, c).wait_send()
+        core_copy(tok_all, tc_send, tc_recv, i, 0, c).wait_send()
+        core_copy(tok_all, tc_send, tc_recv, i, 1, c_x).wait_send()
+        core_copy(cot_all, cc_send, cc_recv, i, 0, c).wait_send()
+        core_copy(cot_all, cc_send, cc_recv, i, 1, c_x).wait_send()
+        core_copy(cot_all, cc_send, cc_recv, i, 0, c_core).wait_recv()
+        core_copy(cot_all, cc_send, cc_recv, i, 1, c_far).wait_recv()
+        for copy in kept(i, 3):
+            copy.start()
+
+    finish_weight(3)
+    last = [
+        keep(17, n, a, b)
+        for n, (a, b) in enumerate(((win, win_o), (wo, wo_o), (we, we_o), (wr, wr_o), (vecs, vec_o)))
+    ]
+    for copy in last:
+        copy.start()
+
+    @pl.loop(0, CHUNKS)
+    def _(i):
+        for stage in range(4):
+            for copy in kept(i, stage):
+                copy.wait()
+        keep_hid(i).wait()
+
+    for copy in last:
+        copy.wait()
+
+
+def forward_call(tok, cot, vec, attn_bias, exp_bias, win_s, wo_s, we_s, wr_s):
+    pairs, width = tok.shape[0], vec.shape[1]
+    chunk = 2 * pairs // CHUNKS
+    full = 4 * width
+    hidden = we_s.shape[1]
+    n = CHUNKS
+
+    def sd(shape, dtype):
+        return jax.ShapeDtypeStruct(shape, dtype)
+
+    outs = [
+        sd((n, chunk, full), BF16),
+        sd((n, chunk, full), BF16),
+        sd((n, chunk, width), BF16),
+        sd((n, width, chunk), BF16),
+        sd((n, chunk, width), BF16),
+        sd((n, width, chunk), BF16),
+        sd((n, chunk, width), BF16),
+        sd((n, chunk, width), F32),
+        sd((n, 8, chunk), F32),
+        sd((n, chunk, width), F32),
+        sd((n, chunk, full), BF16),
+        sd((n, chunk, 128), F32),
+        sd((n, chunk, full), BF16),
+        sd((n, chunk, hidden), BF16),
+        sd((n, chunk, hidden), BF16),
+        sd((full, 3 * width), BF16),
+        sd((width, full), BF16),
+        sd((full, hidden), BF16),
+        sd((hidden, full), BF16),
+        sd((8, full), F32),
+        sd((n, chunk, full), BF16),
+        sd((n, chunk, 128), F32),
+    ]
+    vm = pltpu.VMEM
+    dma = pltpu.SemaphoreType.DMA
+    scratch = [
+        vm((n, chunk, full), BF16), vm((n, chunk, full), BF16), vm((n, chunk, full), BF16),
+        vm((n, chunk, width), BF16), vm((n, width, chunk), BF16),
+        vm((n, chunk, width), BF16), vm((n, width, chunk), BF16),
+        vm((n, chunk, width), BF16), vm((n, width, chunk), BF16),
+        vm((n, chunk, width), BF16), vm((n, chunk, width), F32), vm((n, 8, chunk), F32),
+        vm((n, chunk, full), F32), vm((n, chunk, full), BF16), vm((n, chunk, 128), F32),
+        vm((n, chunk, full), BF16), vm((n, chunk, hidden), BF16), vm((n, chunk, hidden), BF16),
+        vm((full, 3 * width), BF16), vm((width, full), BF16), vm((full, hidden), BF16), vm((hidden, full), BF16),
+        vm((8, full), F32), vm((n, chunk, 128), F32),
+        vm((2, n, chunk, chunk), F32),
+        vm((2, 2, 2, chunk, width), BF16), vm((n, 2, chunk, width), BF16),
+        vm((2, 2, chunk, width), BF16), vm((n, 2, chunk, width), BF16),
+        dma((18, n)), dma((4, 3)), dma((4, 3)), dma((4, 4)), dma((4, 4)), dma((3,)), dma((3,)),
+        dma((n,)), dma((n,)), dma((n, 2)), dma((n, 2)), dma((n,)), dma((n,)), dma((n, 2)), dma((n, 2)),
+        dma((n,)), dma((n,)), dma((n,)), dma((n,)), dma((n, 2)), dma((n, 2)),
+    ]
+    return pl.pallas_call(
+        forward_kernel,
+        out_shape=outs,
+        in_specs=[pl.BlockSpec(memory_space=pltpu.VMEM)] * 9,
+        out_specs=[pl.BlockSpec(memory_space=pl.ANY)] * len(outs),
+        scratch_shapes=scratch,
+        compiler_params=pltpu.CompilerParams(
+            collective_id=0, has_side_effects=True, vmem_limit_bytes=63 << 20
+        ),
+    )(tok, cot, vec, attn_bias, exp_bias, win_s, wo_s, we_s, wr_s)
+
+
+GRAD_KINDS = ("rows", "cols", "rows", "cols")
+
+
+def backward_kernel(
+    tok_h, cot_h, q_h, qt_h, k_h, kt_h, v_h, mixf_h, lse_h, hid_h, unit_h, inv_h,
+    normed_h, act_h, slope_h, win_h, wo_h, we_h, wr_h, vec_h, one_h, stat_h,
+    out_o, tg_o, sums_o, gin_o, gout_o, gexp_o, gred_o,
+    cot, q, qt, k, kt, v, mixf, lse, hid, unit, inv, normed, act, slope, win, wo, we, wr, vecs, stat,
+    grad, dq, dk, dv, tg, out, sb_g, sb_o, rb_g, xr_g, rb_o, xr_o, xr_1, st, st_in,
+    col_sums, hid_sums, packet, packets,
+    ys_in, ys_out, ys_exp, ys_red, oh_in, oh_out, oh_exp, oh_red,
+    yr_in, yr_out, yr_exp, yr_red, zr_in, zr_out, zr_exp, zr_red,
+    gin, gout, gexp, gred,
+    load_sem, store_sem, hid_sem, gy_send, gy_recv, gz_send, gz_recv,
+    h1g_send, h1g_recv, h2g_send, h2g_recv, h3g_send, h3g_recv,
+    h1o_send, h1o_recv, h2o_send, h2o_recv, h1t_send, h1t_recv, h2t_send, h2t_recv,
+    st_send, st_recv, pk_send, pk_recv,
+):
+    r, c = lax.axis_index("row"), lax.axis_index("col")
+    z, y = r // 2, r % 2
+    xx, core = c // 2, c % 2
+    c_x, c_core, c_far = (c + 2) % 4, c + 1 - 2 * core, (c + 2) % 4 + 1 - 2 * core
+    r_y = r + 1 - 2 * y
+    tok, one = act, normed
+    chunk = q.shape[0] // CHUNKS
+    half = chunk // 2
+    width = q.shape[1]
+    full = cot.shape[1]
+    scale = LOG2E * HEAD_DIM ** (-0.5)
+    own = aligned(c, width)
+    others = [(r + step) % 8 for step in range(1, 8)]
+
+    barrier = pltpu.get_barrier_semaphore()
+    for col in (c_x, c_core, c_far):
+        pl.semaphore_signal(barrier, inc=1, device_id=(r, col), device_id_type=MESH)
+    for row in others:
+        pl.semaphore_signal(barrier, inc=1, device_id=(row, c), device_id_type=MESH)
+
+    loads = {}
+    order = (
+        ("wr", wr_h, wr), ("cot", cot_h, cot), ("slope", slope_h, slope), ("we", we_h, we), ("act", act_h, act),
+        ("vec", vec_h, vecs), ("unit", unit_h, unit), ("inv", inv_h, inv), ("wo", wo_h, wo),
+        ("normed", normed_h, normed), ("mixf", mixf_h, mixf), ("lse", lse_h, lse), ("qt", qt_h, qt), ("q", q_h, q),
+        ("k", k_h, k), ("v", v_h, v), ("kt", kt_h, kt), ("win", win_h, win), ("stat", stat_h, stat),
+        ("tok", tok_h, tok), ("one", one_h, one),
+    )
+    for n, (name, src, dst) in enumerate(order):
+        loads[name] = pltpu.make_async_copy(src, dst, load_sem.at[n])
+    late = ("tok", "one")
+    for name, _, _ in order:
+        if name not in late:
+            loads[name].start()
+    dk[...] = jnp.zeros_like(dk)
+    dv[...] = jnp.zeros_like(dv)
+    col_sums[...] = jnp.zeros_like(col_sums)
+    hid_sums[...] = jnp.zeros_like(hid_sums)
+    pl.semaphore_wait(barrier, 10)
+
+    def rows_of(i):
+        return pl.ds(pl.multiple_of(i * chunk, chunk), chunk)
+
+    def h1(sb, rb, send, recv, i):
+        return remote(sb.at[i % 2, 1 - core], rb.at[i], send.at[i], recv.at[i], r, c_core)
+
+    def fill(sb, i, partial):
+        for x in range(2):
+            for side in range(2):
+                block = x * 2 + side
+                sb[i % 2, side, x] = partial[:, block * width : (block + 1) * width].astype(BF16)
+
+    def merge(sb, rb, i):
+        for x in range(2):
+            rb[i, x] = (sb[i % 2, core, x].astype(F32) + rb[i, x].astype(F32)).astype(BF16)
+
+    def h1g(i):
+        return h1(sb_g, rb_g, h1g_send, h1g_recv, i)
+
+    def h1o(i):
+        return h1(sb_o, rb_o, h1o_send, h1o_recv, i)
+
+    def h1t(i):
+        return h1(sb_g, rb_g, h1t_send, h1t_recv, i)
+
+    def h2g(i):
+        return remote(rb_g.at[i], xr_g.at[i], h2g_send.at[i], h2g_recv.at[i], r, c_x)
+
+    def h2o(i):
+        return remote(rb_o.at[i, 1 - xx], xr_o.at[i], h2o_send.at[i], h2o_recv.at[i], r, c_x)
+
+    def h2t(i):
+        return remote(rb_g.at[i, 1 - xx], xr_1.at[i], h2t_send.at[i], h2t_recv.at[i], r, c_x)
+
+    def h3g(i, x, side):
+        block = grad.at[i % 4, :, aligned(x * 2 + side, width)]
+        return remote(block, block, h3g_send.at[i, x], h3g_recv.at[i, x], r, c_core)
+
+    def spread_grad(i):
+        h2g(i).wait()
+        for x in range(2):
+            grad[i % 4, :, aligned(x * 2 + core, width)] = rb_g[i, x].astype(F32) + xr_g[i, x].astype(F32)
+        for x in range(2):
+            h3g(i, x, core).start()
+
+    ys = (ys_in, ys_out, ys_exp, ys_red)
+    oh = (oh_in, oh_out, oh_exp, oh_red)
+    yr = (yr_in, yr_out, yr_exp, yr_red)
+    zr = (zr_in, zr_out, zr_exp, zr_red)
+
+    def gy(w, s):
+        return remote(ys[w].at[s], yr[w].at[s], gy_send.at[w, s], gy_recv.at[w, s], r_y, c)
+
+    def gz(w, s):
+        target = ((z + 1 + s) % 4) * 2 + y
+        return remote(oh[w].at[s], zr[w].at[s], gz_send.at[w, s], gz_recv.at[w, s], target, c)
+
+    def grad_block(w, s, left, right):
+        zt = (z + 1 + s) % 4
+        lanes = aligned(zt, 256)
+        if GRAD_KINDS[w] == "rows":
+            block = lax.dot_general(left[:, lanes], right, TN_DIMS, preferred_element_type=F32).astype(BF16)
+            low, high = block[0:128, :], block[128:256, :]
+        else:
+            block = lax.dot_general(left, right[:, lanes], TN_DIMS, preferred_element_type=F32).astype(BF16)
+            low, high = block[:, 0:128], block[:, 128:256]
+
+        @pl.when(y == 0)
+        def _():
+            oh[w][s] = low
+            ys[w][s] = high
+
+        @pl.when(y == 1)
+        def _():
+            oh[w][s] = high
+            ys[w][s] = low
+
+        gy(w, s).start()
+
+    def pass_on(w, s):
+        gy(w, s).wait()
+        oh[w][s] = (oh[w][s].astype(F32) + yr[w][s].astype(F32)).astype(BF16)
+        gz(w, s).start()
+
+    def finish_grad(w, dst):
+        gy(w, 3).wait()
+        total = oh[w][3].astype(F32) + yr[w][3].astype(F32)
+        for s in range(3):
+            gz(w, s).wait()
+            total = total + zr[w][s].astype(F32)
+        dst[...] = total
+
+    loads["wr"].wait()
+    loads["cot"].wait()
+    loads["slope"].wait()
+    loads["we"].wait()
+    loads["act"].wait()
+
+    @pl.loop(0, CHUNKS + 1)
+    def _(i):
+        @pl.when(i < CHUNKS)
+        def _():
+            rows = rows_of(i)
+            for n in range(slope.shape[1] // 256):
+                lanes = slice(n * 256, (n + 1) * 256)
+                grad_act = lax.dot_general(cot[rows, :], wr[lanes, :], NT_DIMS, preferred_element_type=F32)
+                low = (slope[rows, lanes].astype(F32) * grad_act).astype(BF16)
+                slope[rows, lanes] = low
+                hid_sums[0:1, lanes] += jnp.sum(low.astype(F32), axis=0, keepdims=True)
+            fill(sb_g, i, lax.dot_general(slope[rows, :], we[...], NT_DIMS, preferred_element_type=F32))
+            h1g(i).start()
+
+        @pl.when(i >= 1)
+        def _():
+            h1o(i - 1).wait()
+            merge(sb_o, rb_o, i - 1)
+
+        @pl.when(i < CHUNKS)
+        def _():
+            rows = rows_of(i)
+            fill(sb_o, i, jnp.dot(act[rows, :], wr[...], preferred_element_type=F32))
+            h1o(i).start()
+            h1g(i).wait()
+            merge(sb_g, rb_g, i)
+            h2g(i).start()
+            col_sums[0:1, :] += jnp.sum(cot[rows, :].astype(F32), axis=0, keepdims=True)
+
+    loads["normed"].wait()
+    for s in range(3):
+        grad_block(3, s, act[...], cot)
+    spread_grad(0)
+    for s in range(3):
+        grad_block(2, s, normed, slope[...])
+    spread_grad(1)
+    grad_block(3, 3, act[...], cot)
+    grad_block(2, 3, normed, slope[...])
+    for name in late:
+        loads[name].start()
+    for name in ("unit", "inv", "vec", "wo", "mixf", "lse", "qt", "q", "k", "v", "kt", "win", "stat"):
+        loads[name].wait()
+
+    def hid_load(i):
+        return pltpu.make_async_copy(hid_h.at[rows_of(i), :], hid.at[i % 2], hid_sem.at[i])
+
+    def out_store(i, s):
+        return pltpu.make_async_copy(
+            out.at[i % 2, s], out_o.at[pl.ds(pl.multiple_of(i * half, half), half), pl.ds(s * width, width)],
+            store_sem.at[0, i, s],
+        )
+
+    def tg_store(i, s):
+        return pltpu.make_async_copy(
+            tg.at[i, s], tg_o.at[pl.ds(pl.multiple_of(i * half, half), half), pl.ds(s * width, width)],
+            store_sem.at[1, i, s],
+        )
+
+    def attend_back(i):
+        rows = rows_of(i)
+        go = lax.dot_general(unit[rows, :], wo[...], NT_DIMS, preferred_element_type=F32).astype(BF16)
+        inner = (go.astype(F32) * mixf[rows, :]).T
+        go_t = go.T
+        row_ids = lax.broadcasted_iota(jnp.int32, (128, chunk), 0)
+        lane_ids = lax.broadcasted_iota(jnp.int32, (chunk, 128), 1)
+        for pair in range(width // 128):
+            lanes = slice(pair * 128, (pair + 1) * 128)
+            queries, grads, query_rows, grad_rows, deltas, logs = [], [], [], [], [], []
+            for h in range(2):
+                pick = row_ids // HEAD_DIM == h
+                value = qt[i, lanes, :]
+                queries.append(jnp.where(pick, value, jnp.zeros_like(value)))
+                value = go_t[lanes, :]
+                grads.append(jnp.where(pick, value, jnp.zeros_like(value)))
+                pick = lane_ids // HEAD_DIM == h
+                value = q[rows, lanes]
+                query_rows.append(jnp.where(pick, value, jnp.zeros_like(value)))
+                value = go[:, lanes]
+                grad_rows.append(jnp.where(pick, value, jnp.zeros_like(value)))
+                first = pair * 128 + h * HEAD_DIM
+                deltas.append(jnp.sum(inner[first : first + HEAD_DIM, :], axis=0, keepdims=True))
+                logs.append(lse[i, pair * 2 + h : pair * 2 + h + 1, :])
+
+            def step(j, query_grads):
+                keys = rows_of(j)
+                key_block = k[keys, lanes]
+                value_block = v[keys, lanes]
+                key_sum = dk[keys, lanes]
+                value_sum = dv[keys, lanes]
+                results = []
+                for h in range(2):
+                    block = jnp.dot(key_block, queries[h], preferred_element_type=F32)
+                    probs = jnp.exp2(block * scale - logs[h])
+                    grad_probs = jnp.dot(value_block, grads[h], preferred_element_type=F32)
+                    grad_scores = (probs * (grad_probs - deltas[h])).astype(BF16)
+                    value_sum = value_sum + jnp.dot(probs.astype(BF16), grad_rows[h], preferred_element_type=F32)
+                    key_sum = key_sum + jnp.dot(grad_scores, query_rows[h], preferred_element_type=F32)
+                    first = pair * 128 + h * HEAD_DIM
+                    results.append(
+                        query_grads[h]
+                        + jnp.dot(kt[j, first : first + HEAD_DIM, :], grad_scores, preferred_element_type=F32)
+                    )
+                dk[keys, lanes] = key_sum
+                dv[keys, lanes] = value_sum
+                return tuple(results)
+
+            empty = jnp.zeros((HEAD_DIM, chunk), F32)
+            parts = lax.fori_loop(0, CHUNKS, step, (empty, empty))
+            query_grad = (jnp.concatenate(parts, axis=0).T * HEAD_DIM ** (-0.5)).astype(BF16)
+            dq[rows, lanes] = query_grad
+
+    def finish_out(i):
+        h2o(i).wait()
+        hid_load(i).wait()
+        total = rb_o[i, xx].astype(F32) + xr_o[i].astype(F32)
+        value = (hid[i % 2] + total + vecs[5:6, own]).astype(BF16)
+        for s in range(2):
+            out[i % 2, s] = value[s * half : (s + 1) * half, :]
+        for s in range(2):
+            out_store(i, s).start()
+
+    @pl.loop(0, CHUNKS)
+    def _(i):
+        h2o(i).start()
+        hid_load(i).start()
+        for x in range(2):
+            h3g(i, x, core).wait_send()
+            h3g(i, x, 1 - core).wait_recv()
+        step_rows = chunk // 7
+        for part in range(7):
+            rows = pl.ds(pl.multiple_of(i * chunk + part * step_rows, step_rows), step_rows)
+            span = slice(part * step_rows, (part + 1) * step_rows)
+            incoming = grad[i % 4, span, :]
+            units = unit[rows, :].astype(F32)
+            scaled = incoming * vecs[3:4, :]
+            plain = jnp.mean(scaled, axis=1, keepdims=True)
+            cross = jnp.mean(scaled * units, axis=1, keepdims=True)
+            total = cot[rows, :].astype(F32) + inv[rows, 0:1] * (scaled - plain - units * cross)
+            low = total.astype(BF16)
+            col_sums[1:2, :] += jnp.sum(incoming * units, axis=0, keepdims=True)
+            col_sums[2:3, :] += jnp.sum(incoming, axis=0, keepdims=True)
+            col_sums[3:4, :] += jnp.sum(low.astype(F32), axis=0, keepdims=True)
+            unit[rows, :] = low
+            grad[i % 4, span, :] = total
+        for s in range(2):
+            tg[i, s] = grad[i % 4, s * half : (s + 1) * half, own]
+        attend_back(i)
+
+        @pl.when(i + 2 < CHUNKS)
+        def _():
+            spread_grad(i + 2)
+
+        for s in range(3):
+            @pl.when(i == s)
+            def _():
+                pass_on(3, s)
+
+            @pl.when(i == s + 3)
+            def _():
+                pass_on(2, s)
+
+        @pl.when(i >= 1)
+        def _():
+            @pl.when(i >= 3)
+            def _():
+                for s in range(2):
+                    out_store(i - 3, s).wait()
+            finish_out(i - 1)
+
+    for s in range(2):
+        out_store(CHUNKS - 3, s).wait()
+    finish_out(CHUNKS - 1)
+
+    for i in range(CHUNKS):
+        rows = pl.ds(i * chunk, chunk)
+        k[rows, :] = (dk[rows, :] * HEAD_DIM ** (-0.5)).astype(BF16)
+        low = dv[rows, :].astype(BF16)
+        v[rows, :] = low
+        col_sums[4:5, 0:width] += jnp.sum(dq[rows, :].astype(F32), axis=0, keepdims=True)
+        col_sums[5:6, 0:width] += jnp.sum(low.astype(F32), axis=0, keepdims=True)
+    for name in late:
+        loads[name].wait()
+
+    def inward_block(s):
+        zt = (z + 1 + s) % 4
+        left = one[:, aligned(zt, 256)]
+        for n, right in enumerate((dq, k, v)):
+            lanes = slice(n * width, (n + 1) * width)
+            block = lax.dot_general(left, right[...], TN_DIMS, preferred_element_type=F32).astype(BF16)
+
+            @pl.when(y == 0)
+            def _():
+                oh_in[s, :, lanes] = block[0:128, :]
+                ys_in[s, :, lanes] = block[128:256, :]
+
+            @pl.when(y == 1)
+            def _():
+                oh_in[s, :, lanes] = block[128:256, :]
+                ys_in[s, :, lanes] = block[0:128, :]
+
+        gy(0, s).start()
+
+    for s in range(3):
+        inward_block(s)
+
+    def stat_copy(i, slot, target):
+        return remote(st.at[i], st_in.at[i, slot], st_send.at[i, slot], st_recv.at[i, slot], r, target)
+
+    lane_ids = lax.broadcasted_iota(jnp.int32, (chunk, 128), 1)
+    gain = vecs[0:1, :]
+
+    @pl.loop(0, CHUNKS + 2)
+    def _(i):
+        @pl.when(i < CHUNKS)
+        def _():
+            rows = rows_of(i)
+            partial = lax.dot_general(dq[rows, :], win[:, 0:width], NT_DIMS, preferred_element_type=F32)
+            partial = partial + lax.dot_general(
+                k[rows, :], win[:, width : 2 * width], NT_DIMS, preferred_element_type=F32
+            )
+            partial = partial + lax.dot_general(
+                v[rows, :], win[:, 2 * width : 3 * width], NT_DIMS, preferred_element_type=F32
+            )
+            fill(sb_g, i, partial)
+            h1t(i).start()
+            units = (tok[rows, :].astype(F32) - stat[rows, 0:1]) * stat[rows, 64:65]
+            scaled = partial * gain
+            plain = jnp.sum(scaled, axis=1, keepdims=True)
+            cross = jnp.sum(scaled * units, axis=1, keepdims=True)
+            both = jnp.where(lane_ids == 0, plain, jnp.where(lane_ids == 1, cross, 0.0))
+            st[i] = both.T[0:8, :]
+            for slot, target in enumerate((c_x, c_core, c_far)):
+                stat_copy(i, slot, target).start()
+            h1t(i).wait()
+            merge(sb_g, rb_g, i)
+            h2t(i).start()
+
+        for s in range(3):
+            @pl.when(i == s + 1)
+            def _():
+                pass_on(0, s)
+
+        @pl.when(i == 4)
+        def _():
+            for s in range(3):
+                grad_block(1, s, mixf[...].astype(BF16), unit)
+
+        @pl.when(i == 5)
+        def _():
+            inward_block(3)
+            grad_block(1, 3, mixf[...].astype(BF16), unit)
+
+        @pl.when(i == 6)
+        def _():
+            for s in range(3):
+                pass_on(1, s)
+
+        @pl.when(i >= 2)
+        def _():
+            t = i - 2
+            rows = rows_of(t)
+            h2t(t).wait()
+            total = st[t]
+            for slot, target in enumerate((c_x, c_core, c_far)):
+                stat_copy(t, slot, target).wait()
+                total = total + st_in[t, slot]
+            columns = jnp.concatenate([total, jnp.zeros((120, chunk), F32)], axis=0).T
+            plain = columns[:, 0:1] / full
+            cross = columns[:, 1:2] / full
+            incoming = rb_g[t, xx].astype(F32) + xr_1[t].astype(F32)
+            inverse = stat[rows, 64:65]
+            units = (tok[rows, own].astype(F32) - stat[rows, 0:1]) * inverse
+            back = inverse * (incoming * vecs[0:1, own] - plain - units * cross)
+            for s in range(2):
+                tg[t, s] = tg[t, s] + back[s * half : (s + 1) * half, :]
+            for s in range(2):
+                tg_store(t, s).start()
+            col_sums[6:7, 0:width] += jnp.sum(incoming * units, axis=0, keepdims=True)
+            col_sums[7:8, 0:width] += jnp.sum(incoming, axis=0, keepdims=True)
+
+    packet[0:1, :] = col_sums[6:7, 0:width]
+    packet[1:2, :] = col_sums[7:8, 0:width]
+    packet[2:4, :] = col_sums[4:6, 0:width]
+    packet[4:5, :] = col_sums[3:4, own]
+    packet[5:7, :] = col_sums[1:3, own]
+    packet[7:8, :] = col_sums[0:1, own]
+    for n in range(4):
+        packet[8 + n : 9 + n, :] = hid_sums[0:1, n * width : (n + 1) * width]
+
+    def packet_copy(step):
+        return remote(packet, packets.at[step], pk_send.at[step], pk_recv.at[step], others[step], c)
+
+    for step in range(7):
+        packet_copy(step).start()
+    finish_grad(3, gred)
+    finish_grad(2, gexp)
+    finish_grad(0, gin)
+    finish_grad(1, gout)
+    stores = [
+        pltpu.make_async_copy(src, dst, store_sem.at[2, n, 0])
+        for n, (src, dst) in enumerate(((gin, gin_o), (gout, gout_o), (gexp, gexp_o), (gred, gred_o)))
+    ]
+    for copy in stores:
+        copy.start()
+    total = packet[...]
+    for step in range(7):
+        packet_copy(step).wait()
+        total = total + packets[step]
+    packet[...] = total
+    copy = pltpu.make_async_copy(packet, sums_o, store_sem.at[2, 4, 0])
+    copy.start()
+    copy.wait()
+    for copy in stores:
+        copy.wait()
+    for i in range(CHUNKS - 2, CHUNKS):
+        for s in range(2):
+            out_store(i, s).wait()
+
+    @pl.loop(0, CHUNKS)
+    def _(i):
+        for s in range(2):
+            tg_store(i, s).wait()
+
+
+def backward_call(*arrays):
+    (tok, cot, q, qt, k, kt, v, mixf, lse, hid, unit, inv, normed, act, slope, win, wo, we, wr, vec, one, stat) = arrays
+    rows, width = q.shape
+    full, hidden = we.shape
+    n, chunk = CHUNKS, rows // CHUNKS
+    half = chunk // 2
+    pairs = rows // 2
+
+    def sd(shape, dtype):
+        return jax.ShapeDtypeStruct(shape, dtype)
+
+    outs = [
+        sd((pairs, 2 * width), BF16), sd((pairs, 2 * width), F32), sd((16, width), F32),
+        sd((128, 3 * width), F32), sd((width, 128), F32), sd((128, hidden), F32), sd((hidden, 128), F32),
+    ]
+    vm = pltpu.VMEM
+    dma = pltpu.SemaphoreType.DMA
+
+    def shapes(lead):
+        return [
+            vm((lead, 128, 3 * width), BF16), vm((lead, width, 128), BF16),
+            vm((lead, 128, hidden), BF16), vm((lead, hidden, 128), BF16),
+        ]
+
+    def like(array):
+        return vm(array.shape, array.dtype)
+
+    scratch = [
+        like(cot), like(q), like(qt), like(k), like(kt), like(v), like(mixf), like(lse),
+        vm((2, chunk, width), F32),
+        like(unit), like(inv), like(normed), like(act), like(slope),
+        like(win), like(wo), like(we), like(wr), like(vec), like(stat),
+        vm((4, chunk, full), F32), vm((rows, width), BF16), vm((rows, width), F32), vm((rows, width), F32),
+        vm((n, 2, half, width), F32), vm((2, 2, half, width), BF16),
+        vm((2, 2, 2, chunk, width), BF16), vm((2, 2, 2, chunk, width), BF16),
+        vm((n, 2, chunk, width), BF16), vm((n, 2, chunk, width), BF16),
+        vm((n, 2, chunk, width), BF16), vm((n, chunk, width), BF16), vm((n, chunk, width), BF16),
+        vm((n, 8, chunk), F32), vm((n, 3, 8, chunk), F32),
+        vm((8, full), F32), vm((8, hidden), F32), vm((16, width), F32), vm((7, 16, width), F32),
+        *shapes(4), *shapes(4), *shapes(4), *shapes(3),
+        vm((128, 3 * width), F32), vm((width, 128), F32), vm((128, hidden), F32), vm((hidden, 128), F32),
+        dma((21,)), dma((3, n, 2)), dma((n,)), dma((4, 4)), dma((4, 4)), dma((4, 3)), dma((4, 3)),
+        dma((n,)), dma((n,)), dma((n,)), dma((n,)), dma((n, 2)), dma((n, 2)),
+        dma((n,)), dma((n,)), dma((n,)), dma((n,)), dma((n,)), dma((n,)), dma((n,)), dma((n,)),
+        dma((n, 3)), dma((n, 3)), dma((7,)), dma((7,)),
+    ]
+    return pl.pallas_call(
+        backward_kernel,
+        out_shape=outs,
+        in_specs=[pl.BlockSpec(memory_space=pl.ANY)] * len(arrays),
+        out_specs=[pl.BlockSpec(memory_space=pl.ANY)] * len(outs),
+        scratch_shapes=scratch,
+        compiler_params=pltpu.CompilerParams(
+            collective_id=1, has_side_effects=True, vmem_limit_bytes=63 << 20
+        ),
+    )(*arrays)
+
+
 CONTRACT_ROWS = (((0,), (0,)), ((), ()))
 CONTRACT_COLS = (((1,), (1,)), ((), ()))
 
@@ -189,7 +1130,7 @@
     return (output_value, saved_state)
 
 
-def per_device(
+def plain_device(
     tokens,
     first_gain,
     first_shift,
@@ -386,6 +1327,76 @@
     )
 
 
+def fused_device(
+    tokens,
+    first_gain,
+    first_shift,
+    inward_weight,
+    attention_bias,
+    output_weight,
+    output_bias,
+    second_gain,
+    second_shift,
+    expand_weight,
+    expand_bias,
+    reduce_weight,
+    reduce_bias,
+    cotangent,
+):
+    empty = jnp.zeros_like(first_gain)
+    vectors = jnp.stack(
+        [first_gain, first_shift, output_bias, second_gain, second_shift, reduce_bias, empty, empty]
+    )
+    kept = forward_call(
+        tokens,
+        cotangent,
+        vectors,
+        attention_bias,
+        expand_bias[None],
+        inward_weight.reshape(inward_weight.shape[0], -1),
+        output_weight,
+        expand_weight,
+        reduce_weight,
+    )
+    (tok, cot, q, qt, k, kt, v, mixf, lse, hid, unit, inv, normed, act, slope, win, wo, we, wr, vec, one, stat) = kept
+
+    def flat(array):
+        return array.reshape(-1, array.shape[-1])
+
+    outs = backward_call(
+        flat(tok), flat(cot), flat(q), qt, flat(k), kt, flat(v), flat(mixf), lse, flat(hid), flat(unit), flat(inv),
+        flat(normed), flat(act), flat(slope), win, wo, we, wr, vec, flat(one), flat(stat),
+    )
+    layer_output, tokens_grad, sums, inward_grad, output_grad, expand_grad, reduce_grad = outs
+    return (
+        layer_output,
+        tokens_grad,
+        sums[0],
+        sums[1],
+        inward_grad.reshape(inward_weight.shape),
+        sums[2:4],
+        output_grad,
+        sums[4],
+        sums[5],
+        sums[6],
+        expand_grad,
+        sums[8:12].reshape(-1),
+        reduce_grad,
+        sums[7],
+    )
+
+
+def per_device(rows, cols, *arrays):
+    tokens, inward_weight, expand_weight = arrays[0], arrays[3], arrays[9]
+    fits = (
+        (rows, cols) == (8, 4)
+        and tokens.shape == (SEQ // 2, 512)
+        and inward_weight.shape == (128, 3, 256)
+        and expand_weight.shape == (128, 1024)
+    )
+    return fused_device(*arrays) if fits else plain_device(*arrays)
+
+
 def solution(mesh):
     in_specs = (
         P("row", "col"),
@@ -420,5 +1431,6 @@
         P("col"),
     )
     return jax.shard_map(
-        per_device, mesh=mesh, in_specs=in_specs, out_specs=out_specs, check_vma=False
-    )
+        functools.partial(per_device, mesh.shape["row"], mesh.shape["col"]),
+        mesh=mesh, in_specs=in_specs, out_specs=out_specs, check_vma=False
+    )

time: 1180 us -> 302 us (0.26)
  waiting for transfers between devices: 650 us -> 0 us
  Pallas kernels: 0 us -> 286 us
  matrix products: 250 us -> 0 us
  blocking collectives: 114 us -> 0 us
  other arithmetic: 79.1 us -> 0 us
  local copies, waits for them, and re-layouts: 61.6 us -> 15.2 us
  between operations: 14.8 us -> 0.7 us
    reduce_scatter x7 -> x0, waiting for transfers between devices: 351 us -> none  [the longest x2 117 us: sum_grad_partials(): return lax.psum_scatter(values, 'col', scatter_dimension=1, tiled=True)]
    pallas_call x0 -> x2, Pallas kernels: none -> 286 us  [the longest x1 153 us: backward_call(): pl.pallas_call(backward_kernel, out_shape=outs, in_specs=[pl.BlockSpec(me...]
    dot_general x29 -> x0, matrix products: 235 us -> none  [the longest x4 31.2 us: one_block(): jnp.einsum('hqk,khd->qhd', prob_low, value_rows, preferred_element_type=j...]
    all_gather x8 -> x0, waiting for transfers between devices: 196 us -> none  [the longest x2 60.1 us: spread_grads(): return lax.all_gather(values, 'col', axis=1, tiled=True)]
    unnamed x19 -> x0, waiting for transfers between devices: 103 us -> none
    psum x7 -> x0, blocking collectives: 82.4 us -> none  [the longest x1 35.2 us: per_device(): lax.psum((first_gain_grad, first_shift_grad, attention_bias_grad, output_...]
    convert_element_type x13 -> x0, other arithmetic: 51 us -> none  [the longest x2 36.3 us: step_block(): grad_scores = (probs * (grad_probs - inner_sum)).astype(jnp.bfloat16)]
    all_gather x1 -> x0, blocking collectives: 32 us -> none  [fetch_weights(): lax.all_gather(output_weight, 'row', axis=1, tiled=True)]
  transfers between devices with their start and end apart: 17 -> 0, of which waited for: 16 -> 0; matrix products, arithmetic and copies ran while one was open for 12% -> 0% of each run, Pallas kernels for 0% -> 0%
where the time goes in v1:
time: 302 us
  Pallas kernels  286 us (95%)
  local copies, waits for them, and re-layouts  15.2 us (5%)
    pallas_call x1, Pallas kernels, backward_call(): pl.pallas_call(backward_kernel, out_shape=outs, in_specs=[pl.BlockSpec(me...  153 us
    pallas_call x1, Pallas kernels, forward_call(): pl.pallas_call(forward_kernel, out_shape=outs, in_specs=[pl.BlockSpec(mem...  133 us
    unnamed x17, local copies, waits for them, and re-layouts  8.84 us

profile of v1, /device:TPU:0, one launch (start us, length us, event | category | flops | bytes accessed | tf_op | source)
XLA Modules:
  0.0 301.9 jit_solution(16923431285433544212)
XLA Ops:
  0.7 1.4 stack.31.vec
  2.0 1.1 copy.30
  3.1 0.8 copy.31.win_s
  4.0 133.2 %shard_map.245 = (bf16[7,224,1024]{2,1,0:T(8,128)(2,1)}, bf16[7,224,1024]{2,1,0:T(8,128)(2,1)}, bf16[7,224,256]{2,1,0:T(8,128)(2,1)}, bf16[7,256,224]{2,1,0:T(8,...) custom-call(bf16[784,512]{1,0:T(8,128)(2,1)} %tok.1, ...), custom_call_target="tpu_custom_call" | custom-call | tf_op jit(solution)/shard_map/pallas_call | solution.py:402
  137.1 152.9 %shard_map.246 = (bf16[784,512]{1,0:T(8,128)(2,1)}, f32[784,512]{1,0:T(8,128)}, f32[16,256]{1,0:T(8,128)}, f32[128,768]{1,0:T(8,128)}, f32[256,128]{1,0:T(8,128)...) custom-call(bf16[1568,1024]{1,0:T(8,128)(2,1)} %bitcast.32, bf16[1568,1024]{1,0:T(8,128)(2,1)} %bitcast.33, ...), custom_call_target="tpu_custom_call" | custom-call | tf_op jit(solution)/shard_map/pallas_call | solution.py:940
  290.0 0.0 copy-start
  290.0 1.4 slice.26
  291.4 0.7 slice_bitcast_fusion
  292.1 1.5 fusion
  293.6 0.0 copy-start.3
  293.6 0.6 copy.34
  294.2 0.0 copy-start.2
  294.2 1.2 copy.32
  295.4 0.9 copy.33
  296.3 0.0 copy-start.1
  296.3 2.1 copy.40
  298.5 0.0 copy-done
  298.5 1.2 copy.41
  299.6 0.0 copy-done.3
  299.6 0.7 copy.42
  300.3 0.0 copy-done.2
  300.3 0.8 copy.43
  301.1 0.0 copy-done.1
  301.1 0.8 copy.44
  (1 shorter events, 0.0 us)
Async XLA Ops:
  290.0 8.5 %copy-start = (f32[784,512]{1,0:T(8,128)S(1)}, f32[784,512]{1,0:T(8,128)}, u32[]{:S(2)}) copy-start(f32[784,512]{1,0:T(8,128)} %get-tuple-element.121) | copy-start | bytes 4816900
  293.6 6.0 %copy-start.3 = (f32[256,128]{1,0:T(8,128)S(1)}, f32[256,128]{1,0:T(8,128)}, u32[]{:S(2)}) copy-start(f32[256,128]{1,0:T(8,128)} %get-tuple-element.126) | copy-start | bytes 393220
  294.2 6.1 %copy-start.2 = (f32[128,1024]{1,0:T(8,128)S(1)}, f32[128,1024]{1,0:T(8,128)}, u32[]{:S(2)}) copy-start(f32[128,1024]{1,0:T(8,128)} %get-tuple-element.130) | copy-start | bytes 1572868
  296.3 4.7 %copy-start.1 = (f32[1024,128]{1,0:T(8,128)S(1)}, f32[1024,128]{1,0:T(8,128)}, u32[]{:S(2)}) copy-start(f32[1024,128]{1,0:T(8,128)} %get-tuple-element.132) | copy-start | bytes 1572868

commit v2 on v1

--- a/solution.py
+++ b/solution.py
@@ -10,6 +10,7 @@
 SEQ = 1568
 EPSILON = 1e-06
 CHUNKS = 7
+EARLY = 3
 F32 = jnp.float32
 BF16 = jnp.bfloat16
 MESH = pl.DeviceIdType.MESH
@@ -37,22 +38,24 @@
 
 
 def weight_blocks(ref, kind, row):
+    if kind == "three":
+        return ref.at[:, aligned(row, 128), :]
     if kind == "rows":
         return ref.at[aligned(row, 128), :]
     return ref.at[:, aligned(row, 128)]
 
 
-WEIGHT_KINDS = ("rows", "cols", "rows", "cols")
+WEIGHT_KINDS = ("three", "cols", "rows", "cols")
 
 
 def forward_kernel(
-    tok, cot, vec, attn_bias, exp_bias, win_s, wo_s, we_s, wr_s,
+    tok, cot, g_one, s_one, b_out, g_two, s_two, b_red, attn_bias, exp_bias, win_s, wo_s, we_s, wr_s,
     tok_o, cot_o, q_o, qt_o, k_o, kt_o, v_o, mixf_o, lse_o, hid_o, unit_o, inv_o,
     norm_o, act_o, slope_o, win_o, wo_o, we_o, wr_o, vec_o, one_o, stat_o,
     tok_all, cot_all, norm_one, q, qt, k, kt, v, vt, mixed, mixf, lse, hid, unit, inv, norm_two, act, slope,
-    win, wo, we, wr, vecs, stat, scores, sb, rb, xb, xr,
-    local_sem, wz_send, wz_recv, wy_send, wy_recv, vec_send, vec_recv,
-    tx_send, tx_recv, tc_send, tc_recv, cx_send, cx_recv, cc_send, cc_recv,
+    win, wo, we, wr, vecs, stat, scores, sb, rb, xr,
+    local_sem, shard_sem, tok_sem, cot_sem, wz_send, wz_recv, wy_send, wy_recv, vec_send, vec_recv,
+    tx_send, tx_recv, tc_send, tc_recv, tp_send, tp_recv, cx_send, cx_recv, cc_send, cc_recv, cp_send, cp_recv,
     h1_send, h1_recv, h2_send, h2_recv, h3_send, h3_recv,
 ):
     r, c = lax.axis_index("row"), lax.axis_index("col")
@@ -60,87 +63,154 @@
     xx, core = c // 2, c % 2
     c_x, c_core, c_far = (c + 2) % 4, c + 1 - 2 * core, (c + 2) % 4 + 1 - 2 * core
     r_y = r + 1 - 2 * y
-    z_peers = [((z + step) % 4) * 2 + y for step in (1, 2, 3)]
     half = tok.shape[0] // CHUNKS
     chunk = 2 * half
-    width = vec.shape[1]
+    width = g_one.shape[1]
     scale = LOG2E * HEAD_DIM ** (-0.5)
 
     barrier = pltpu.get_barrier_semaphore()
     for col in (c_x, c_core, c_far):
         pl.semaphore_signal(barrier, inc=1, device_id=(r, col), device_id_type=MESH)
-    for row in (r_y, *z_peers):
-        pl.semaphore_signal(barrier, inc=1, device_id=(row, c), device_id_type=MESH)
+    pl.semaphore_signal(barrier, inc=1, device_id=(r_y, c), device_id_type=MESH)
+
+    @pl.when(z >= 1)
+    def _():
+        pl.semaphore_signal(barrier, inc=1, device_id=(r - 2, c), device_id_type=MESH)
+
+    @pl.when(z <= 2)
+    def _():
+        pl.semaphore_signal(barrier, inc=1, device_id=(r + 2, c), device_id_type=MESH)
+
 
     own = aligned(c, width)
+    shards = (win_s, wo_s, we_s, wr_s)
+    fulls = (win, wo, we, wr)
+    shard_loads = [
+        pltpu.make_async_copy(shards[w], weight_blocks(fulls[w], WEIGHT_KINDS[w], r), shard_sem.at[w])
+        for w in range(4)
+    ]
+    for copy in shard_loads:
+        copy.start()
+
+    def half_source(ref, i, s):
+        return ref.at[pl.ds(pl.multiple_of(i * half, half), half), pl.ds(s * width, width)]
+
+    def half_load(ref, full_ref, sem, i, s):
+        return pltpu.make_async_copy(
+            half_source(ref, i, s), full_ref.at[i, pl.ds(s * half, half), own], sem.at[i, s]
+        )
+
     for i in range(CHUNKS):
         for s in range(2):
-            rows = pl.ds(i * half, half)
-            tok_all[i, s * half : (s + 1) * half, own] = tok[rows, s * width : (s + 1) * width]
-            cot_all[i, s * half : (s + 1) * half, own] = cot[rows, s * width : (s + 1) * width]
-    vecs[:, own] = vec[...]
-    shards = (win_s, wo_s, we_s, wr_s)
-    fulls = (win, wo, we, wr)
-    for w in range(4):
-        weight_blocks(fulls[w], WEIGHT_KINDS[w], r)[...] = shards[w][...]
-    pl.semaphore_wait(barrier, 7)
-
-    def z_send(w, step):
-        block = weight_blocks(fulls[w], WEIGHT_KINDS[w], r)
-        return remote(shards[w], block, wz_send.at[w, step], wz_recv.at[w, step], z_peers[step], c)
-
-    def z_arrival(w, step):
-        source = ((z + 4 - (step + 1)) % 4) * 2 + y
-        block = weight_blocks(fulls[w], WEIGHT_KINDS[w], source)
-        return remote(block, block, wz_send.at[w, step], wz_recv.at[w, step], source, c), source
-
-    def y_send(w, slot, row):
-        block = weight_blocks(fulls[w], WEIGHT_KINDS[w], row)
-        return remote(block, block, wy_send.at[w, slot], wy_recv.at[w, slot], r_y, c)
+            half_load(tok, tok_all, tok_sem, i, s).start()
+            if i < EARLY:
+                half_load(cot, cot_all, cot_sem, i, s).start()
+    for n, vector in enumerate((g_one, s_one, b_out, g_two, s_two, b_red, b_red, b_red)):
+        vecs[n : n + 1, own] = vector[...]
+    pl.semaphore_wait(barrier, 4 + jnp.where(z >= 1, 1, 0) + jnp.where(z <= 2, 1, 0))
+
+    def weight_ref(w, zb, side):
+        return weight_blocks(fulls[w], WEIGHT_KINDS[w], zb * 2 + side)
+
+    def line_copy(w, up, hop):
+        zb = z - hop if up else z + hop
+        block = weight_ref(w, zb, y)
+        target = (z + 1 if up else z - 1) * 2 + y
+        return remote(shards[w] if hop == 0 else block, block, wz_send.at[w, up, hop], wz_recv.at[w, up, hop], target, c)
+
+    def line_sends(up, hop):
+        return (z >= hop) & (z <= 2) if up else (z <= 3 - hop) & (z >= 1)
+
+    def line_receives(up, hop):
+        return z >= hop + 1 if up else z <= 2 - hop
+
+    def y_copy(w, zb, side):
+        block = weight_ref(w, zb, side)
+        return remote(block, block, wy_send.at[w, zb], wy_recv.at[w, zb], r_y, c)
 
     def start_weight(w):
-        for step in range(3):
-            z_send(w, step).start()
-        y_send(w, 3, r).start()
-
-    def forward_weight(w):
-        for step in (0, 2, 1):
-            arrival, source = z_arrival(w, step)
-            arrival.wait_recv()
-            y_send(w, step, source).start()
+        for up in (0, 1):
+            @pl.when(line_sends(up, 0))
+            def _():
+                line_copy(w, up, 0).start()
+
+    def own_to_y(w):
+        return remote(shards[w], weight_ref(w, z, y), wy_send.at[w, z], wy_recv.at[w, z], r_y, c)
+
+    def forward_weight(w, hop):
+        for up in (0, 1):
+            @pl.when(line_receives(up, hop))
+            def _():
+                zb = z - 1 - hop if up else z + 1 + hop
+                block = weight_ref(w, zb, y)
+                remote(block, block, wz_send.at[w, up, hop], wz_recv.at[w, up, hop], r_y, c).wait_recv()
+                y_copy(w, zb, y).start()
+
+            if hop < 2:
+                @pl.when(line_receives(up, hop) & line_sends(up, hop + 1))
+                def _():
+                    line_copy(w, up, hop + 1).start()
 
     def finish_weight(w):
-        for step in range(3):
-            z_send(w, step).wait_send()
-            source = ((z + 4 - (step + 1)) % 4) * 2 + y
-            y_send(w, step, source).wait_send()
-            pair = source + 1 - 2 * y
-            y_send(w, step, pair).wait_recv()
-        y_send(w, 3, r).wait_send()
-        y_send(w, 3, r_y).wait_recv()
-
-    def x_copy(ref, send, recv, i, col):
-        block = ref.at[i, :, aligned(col, width)]
-        return remote(block, block, send.at[i], recv.at[i], r, c_x)
-
-    def core_copy(ref, send, recv, i, slot, col):
-        block = ref.at[i, :, aligned(col, width)]
-        return remote(block, block, send.at[i, slot], recv.at[i, slot], r, c_core)
+        for up in (0, 1):
+            for hop in range(3):
+                @pl.when(line_sends(up, hop))
+                def _():
+                    line_copy(w, up, hop).wait_send()
+        for zb in range(4):
+            y_copy(w, zb, y).wait_send()
+            y_copy(w, zb, 1 - y).wait_recv()
 
     def vec_copy(slot, target, col):
         block = vecs.at[:, aligned(col, width)]
         return remote(block, block, vec_send.at[slot], vec_recv.at[slot], r, target)
 
-    for i in range(CHUNKS):
-        x_copy(tok_all, tx_send, tx_recv, i, c).start()
-        core_copy(tok_all, tc_send, tc_recv, i, 0, c).start()
+    def half_x(ref, full_ref, send, recv, i, s, col):
+        block = full_ref.at[i, pl.ds(s * half, half), aligned(col, width)]
+        return remote(half_source(ref, i, s), block, send.at[i, s], recv.at[i, s], r, c_x)
+
+    def half_core(ref, full_ref, send, recv, i, s, col):
+        block = full_ref.at[i, pl.ds(s * half, half), aligned(col, width)]
+        return remote(half_source(ref, i, s), block, send.at[i, s], recv.at[i, s], r, c_core)
+
+    def tok_x(i, s, col):
+        return half_x(tok, tok_all, tx_send, tx_recv, i, s, col)
+
+    def tok_core(i, s, col):
+        return half_core(tok, tok_all, tc_send, tc_recv, i, s, col)
+
+    def cot_x(i, s, col):
+        return half_x(cot, cot_all, cx_send, cx_recv, i, s, col)
+
+    def cot_core(i, s, col):
+        return half_core(cot, cot_all, cc_send, cc_recv, i, s, col)
+
+    def pass_core(full_ref, send, recv, i, col):
+        block = full_ref.at[i, :, aligned(col, width)]
+        return remote(block, block, send.at[i], recv.at[i], r, c_core)
+
+    def tok_pass(i, col):
+        return pass_core(tok_all, tp_send, tp_recv, i, col)
+
+    def cot_pass(i, col):
+        return pass_core(cot_all, cp_send, cp_recv, i, col)
+
+    def send_cot(i):
+        for s in range(2):
+            cot_x(i, s, c).start()
+            cot_core(i, s, c).start()
+
+    def send_tok(i):
+        for s in range(2):
+            tok_x(i, s, c).start()
+            tok_core(i, s, c).start()
+
+    start_weight(0)
+    own_to_y(0).start()
+    send_tok(0)
+    send_tok(1)
     for slot, target in enumerate((c_x, c_core, c_far)):
         vec_copy(slot, target, c).start()
-    start_weight(0)
-    start_weight(1)
-    for slot, target in enumerate((c_x, c_core, c_far)):
-        vec_copy(slot, target, c).wait_send()
-        vec_copy(slot, target, target).wait_recv()
 
     def keep(index, i, src, dst):
         return pltpu.make_async_copy(src, dst, local_sem.at[index, i])
@@ -165,38 +235,87 @@
 
     lane_ids = lax.broadcasted_iota(jnp.int32, (chunk // 7, 128), 1)
 
-    @pl.loop(0, CHUNKS)
-    def _(i):
-        x_copy(tok_all, tx_send, tx_recv, i, c_x).wait_recv()
-        core_copy(tok_all, tc_send, tc_recv, i, 1, c_x).start()
-        core_copy(tok_all, tc_send, tc_recv, i, 0, c_core).wait_recv()
-        core_copy(tok_all, tc_send, tc_recv, i, 1, c_far).wait_recv()
+    def first_norm(i):
+        for s in range(2):
+            half_load(tok, tok_all, tok_sem, i, s).wait()
+            tok_core(i, s, c_core).wait_recv()
+        tok_pass(i, c_far).wait_recv()
         for part in range(7):
             rows = pl.ds(part * (chunk // 7), chunk // 7)
             units, mean, inverse = row_norm(tok_all[i, rows, :].astype(F32))
             stat[i, rows, :] = jnp.where(lane_ids < 64, mean, inverse)
             norm_one[i, rows, :] = (units * vecs[0:1, :] + vecs[1:2, :]).astype(BF16)
 
-    forward_weight(0)
-    start_weight(2)
-    forward_weight(1)
+    @pl.loop(0, CHUNKS // 2 + 1)
+    def _(g):
+        @pl.loop(2 * g, jnp.minimum(2 * g + 2, CHUNKS))
+        def _(i):
+            for s in range(2):
+                tok_x(i, s, c_x).wait_recv()
+
+            @pl.when(i + 2 < CHUNKS)
+            def _():
+                send_tok(i + 2)
+
+            @pl.when(i == CHUNKS - 2)
+            def _():
+                send_cot(0)
+
+            tok_pass(i, c_x).start()
+
+        @pl.when(g == 0)
+        def _():
+            for slot, target in enumerate((c_x, c_core, c_far)):
+                vec_copy(slot, target, c).wait_send()
+                vec_copy(slot, target, target).wait_recv()
+
+        for hop in range(3):
+            @pl.when(g == hop)
+            def _():
+                forward_weight(0, hop)
+
+        @pl.when(g == 2)
+        def _():
+            start_weight(1)
+            start_weight(2)
+
+        @pl.loop(2 * g, jnp.minimum(2 * g + 2, CHUNKS))
+        def _(i):
+            first_norm(i)
+
+    send_cot(1)
+    send_cot(2)
+    forward_weight(1, 0)
+    for w in range(4):
+        shard_loads[w].wait()
     finish_weight(0)
+    own_to_y(1).start()
+    own_to_y(2).start()
+    forward_weight(1, 1)
 
     @pl.loop(0, CHUNKS)
     def _(i):
-        part = jnp.dot(norm_one[i], win[:, 0:width], preferred_element_type=F32)
+        part = jnp.dot(norm_one[i], win[0], preferred_element_type=F32)
         part = (part + attn_bias[0:1, :]).astype(BF16)
         q[i] = part
         qt[i] = part.T
-        part = jnp.dot(norm_one[i], win[:, width : 2 * width], preferred_element_type=F32).astype(BF16)
+        part = jnp.dot(norm_one[i], win[1], preferred_element_type=F32).astype(BF16)
         k[i] = part
         kt[i] = part.T
-        part = jnp.dot(norm_one[i], win[:, 2 * width : 3 * width], preferred_element_type=F32)
+        part = jnp.dot(norm_one[i], win[2], preferred_element_type=F32)
         part = (part + attn_bias[1:2, :]).astype(BF16)
         v[i] = part
         vt[i] = part.T
         for copy in kept(i, 0):
             copy.start()
+
+        @pl.when(i == 2)
+        def _():
+            forward_weight(1, 2)
+
+        @pl.when(i == 4)
+        def _():
+            forward_weight(2, 0)
 
     finish_weight(1)
 
@@ -236,96 +355,125 @@
         return remote(sb.at[slot, 1 - core], rb.at[i], h1_send.at[i], h1_recv.at[i], r, c_core)
 
     def h2(i):
-        return remote(xb.at[i % 2], xr.at[i], h2_send.at[i], h2_recv.at[i], r, c_x)
+        return remote(rb.at[i], xr.at[i], h2_send.at[i], h2_recv.at[i], r, c_x)
 
     def h3(i, x, side):
         block = hid.at[i, :, aligned(x * 2 + side, width)]
         return remote(block, block, h3_send.at[i, x], h3_recv.at[i, x], r, c_core)
 
-    @pl.loop(0, CHUNKS + 2)
-    def _(i):
-        @pl.when(i < CHUNKS)
-        def _():
-            x_copy(cot_all, cx_send, cx_recv, i, c).start()
-            core_copy(cot_all, cc_send, cc_recv, i, 0, c).start()
-            attend(i)
-            for copy in kept(i, 1):
-                copy.start()
-            partial = jnp.dot(mixed[i], wo[...], preferred_element_type=F32)
-            for x in range(2):
-                for side in range(2):
-                    block = x * 2 + side
-                    sb[i % 2, side, x] = partial[:, block * width : (block + 1) * width].astype(BF16)
-            h1(i).start()
-
-        @pl.when(i == 1)
-        def _():
-            forward_weight(2)
-            start_weight(3)
-
-        @pl.when(i == 2)
-        def _():
-            finish_weight(2)
-
-        @pl.when(i == 5)
-        def _():
-            forward_weight(3)
-
-        @pl.when(i >= 2)
-        def _():
-            t = i - 2
-            for x in range(2):
-                h3(t, x, core).wait_send()
-                h3(t, x, 1 - core).wait_recv()
-            for part in range(7):
-                rows = pl.ds(part * (chunk // 7), chunk // 7)
-                units, _, inverse = row_norm(hid[t, rows, :])
-                unit[t, rows, :] = units.astype(BF16)
-                inv[t, rows, :] = jnp.broadcast_to(inverse, (chunk // 7, 128))
-                norm_two[t, rows, :] = (units * vecs[3:4, :] + vecs[4:5, :]).astype(BF16)
-            for n in range(we.shape[1] // 256):
-                lanes = slice(n * 256, (n + 1) * 256)
-                expanded = jnp.dot(norm_two[t], we[:, lanes], preferred_element_type=F32) + exp_bias[:, lanes]
-                gate = 0.5 + 0.5 * lax.erf(expanded * (0.5 ** 0.5))
-                act[t, :, lanes] = (expanded * gate).astype(BF16)
-                bell = jnp.exp2(expanded * expanded * (-0.5 * LOG2E)) * 0.3989422804014327
-                slope[t, :, lanes] = (gate + expanded * bell).astype(BF16)
-            for copy in kept(t, 2):
-                copy.start()
-            keep_hid(t).start()
-
-        @pl.when(i < CHUNKS)
-        def _():
-            h1(i).wait()
-            for x in range(2):
-                xb[i % 2, x] = (sb[i % 2, core, x].astype(F32) + rb[i, x].astype(F32)).astype(BF16)
-            h2(i).start()
-
-        @pl.when((i >= 1) & (i <= CHUNKS))
-        def _():
-            t = i - 1
-            x_copy(cot_all, cx_send, cx_recv, t, c_x).wait_recv()
-            core_copy(cot_all, cc_send, cc_recv, t, 1, c_x).start()
-            h2(t).wait()
-            for x in range(2):
-                lanes = aligned(x * 2 + core, width)
-                total = xb[t % 2, x].astype(F32) + xr[t, x].astype(F32)
-                hid[t, :, lanes] = tok_all[t, :, lanes].astype(F32) + total + vecs[2:3, lanes]
-            for x in range(2):
-                h3(t, x, core).start()
+    def expand(t):
+        for x in range(2):
+            h3(t, x, core).wait_send()
+            h3(t, x, 1 - core).wait_recv()
+        for part in range(7):
+            rows = pl.ds(part * (chunk // 7), chunk // 7)
+            units, _, inverse = row_norm(hid[t, rows, :])
+            unit[t, rows, :] = units.astype(BF16)
+            inv[t, rows, :] = jnp.broadcast_to(inverse, (chunk // 7, 128))
+            norm_two[t, rows, :] = (units * vecs[3:4, :] + vecs[4:5, :]).astype(BF16)
+        for n in range(we.shape[1] // 256):
+            lanes = slice(n * 256, (n + 1) * 256)
+            expanded = jnp.dot(norm_two[t], we[:, lanes], preferred_element_type=F32) + exp_bias[:, lanes]
+            gate = 0.5 + 0.5 * lax.erf(expanded * (0.5 ** 0.5))
+            act[t, :, lanes] = (expanded * gate).astype(BF16)
+            bell = jnp.exp2(expanded * expanded * (-0.5 * LOG2E)) * 0.3989422804014327
+            slope[t, :, lanes] = (gate + expanded * bell).astype(BF16)
+        for copy in kept(t, 2):
+            copy.start()
+        keep_hid(t).start()
+
+    def spread_hidden(t):
+        h2(t).wait()
+        for x in range(2):
+            lanes = aligned(x * 2 + core, width)
+            total = rb[t, x].astype(F32) + xr[t, x].astype(F32)
+            hid[t, :, lanes] = tok_all[t, :, lanes].astype(F32) + total + vecs[2:3, lanes]
+        for x in range(2):
+            h3(t, x, core).start()
 
     @pl.loop(0, CHUNKS)
     def _(i):
-        x_copy(tok_all, tx_send, tx_recv, i, c).wait_send()
-        x_copy(cot_all, cx_send, cx_recv, i, c).wait_send()
-        core_copy(tok_all, tc_send, tc_recv, i, 0, c).wait_send()
-        core_copy(tok_all, tc_send, tc_recv, i, 1, c_x).wait_send()
-        core_copy(cot_all, cc_send, cc_recv, i, 0, c).wait_send()
-        core_copy(cot_all, cc_send, cc_recv, i, 1, c_x).wait_send()
-        core_copy(cot_all, cc_send, cc_recv, i, 0, c_core).wait_recv()
-        core_copy(cot_all, cc_send, cc_recv, i, 1, c_far).wait_recv()
+        attend(i)
+        for copy in kept(i, 1):
+            copy.start()
+        partial = jnp.dot(mixed[i], wo[...], preferred_element_type=F32)
+        for x in range(2):
+            for side in range(2):
+                block = x * 2 + side
+                sb[i % 2, side, x] = partial[:, block * width : (block + 1) * width].astype(BF16)
+        h1(i).start()
+
+        @pl.when(i == 0)
+        def _():
+            forward_weight(2, 1)
+
+        @pl.when(i == 1)
+        def _():
+            forward_weight(2, 2)
+            start_weight(3)
+
+        @pl.when(i == 2)
+        def _():
+            own_to_y(3).start()
+            forward_weight(3, 0)
+
+        @pl.when(i == 3)
+        def _():
+            forward_weight(3, 1)
+
+        @pl.when(i == 4)
+        def _():
+            forward_weight(3, 2)
+
+        @pl.when((i >= 1) & (i <= EARLY))
+        def _():
+            for s in range(2):
+                cot_x(i - 1, s, c_x).wait_recv()
+                half_load(cot, cot_all, cot_sem, i - 1, s).wait()
+            cot_pass(i - 1, c_x).start()
+
+        h1(i).wait()
+        for x in range(2):
+            rb[i, x] = (sb[i % 2, core, x].astype(F32) + rb[i, x].astype(F32)).astype(BF16)
+        h2(i).start()
+
+        @pl.when(i >= 1)
+        def _():
+            spread_hidden(i - 1)
+
+        @pl.when(i == 5)
+        def _():
+            finish_weight(2)
+
+        @pl.loop(jnp.maximum(2 * (i - 5), 0), jnp.maximum(2 * (i - 4), 0))
+        def _(t):
+            expand(t)
+
+    @pl.loop(4, CHUNKS)
+    def _(t):
+        @pl.when(t == CHUNKS - 1)
+        def _():
+            spread_hidden(CHUNKS - 1)
+
+        expand(t)
+
+    @pl.loop(0, EARLY)
+    def _(i):
+        for s in range(2):
+            cot_x(i, s, c).wait_send()
+            cot_core(i, s, c).wait_send()
+            cot_core(i, s, c_core).wait_recv()
+        cot_pass(i, c_x).wait_send()
+        cot_pass(i, c_far).wait_recv()
         for copy in kept(i, 3):
             copy.start()
+
+    @pl.loop(0, CHUNKS)
+    def _(i):
+        for s in range(2):
+            tok_x(i, s, c).wait_send()
+            tok_core(i, s, c).wait_send()
+        tok_pass(i, c_x).wait_send()
 
     finish_weight(3)
     last = [
@@ -337,17 +485,23 @@
 
     @pl.loop(0, CHUNKS)
     def _(i):
-        for stage in range(4):
+        for stage in range(3):
             for copy in kept(i, stage):
                 copy.wait()
         keep_hid(i).wait()
 
+        @pl.when(i < EARLY)
+        def _():
+            for copy in kept(i, 3):
+                copy.wait()
+
     for copy in last:
         copy.wait()
 
 
-def forward_call(tok, cot, vec, attn_bias, exp_bias, win_s, wo_s, we_s, wr_s):
-    pairs, width = tok.shape[0], vec.shape[1]
+def forward_call(*arrays):
+    tok, we_s = arrays[0], arrays[-2]
+    pairs, width = tok.shape[0], tok.shape[1] // 2
     chunk = 2 * pairs // CHUNKS
     full = 4 * width
     hidden = we_s.shape[1]
@@ -358,7 +512,7 @@
 
     outs = [
         sd((n, chunk, full), BF16),
-        sd((n, chunk, full), BF16),
+        sd((EARLY, chunk, full), BF16),
         sd((n, chunk, width), BF16),
         sd((n, width, chunk), BF16),
         sd((n, chunk, width), BF16),
@@ -372,7 +526,7 @@
         sd((n, chunk, full), BF16),
         sd((n, chunk, hidden), BF16),
         sd((n, chunk, hidden), BF16),
-        sd((full, 3 * width), BF16),
+        sd((3, full, width), BF16),
         sd((width, full), BF16),
         sd((full, hidden), BF16),
         sd((hidden, full), BF16),
@@ -383,39 +537,40 @@
     vm = pltpu.VMEM
     dma = pltpu.SemaphoreType.DMA
     scratch = [
-        vm((n, chunk, full), BF16), vm((n, chunk, full), BF16), vm((n, chunk, full), BF16),
+        vm((n, chunk, full), BF16), vm((EARLY, chunk, full), BF16), vm((n, chunk, full), BF16),
         vm((n, chunk, width), BF16), vm((n, width, chunk), BF16),
         vm((n, chunk, width), BF16), vm((n, width, chunk), BF16),
         vm((n, chunk, width), BF16), vm((n, width, chunk), BF16),
         vm((n, chunk, width), BF16), vm((n, chunk, width), F32), vm((n, 8, chunk), F32),
         vm((n, chunk, full), F32), vm((n, chunk, full), BF16), vm((n, chunk, 128), F32),
         vm((n, chunk, full), BF16), vm((n, chunk, hidden), BF16), vm((n, chunk, hidden), BF16),
-        vm((full, 3 * width), BF16), vm((width, full), BF16), vm((full, hidden), BF16), vm((hidden, full), BF16),
+        vm((3, full, width), BF16), vm((width, full), BF16), vm((full, hidden), BF16), vm((hidden, full), BF16),
         vm((8, full), F32), vm((n, chunk, 128), F32),
         vm((2, n, chunk, chunk), F32),
         vm((2, 2, 2, chunk, width), BF16), vm((n, 2, chunk, width), BF16),
-        vm((2, 2, chunk, width), BF16), vm((n, 2, chunk, width), BF16),
-        dma((18, n)), dma((4, 3)), dma((4, 3)), dma((4, 4)), dma((4, 4)), dma((3,)), dma((3,)),
-        dma((n,)), dma((n,)), dma((n, 2)), dma((n, 2)), dma((n,)), dma((n,)), dma((n, 2)), dma((n, 2)),
+        vm((n, 2, chunk, width), BF16),
+        dma((18, n)), dma((4,)), dma((n, 2)), dma((EARLY, 2)), dma((4, 2, 3)), dma((4, 2, 3)), dma((4, 4)), dma((4, 4)), dma((3,)), dma((3,)),
+        dma((n, 2)), dma((n, 2)), dma((n, 2)), dma((n, 2)), dma((n,)), dma((n,)),
+        dma((EARLY, 2)), dma((EARLY, 2)), dma((EARLY, 2)), dma((EARLY, 2)), dma((EARLY,)), dma((EARLY,)),
         dma((n,)), dma((n,)), dma((n,)), dma((n,)), dma((n, 2)), dma((n, 2)),
     ]
     return pl.pallas_call(
         forward_kernel,
         out_shape=outs,
-        in_specs=[pl.BlockSpec(memory_space=pltpu.VMEM)] * 9,
+        in_specs=[pl.BlockSpec(memory_space=pl.ANY if n in (0, 1, 10, 11, 12, 13) else pltpu.VMEM) for n in range(len(arrays))],
         out_specs=[pl.BlockSpec(memory_space=pl.ANY)] * len(outs),
         scratch_shapes=scratch,
         compiler_params=pltpu.CompilerParams(
             collective_id=0, has_side_effects=True, vmem_limit_bytes=63 << 20
         ),
-    )(tok, cot, vec, attn_bias, exp_bias, win_s, wo_s, we_s, wr_s)
-
-
-GRAD_KINDS = ("rows", "cols", "rows", "cols")
+    )(*arrays)
+
+
+GRAD_KINDS = ("three", "cols", "rows", "cols")
 
 
 def backward_kernel(
-    tok_h, cot_h, q_h, qt_h, k_h, kt_h, v_h, mixf_h, lse_h, hid_h, unit_h, inv_h,
+    tok_h, cot_h, cot_in, q_h, qt_h, k_h, kt_h, v_h, mixf_h, lse_h, hid_h, unit_h, inv_h,
     normed_h, act_h, slope_h, win_h, wo_h, we_h, wr_h, vec_h, one_h, stat_h,
     out_o, tg_o, sums_o, gin_o, gout_o, gexp_o, gred_o,
     cot, q, qt, k, kt, v, mixf, lse, hid, unit, inv, normed, act, slope, win, wo, we, wr, vecs, stat,
@@ -424,7 +579,7 @@
     ys_in, ys_out, ys_exp, ys_red, oh_in, oh_out, oh_exp, oh_red,
     yr_in, yr_out, yr_exp, yr_red, zr_in, zr_out, zr_exp, zr_red,
     gin, gout, gexp, gred,
-    load_sem, store_sem, hid_sem, gy_send, gy_recv, gz_send, gz_recv,
+    load_sem, store_sem, hid_sem, cot_sem, cx_send, cx_recv, cc_send, cc_recv, cp_send, cp_recv, gy_send, gy_recv, gz_send, gz_recv,
     h1g_send, h1g_recv, h2g_send, h2g_recv, h3g_send, h3g_recv,
     h1o_send, h1o_recv, h2o_send, h2o_recv, h1t_send, h1t_recv, h2t_send, h2t_recv,
     st_send, st_recv, pk_send, pk_recv,
@@ -451,7 +606,7 @@
 
     loads = {}
     order = (
-        ("wr", wr_h, wr), ("cot", cot_h, cot), ("slope", slope_h, slope), ("we", we_h, we), ("act", act_h, act),
+        ("wr", wr_h, wr), ("cot", cot_h, cot.at[pl.ds(0, EARLY * chunk), :]), ("slope", slope_h, slope), ("we", we_h, we), ("act", act_h, act),
         ("vec", vec_h, vecs), ("unit", unit_h, unit), ("inv", inv_h, inv), ("wo", wo_h, wo),
         ("normed", normed_h, normed), ("mixf", mixf_h, mixf), ("lse", lse_h, lse), ("qt", qt_h, qt), ("q", q_h, q),
         ("k", k_h, k), ("v", v_h, v), ("kt", kt_h, kt), ("win", win_h, win), ("stat", stat_h, stat),
@@ -463,6 +618,18 @@
     for name, _, _ in order:
         if name not in late:
             loads[name].start()
+    def cot_source(i, s):
+        return cot_in.at[pl.ds(pl.multiple_of(i * half, half), half), pl.ds(s * width, width)]
+
+    def cot_block(i, s, col):
+        return cot.at[pl.ds(pl.multiple_of(i * chunk + s * half, half), half), aligned(col, width)]
+
+    def cot_load(i, s):
+        return pltpu.make_async_copy(cot_source(i, s), cot_block(i, s, c), cot_sem.at[i, s])
+
+    for i in range(EARLY, CHUNKS):
+        for s in range(2):
+            cot_load(i, s).start()
     dk[...] = jnp.zeros_like(dk)
     dv[...] = jnp.zeros_like(dv)
     col_sums[...] = jnp.zeros_like(col_sums)
@@ -472,6 +639,38 @@
     def rows_of(i):
         return pl.ds(pl.multiple_of(i * chunk, chunk), chunk)
 
+    def cot_x(i, s, col):
+        return remote(cot_source(i, s), cot_block(i, s, col), cx_send.at[i, s], cx_recv.at[i, s], r, c_x)
+
+    def cot_core(i, s, col):
+        return remote(cot_source(i, s), cot_block(i, s, col), cc_send.at[i, s], cc_recv.at[i, s], r, c_core)
+
+    def cot_pass(i, col):
+        block = cot.at[rows_of(i), aligned(col, width)]
+        return remote(block, block, cp_send.at[i], cp_recv.at[i], r, c_core)
+
+    def send_cot(i):
+        for s in range(2):
+            cot_x(i, s, c).start()
+            cot_core(i, s, c).start()
+
+    def pass_cot(i):
+        for s in range(2):
+            cot_x(i, s, c_x).wait_recv()
+        cot_pass(i, c_x).start()
+
+    def finish_cot(i):
+        for s in range(2):
+            cot_load(i, s).wait()
+            cot_x(i, s, c).wait_send()
+            cot_core(i, s, c).wait_send()
+            cot_core(i, s, c_core).wait_recv()
+        cot_pass(i, c_x).wait_send()
+        cot_pass(i, c_far).wait_recv()
+
+    send_cot(EARLY)
+    send_cot(EARLY + 1)
+
     def h1(sb, rb, send, recv, i):
         return remote(sb.at[i % 2, 1 - core], rb.at[i], send.at[i], recv.at[i], r, c_core)
 
@@ -509,6 +708,13 @@
 
     def spread_grad(i):
         h2g(i).wait()
+        if isinstance(i, int):
+            h2g(i + 2).start()
+        else:
+            @pl.when(i + 2 < CHUNKS)
+            def _():
+                h2g(i + 2).start()
+
         for x in range(2):
             grad[i % 4, :, aligned(x * 2 + core, width)] = rb_g[i, x].astype(F32) + xr_g[i, x].astype(F32)
         for x in range(2):
@@ -546,8 +752,6 @@
             oh[w][s] = high
             ys[w][s] = low
 
-        gy(w, s).start()
-
     def pass_on(w, s):
         gy(w, s).wait()
         oh[w][s] = (oh[w][s].astype(F32) + yr[w][s].astype(F32)).astype(BF16)
@@ -567,41 +771,58 @@
     loads["we"].wait()
     loads["act"].wait()
 
-    @pl.loop(0, CHUNKS + 1)
+    @pl.loop(0, CHUNKS)
     def _(i):
-        @pl.when(i < CHUNKS)
-        def _():
-            rows = rows_of(i)
-            for n in range(slope.shape[1] // 256):
-                lanes = slice(n * 256, (n + 1) * 256)
-                grad_act = lax.dot_general(cot[rows, :], wr[lanes, :], NT_DIMS, preferred_element_type=F32)
-                low = (slope[rows, lanes].astype(F32) * grad_act).astype(BF16)
-                slope[rows, lanes] = low
-                hid_sums[0:1, lanes] += jnp.sum(low.astype(F32), axis=0, keepdims=True)
-            fill(sb_g, i, lax.dot_general(slope[rows, :], we[...], NT_DIMS, preferred_element_type=F32))
-            h1g(i).start()
+        @pl.when(i >= EARLY)
+        def _():
+            finish_cot(i)
+
+        rows = rows_of(i)
+        for n in range(slope.shape[1] // 256):
+            lanes = slice(n * 256, (n + 1) * 256)
+            grad_act = lax.dot_general(cot[rows, :], wr[lanes, :], NT_DIMS, preferred_element_type=F32)
+            low = (slope[rows, lanes].astype(F32) * grad_act).astype(BF16)
+            slope[rows, lanes] = low
+            hid_sums[0:1, lanes] += jnp.sum(low.astype(F32), axis=0, keepdims=True)
+        fill(sb_g, i, lax.dot_general(slope[rows, :], we[...], NT_DIMS, preferred_element_type=F32))
+        h1g(i).start()
 
         @pl.when(i >= 1)
         def _():
             h1o(i - 1).wait()
             merge(sb_o, rb_o, i - 1)
 
-        @pl.when(i < CHUNKS)
-        def _():
-            rows = rows_of(i)
-            fill(sb_o, i, jnp.dot(act[rows, :], wr[...], preferred_element_type=F32))
-            h1o(i).start()
-            h1g(i).wait()
-            merge(sb_g, rb_g, i)
-            h2g(i).start()
-            col_sums[0:1, :] += jnp.sum(cot[rows, :].astype(F32), axis=0, keepdims=True)
-
+        fill(sb_o, i, jnp.dot(act[rows, :], wr[...], preferred_element_type=F32))
+        h1o(i).start()
+        h1g(i).wait()
+        merge(sb_g, rb_g, i)
+
+        @pl.when((i >= 1) & (i + 2 < CHUNKS))
+        def _():
+            pass_cot(i + 2)
+
+            @pl.when(i + 4 < CHUNKS)
+            def _():
+                send_cot(i + 4)
+
+        @pl.when((i == 3) | (i == 4))
+        def _():
+            h2g(i - 3).start()
+
+        col_sums[0:1, :] += jnp.sum(cot[rows, :].astype(F32), axis=0, keepdims=True)
+
+    h1o(CHUNKS - 1).wait()
+    merge(sb_o, rb_o, CHUNKS - 1)
     loads["normed"].wait()
     for s in range(3):
         grad_block(3, s, act[...], cot)
+        if s < 2:
+            gy(3, s).start()
     spread_grad(0)
     for s in range(3):
         grad_block(2, s, normed, slope[...])
+    pass_on(3, 0)
+    gy(3, 2).start()
     spread_grad(1)
     grad_block(3, 3, act[...], cot)
     grad_block(2, 3, normed, slope[...])
@@ -632,51 +853,47 @@
         go_t = go.T
         row_ids = lax.broadcasted_iota(jnp.int32, (128, chunk), 0)
         lane_ids = lax.broadcasted_iota(jnp.int32, (chunk, 128), 1)
-        for pair in range(width // 128):
-            lanes = slice(pair * 128, (pair + 1) * 128)
-            queries, grads, query_rows, grad_rows, deltas, logs = [], [], [], [], [], []
-            for h in range(2):
-                pick = row_ids // HEAD_DIM == h
-                value = qt[i, lanes, :]
-                queries.append(jnp.where(pick, value, jnp.zeros_like(value)))
-                value = go_t[lanes, :]
-                grads.append(jnp.where(pick, value, jnp.zeros_like(value)))
-                pick = lane_ids // HEAD_DIM == h
-                value = q[rows, lanes]
-                query_rows.append(jnp.where(pick, value, jnp.zeros_like(value)))
-                value = go[:, lanes]
-                grad_rows.append(jnp.where(pick, value, jnp.zeros_like(value)))
-                first = pair * 128 + h * HEAD_DIM
-                deltas.append(jnp.sum(inner[first : first + HEAD_DIM, :], axis=0, keepdims=True))
-                logs.append(lse[i, pair * 2 + h : pair * 2 + h + 1, :])
-
-            def step(j, query_grads):
-                keys = rows_of(j)
-                key_block = k[keys, lanes]
-                value_block = v[keys, lanes]
-                key_sum = dk[keys, lanes]
-                value_sum = dv[keys, lanes]
-                results = []
-                for h in range(2):
-                    block = jnp.dot(key_block, queries[h], preferred_element_type=F32)
-                    probs = jnp.exp2(block * scale - logs[h])
-                    grad_probs = jnp.dot(value_block, grads[h], preferred_element_type=F32)
-                    grad_scores = (probs * (grad_probs - deltas[h])).astype(BF16)
-                    value_sum = value_sum + jnp.dot(probs.astype(BF16), grad_rows[h], preferred_element_type=F32)
-                    key_sum = key_sum + jnp.dot(grad_scores, query_rows[h], preferred_element_type=F32)
-                    first = pair * 128 + h * HEAD_DIM
-                    results.append(
-                        query_grads[h]
-                        + jnp.dot(kt[j, first : first + HEAD_DIM, :], grad_scores, preferred_element_type=F32)
-                    )
-                dk[keys, lanes] = key_sum
-                dv[keys, lanes] = value_sum
-                return tuple(results)
-
-            empty = jnp.zeros((HEAD_DIM, chunk), F32)
-            parts = lax.fori_loop(0, CHUNKS, step, (empty, empty))
-            query_grad = (jnp.concatenate(parts, axis=0).T * HEAD_DIM ** (-0.5)).astype(BF16)
-            dq[rows, lanes] = query_grad
+        heads = width // HEAD_DIM
+        queries, grads, query_rows, grad_rows, deltas, logs = [], [], [], [], [], []
+        for h in range(heads):
+            lanes = slice(h // 2 * 128, h // 2 * 128 + 128)
+            pick = row_ids // HEAD_DIM == h % 2
+            value = qt[i, lanes, :]
+            queries.append(jnp.where(pick, value, jnp.zeros_like(value)))
+            value = go_t[lanes, :]
+            grads.append(jnp.where(pick, value, jnp.zeros_like(value)))
+            pick = lane_ids // HEAD_DIM == h % 2
+            value = q[rows, lanes]
+            query_rows.append(jnp.where(pick, value, jnp.zeros_like(value)))
+            value = go[:, lanes]
+            grad_rows.append(jnp.where(pick, value, jnp.zeros_like(value)))
+            deltas.append(jnp.sum(inner[h * HEAD_DIM : (h + 1) * HEAD_DIM, :], axis=0, keepdims=True))
+            logs.append(lse[i, h : h + 1, :])
+
+        parts = [jnp.zeros((HEAD_DIM, chunk), F32)] * heads
+        for j in range(CHUNKS):
+            keys = pl.ds(j * chunk, chunk)
+            probs, grad_scores = [], []
+            for h in range(heads):
+                lanes = slice(h // 2 * 128, h // 2 * 128 + 128)
+                block = jnp.dot(k[keys, lanes], queries[h], preferred_element_type=F32)
+                grad_probs = jnp.dot(v[keys, lanes], grads[h], preferred_element_type=F32)
+                prob = jnp.exp2(block * scale - logs[h])
+                probs.append(prob.astype(BF16))
+                grad_scores.append((prob * (grad_probs - deltas[h])).astype(BF16))
+            for pair in range(heads // 2):
+                lanes = slice(pair * 128, pair * 128 + 128)
+                h = 2 * pair
+                dv[keys, lanes] += jnp.dot(
+                    probs[h], grad_rows[h], preferred_element_type=F32
+                ) + jnp.dot(probs[h + 1], grad_rows[h + 1], preferred_element_type=F32)
+                dk[keys, lanes] += jnp.dot(
+                    grad_scores[h], query_rows[h], preferred_element_type=F32
+                ) + jnp.dot(grad_scores[h + 1], query_rows[h + 1], preferred_element_type=F32)
+            for h in range(heads):
+                rows_h = slice(h * HEAD_DIM, (h + 1) * HEAD_DIM)
+                parts[h] = parts[h] + jnp.dot(kt[j, rows_h, :], grad_scores[h], preferred_element_type=F32)
+        dq[rows, :] = (jnp.concatenate(parts, axis=0).T * HEAD_DIM ** (-0.5)).astype(BF16)
 
     def finish_out(i):
         h2o(i).wait()
@@ -690,7 +907,6 @@
 
     @pl.loop(0, CHUNKS)
     def _(i):
-        h2o(i).start()
         hid_load(i).start()
         for x in range(2):
             h3g(i, x, core).wait_send()
@@ -713,20 +929,19 @@
             grad[i % 4, span, :] = total
         for s in range(2):
             tg[i, s] = grad[i % 4, s * half : (s + 1) * half, own]
+        h2o(i).start()
         attend_back(i)
 
         @pl.when(i + 2 < CHUNKS)
         def _():
             spread_grad(i + 2)
 
-        for s in range(3):
-            @pl.when(i == s)
+        queue = ((3, 0), (3, 1), (3, 2), (2, 0), (2, 1), (2, 2), (3, 3), (2, 3))
+        for at in range(5):
+            @pl.when(i == at)
             def _():
-                pass_on(3, s)
-
-            @pl.when(i == s + 3)
-            def _():
-                pass_on(2, s)
+                pass_on(*queue[at + 1])
+                gy(*queue[at + 3]).start()
 
         @pl.when(i >= 1)
         def _():
@@ -754,18 +969,17 @@
         zt = (z + 1 + s) % 4
         left = one[:, aligned(zt, 256)]
         for n, right in enumerate((dq, k, v)):
-            lanes = slice(n * width, (n + 1) * width)
             block = lax.dot_general(left, right[...], TN_DIMS, preferred_element_type=F32).astype(BF16)
 
             @pl.when(y == 0)
             def _():
-                oh_in[s, :, lanes] = block[0:128, :]
-                ys_in[s, :, lanes] = block[128:256, :]
+                oh_in[s, n] = block[0:128, :]
+                ys_in[s, n] = block[128:256, :]
 
             @pl.when(y == 1)
             def _():
-                oh_in[s, :, lanes] = block[128:256, :]
-                ys_in[s, :, lanes] = block[0:128, :]
+                oh_in[s, n] = block[128:256, :]
+                ys_in[s, n] = block[0:128, :]
 
         gy(0, s).start()
 
@@ -783,12 +997,12 @@
         @pl.when(i < CHUNKS)
         def _():
             rows = rows_of(i)
-            partial = lax.dot_general(dq[rows, :], win[:, 0:width], NT_DIMS, preferred_element_type=F32)
+            partial = lax.dot_general(dq[rows, :], win[0], NT_DIMS, preferred_element_type=F32)
             partial = partial + lax.dot_general(
-                k[rows, :], win[:, width : 2 * width], NT_DIMS, preferred_element_type=F32
+                k[rows, :], win[1], NT_DIMS, preferred_element_type=F32
             )
             partial = partial + lax.dot_general(
-                v[rows, :], win[:, 2 * width : 3 * width], NT_DIMS, preferred_element_type=F32
+                v[rows, :], win[2], NT_DIMS, preferred_element_type=F32
             )
             fill(sb_g, i, partial)
             h1t(i).start()
@@ -813,11 +1027,13 @@
         def _():
             for s in range(3):
                 grad_block(1, s, mixf[...].astype(BF16), unit)
+                gy(1, s).start()
 
         @pl.when(i == 5)
         def _():
             inward_block(3)
             grad_block(1, 3, mixf[...].astype(BF16), unit)
+            gy(1, 3).start()
 
         @pl.when(i == 6)
         def _():
@@ -892,7 +1108,7 @@
 
 
 def backward_call(*arrays):
-    (tok, cot, q, qt, k, kt, v, mixf, lse, hid, unit, inv, normed, act, slope, win, wo, we, wr, vec, one, stat) = arrays
+    (tok, cot, cot_in, q, qt, k, kt, v, mixf, lse, hid, unit, inv, normed, act, slope, win, wo, we, wr, vec, one, stat) = arrays
     rows, width = q.shape
     full, hidden = we.shape
     n, chunk = CHUNKS, rows // CHUNKS
@@ -904,14 +1120,14 @@
 
     outs = [
         sd((pairs, 2 * width), BF16), sd((pairs, 2 * width), F32), sd((16, width), F32),
-        sd((128, 3 * width), F32), sd((width, 128), F32), sd((128, hidden), F32), sd((hidden, 128), F32),
+        sd((3, 128, width), F32), sd((width, 128), F32), sd((128, hidden), F32), sd((hidden, 128), F32),
     ]
     vm = pltpu.VMEM
     dma = pltpu.SemaphoreType.DMA
 
     def shapes(lead):
         return [
-            vm((lead, 128, 3 * width), BF16), vm((lead, width, 128), BF16),
+            vm((lead, 3, 128, width), BF16), vm((lead, width, 128), BF16),
             vm((lead, 128, hidden), BF16), vm((lead, hidden, 128), BF16),
         ]
 
@@ -919,7 +1135,7 @@
         return vm(array.shape, array.dtype)
 
     scratch = [
-        like(cot), like(q), like(qt), like(k), like(kt), like(v), like(mixf), like(lse),
+        vm((rows, full), BF16), like(q), like(qt), like(k), like(kt), like(v), like(mixf), like(lse),
         vm((2, chunk, width), F32),
         like(unit), like(inv), like(normed), like(act), like(slope),
         like(win), like(wo), like(we), like(wr), like(vec), like(stat),
@@ -931,8 +1147,9 @@
         vm((n, 8, chunk), F32), vm((n, 3, 8, chunk), F32),
         vm((8, full), F32), vm((8, hidden), F32), vm((16, width), F32), vm((7, 16, width), F32),
         *shapes(4), *shapes(4), *shapes(4), *shapes(3),
-        vm((128, 3 * width), F32), vm((width, 128), F32), vm((128, hidden), F32), vm((hidden, 128), F32),
-        dma((21,)), dma((3, n, 2)), dma((n,)), dma((4, 4)), dma((4, 4)), dma((4, 3)), dma((4, 3)),
+        vm((3, 128, width), F32), vm((width, 128), F32), vm((128, hidden), F32), vm((hidden, 128), F32),
+        dma((21,)), dma((3, n, 2)), dma((n,)), dma((n, 2)), dma((n, 2)), dma((n, 2)), dma((n, 2)), dma((n, 2)), dma((n,)), dma((n,)),
+        dma((4, 4)), dma((4, 4)), dma((4, 3)), dma((4, 3)),
         dma((n,)), dma((n,)), dma((n,)), dma((n,)), dma((n, 2)), dma((n, 2)),
         dma((n,)), dma((n,)), dma((n,)), dma((n,)), dma((n,)), dma((n,)), dma((n,)), dma((n,)),
         dma((n, 3)), dma((n, 3)), dma((7,)), dma((7,)),
@@ -947,6 +1164,47 @@
             collective_id=1, has_side_effects=True, vmem_limit_bytes=63 << 20
         ),
     )(*arrays)
+
+
+def finish_kernel(out_i, tg_i, sums_i, gin_i, gout_i, gexp_i, gred_i, *refs):
+    outs, vector_o, buffers = refs[:6], refs[6:14], refs[14:20]
+    load_sem, store_sem = refs[20:]
+    ins = (out_i, tg_i, gin_i, gout_i, gexp_i, gred_i)
+    loads = [pltpu.make_async_copy(a, b, load_sem.at[n]) for n, (a, b) in enumerate(zip(ins, buffers))]
+    stores = [pltpu.make_async_copy(a, b, store_sem.at[n]) for n, (a, b) in enumerate(zip(buffers, outs))]
+    order = (0, 2, 3, 4, 5, 1)
+    for n in order:
+        loads[n].start()
+    first_gain, first_shift, attn, b_out, g_two, s_two, b_red, b_exp = vector_o
+    first_gain[...] = sums_i[0:1, :]
+    first_shift[...] = sums_i[1:2, :]
+    attn[...] = sums_i[2:4, :]
+    b_out[...] = sums_i[4:5, :]
+    g_two[...] = sums_i[5:6, :]
+    s_two[...] = sums_i[6:7, :]
+    b_red[...] = sums_i[7:8, :]
+    for n in range(4):
+        width = sums_i.shape[1]
+        b_exp[:, n * width : (n + 1) * width] = sums_i[8 + n : 9 + n, :]
+    for n in order:
+        loads[n].wait()
+        stores[n].start()
+    for n in order:
+        stores[n].wait()
+
+
+def finish_call(out, tg, sums, gin, gout, gexp, gred):
+    width = sums.shape[1]
+    big = [jax.ShapeDtypeStruct(a.shape, a.dtype) for a in (out, tg, gin, gout, gexp, gred)]
+    small = [jax.ShapeDtypeStruct((n, m), F32) for n, m in ((1, width),) * 2 + ((2, width),) + ((1, width),) * 4 + ((1, 4 * width),)]
+    hbm, vm = pl.BlockSpec(memory_space=pl.ANY), pl.BlockSpec(memory_space=pltpu.VMEM)
+    return pl.pallas_call(
+        finish_kernel,
+        out_shape=big + small,
+        in_specs=[hbm, hbm, vm, hbm, hbm, hbm, hbm],
+        out_specs=[hbm] * 6 + [vm] * 8,
+        scratch_shapes=[pltpu.VMEM(a.shape, a.dtype) for a in big] + [pltpu.SemaphoreType.DMA((6,))] * 2,
+    )(out, tg, sums, gin, gout, gexp, gred)
 
 
 CONTRACT_ROWS = (((0,), (0,)), ((), ()))
@@ -1343,17 +1601,18 @@
     reduce_bias,
     cotangent,
 ):
-    empty = jnp.zeros_like(first_gain)
-    vectors = jnp.stack(
-        [first_gain, first_shift, output_bias, second_gain, second_shift, reduce_bias, empty, empty]
-    )
     kept = forward_call(
         tokens,
         cotangent,
-        vectors,
+        first_gain[None],
+        first_shift[None],
+        output_bias[None],
+        second_gain[None],
+        second_shift[None],
+        reduce_bias[None],
         attention_bias,
         expand_bias[None],
-        inward_weight.reshape(inward_weight.shape[0], -1),
+        inward_weight.transpose(1, 0, 2),
         output_weight,
         expand_weight,
         reduce_weight,
@@ -1364,25 +1623,27 @@
         return array.reshape(-1, array.shape[-1])
 
     outs = backward_call(
-        flat(tok), flat(cot), flat(q), qt, flat(k), kt, flat(v), flat(mixf), lse, flat(hid), flat(unit), flat(inv),
-        flat(normed), flat(act), flat(slope), win, wo, we, wr, vec, flat(one), flat(stat),
-    )
-    layer_output, tokens_grad, sums, inward_grad, output_grad, expand_grad, reduce_grad = outs
+        flat(tok), flat(cot), cotangent, flat(q), qt, flat(k), kt, flat(v), flat(mixf), lse, flat(hid), flat(unit),
+        flat(inv), flat(normed), flat(act), flat(slope), win, wo, we, wr, vec, flat(one), flat(stat),
+    )
+    outs = finish_call(*outs)
+    layer_output, tokens_grad, inward_grad, output_grad, expand_grad, reduce_grad = outs[:6]
+    first_gain_grad, first_shift_grad, attention_grad, out_grad, gain_grad, shift_grad, red_grad, exp_grad = outs[6:]
     return (
         layer_output,
         tokens_grad,
-        sums[0],
-        sums[1],
-        inward_grad.reshape(inward_weight.shape),
-        sums[2:4],
+        first_gain_grad[0],
+        first_shift_grad[0],
+        inward_grad.transpose(1, 0, 2),
+        attention_grad,
         output_grad,
-        sums[4],
-        sums[5],
-        sums[6],
+        out_grad[0],
+        gain_grad[0],
+        shift_grad[0],
         expand_grad,
-        sums[8:12].reshape(-1),
+        exp_grad[0],
         reduce_grad,
-        sums[7],
+        red_grad[0],
     )
 
 

time: 302 us -> 232 us (0.77)
  Pallas kernels: 286 us -> 231 us
  local copies, waits for them, and re-layouts: 15.2 us -> 0 us
    pallas_call x1, Pallas kernels: 133 us -> 102 us  [forward_call(): pl.pallas_call(forward_kernel, out_shape=outs, in_specs=[pl.BlockSpec(mem...]
    pallas_call x1, Pallas kernels: 153 us -> 124 us  [backward_call(): pl.pallas_call(backward_kernel, out_shape=outs, in_specs=[pl.BlockSpec(me...]
    unnamed x17 -> x0, local copies, waits for them, and re-layouts: 8.84 us -> none
    pallas_call x0 -> x1, Pallas kernels: none -> 4.85 us  [finish_call(): pl.pallas_call(finish_kernel, out_shape=big + small, in_specs=[hbm, hbm,...]
where the time goes in v2:
time: 232 us
  Pallas kernels  231 us (100%)
    pallas_call x1, Pallas kernels, backward_call(): pl.pallas_call(backward_kernel, out_shape=outs, in_specs=[pl.BlockSpec(me...  124 us
    pallas_call x1, Pallas kernels, forward_call(): pl.pallas_call(forward_kernel, out_shape=outs, in_specs=[pl.BlockSpec(mem...  102 us
    pallas_call x1, Pallas kernels, finish_call(): pl.pallas_call(finish_kernel, out_shape=big + small, in_specs=[hbm, hbm,...  4.85 us

profile of v2, /device:TPU:0, one launch (start us, length us, event | category | flops | bytes accessed | tf_op | source)
XLA Modules:
  0.0 232.1 jit_solution(2548201221489805175)
XLA Ops:
  0.7 102.1 %shard_map.245 = (bf16[7,224,1024]{2,1,0:T(8,128)(2,1)}, bf16[3,224,1024]{2,1,0:T(8,128)(2,1)}, bf16[7,224,256]{2,1,0:T(8,128)(2,1)}, bf16[7,256,224]{2,1,0:T(8,...) custom-call(bf16[784,512]{1,0:T(8,128)(2,1)} %tok.1, ...), custom_call_target="tpu_custom_call" | custom-call | tf_op jit(solution)/shard_map/pallas_call | solution.py:557
  102.7 124.4 %shard_map.246 = (bf16[784,512]{1,0:T(8,128)(2,1)}, f32[784,512]{1,0:T(8,128)}, f32[16,256]{1,0:T(8,128)}, f32[3,128,256]{2,1,0:T(8,128)}, f32[256,128]{1,0:T(8,...) custom-call(bf16[1568,1024]{1,0:T(8,128)(2,1)} %bitcast.30, bf16[672,1024]{1,0:T(8,128)(2,1)} %bitcast.38, ...), custom_call_target="tpu_custom_call" | custom-call | tf_op jit(solution)/shard_map/pallas_call | solution.py:1157
  227.1 4.8 %shard_map.247 = (bf16[784,512]{1,0:T(8,128)(2,1)}, f32[784,512]{1,0:T(8,128)}, f32[3,128,256]{2,1,0:T(8,128)}, f32[256,128]{1,0:T(8,128)}, f32[128,1024]{1,0:T(...) custom-call(bf16[784,512]{1,0:T(8,128)(2,1)} %get-tuple-element.79.o, ...), custom_call_target="tpu_custom_call" | custom-call | tf_op jit(solution)/shard_map/pallas_call | solution.py:1201

commit v3 on v2

--- a/solution.py
+++ b/solution.py
@@ -10,7 +10,7 @@
 SEQ = 1568
 EPSILON = 1e-06
 CHUNKS = 7
-EARLY = 3
+WINDOW = 2
 F32 = jnp.float32
 BF16 = jnp.bfloat16
 MESH = pl.DeviceIdType.MESH
@@ -53,10 +53,10 @@
     tok_o, cot_o, q_o, qt_o, k_o, kt_o, v_o, mixf_o, lse_o, hid_o, unit_o, inv_o,
     norm_o, act_o, slope_o, win_o, wo_o, we_o, wr_o, vec_o, one_o, stat_o,
     tok_all, cot_all, norm_one, q, qt, k, kt, v, vt, mixed, mixf, lse, hid, unit, inv, norm_two, act, slope,
-    win, wo, we, wr, vecs, stat, scores, sb, rb, xr,
+    win, wo, we, wr, vecs, stat, scores,
     local_sem, shard_sem, tok_sem, cot_sem, wz_send, wz_recv, wy_send, wy_recv, vec_send, vec_recv,
     tx_send, tx_recv, tc_send, tc_recv, tp_send, tp_recv, cx_send, cx_recv, cc_send, cc_recv, cp_send, cp_recv,
-    h1_send, h1_recv, h2_send, h2_recv, h3_send, h3_recv,
+    wx_send, wx_recv, wc_send, wc_recv, mx_send, mx_recv, mc_send, mc_recv,
 ):
     r, c = lax.axis_index("row"), lax.axis_index("col")
     z, y = r // 2, r % 2
@@ -86,7 +86,12 @@
     shards = (win_s, wo_s, we_s, wr_s)
     fulls = (win, wo, we, wr)
     shard_loads = [
-        pltpu.make_async_copy(shards[w], weight_blocks(fulls[w], WEIGHT_KINDS[w], r), shard_sem.at[w])
+        pltpu.make_async_copy(
+            shards[w],
+            wo.at[aligned(core * 2 + xx, width), aligned(r, 128)] if w == 1
+            else weight_blocks(fulls[w], WEIGHT_KINDS[w], r),
+            shard_sem.at[w],
+        )
         for w in range(4)
     ]
     for copy in shard_loads:
@@ -103,20 +108,38 @@
     for i in range(CHUNKS):
         for s in range(2):
             half_load(tok, tok_all, tok_sem, i, s).start()
-            if i < EARLY:
-                half_load(cot, cot_all, cot_sem, i, s).start()
+            half_load(cot, cot_all, cot_sem, i, s).start()
     for n, vector in enumerate((g_one, s_one, b_out, g_two, s_two, b_red, b_red, b_red)):
         vecs[n : n + 1, own] = vector[...]
     pl.semaphore_wait(barrier, 4 + jnp.where(z >= 1, 1, 0) + jnp.where(z <= 2, 1, 0))
 
+    slab = core * 2 + xx
+
+    def out_piece(x, row):
+        return wo.at[aligned(core * 2 + x, width), aligned(row, 128)]
+
+    def out_x():
+        return remote(wo_s, out_piece(xx, r), wx_send.at[0], wx_recv.at[0], r, c_x)
+
+    def out_y(row):
+        block = wo.at[aligned(core, 2 * width), aligned(row, 128)]
+        return remote(block, block, wy_send.at[1, 0], wy_recv.at[1, 0], r_y, c)
+
+    def out_core(side):
+        block = wo.at[aligned(side, 2 * width), :]
+        return remote(block, block, wc_send.at[0], wc_recv.at[0], r, c_core)
+
     def weight_ref(w, zb, side):
+        if w == 1:
+            return wo.at[aligned(core, 2 * width), aligned(zb, 256)]
         return weight_blocks(fulls[w], WEIGHT_KINDS[w], zb * 2 + side)
 
     def line_copy(w, up, hop):
         zb = z - hop if up else z + hop
         block = weight_ref(w, zb, y)
         target = (z + 1 if up else z - 1) * 2 + y
-        return remote(shards[w] if hop == 0 else block, block, wz_send.at[w, up, hop], wz_recv.at[w, up, hop], target, c)
+        source = shards[w] if hop == 0 and w != 1 else block
+        return remote(source, block, wz_send.at[w, up, hop], wz_recv.at[w, up, hop], target, c)
 
     def line_sends(up, hop):
         return (z >= hop) & (z <= 2) if up else (z <= 3 - hop) & (z >= 1)
@@ -144,7 +167,8 @@
                 zb = z - 1 - hop if up else z + 1 + hop
                 block = weight_ref(w, zb, y)
                 remote(block, block, wz_send.at[w, up, hop], wz_recv.at[w, up, hop], r_y, c).wait_recv()
-                y_copy(w, zb, y).start()
+                if w != 1:
+                    y_copy(w, zb, y).start()
 
             if hop < 2:
                 @pl.when(line_receives(up, hop) & line_sends(up, hop + 1))
@@ -157,9 +181,10 @@
                 @pl.when(line_sends(up, hop))
                 def _():
                     line_copy(w, up, hop).wait_send()
-        for zb in range(4):
-            y_copy(w, zb, y).wait_send()
-            y_copy(w, zb, 1 - y).wait_recv()
+        if w != 1:
+            for zb in range(4):
+                y_copy(w, zb, y).wait_send()
+                y_copy(w, zb, 1 - y).wait_recv()
 
     def vec_copy(slot, target, col):
         block = vecs.at[:, aligned(col, width)]
@@ -207,8 +232,9 @@
 
     start_weight(0)
     own_to_y(0).start()
-    send_tok(0)
-    send_tok(1)
+    for i in range(WINDOW):
+        send_tok(i)
+    out_x().start()
     for slot, target in enumerate((c_x, c_core, c_far)):
         vec_copy(slot, target, c).start()
 
@@ -231,7 +257,7 @@
         return [keep(base + n, i, a.at[i], b.at[i]) for n, (a, b) in enumerate(pairs)]
 
     def keep_hid(i):
-        return keep(16, i, hid.at[i, :, own], hid_o.at[i])
+        return keep(16, i, hid.at[i % 2, :, own], hid_o.at[i])
 
     lane_ids = lax.broadcasted_iota(jnp.int32, (chunk // 7, 128), 1)
 
@@ -253,13 +279,9 @@
             for s in range(2):
                 tok_x(i, s, c_x).wait_recv()
 
-            @pl.when(i + 2 < CHUNKS)
+            @pl.when(i + WINDOW < CHUNKS)
             def _():
-                send_tok(i + 2)
-
-            @pl.when(i == CHUNKS - 2)
-            def _():
-                send_cot(0)
+                send_tok(i + WINDOW)
 
             tok_pass(i, c_x).start()
 
@@ -274,24 +296,27 @@
             def _():
                 forward_weight(0, hop)
 
-        @pl.when(g == 2)
-        def _():
+        @pl.when(g == 0)
+        def _():
+            shard_loads[1].wait()
+            out_x().wait()
+            out_y(r).start()
+            start_weight(2)
+
+        @pl.when(g == 3)
+        def _():
+            out_y(r).wait_send()
+            out_y(r_y).wait_recv()
             start_weight(1)
-            start_weight(2)
 
         @pl.loop(2 * g, jnp.minimum(2 * g + 2, CHUNKS))
         def _(i):
             first_norm(i)
 
-    send_cot(1)
-    send_cot(2)
-    forward_weight(1, 0)
-    for w in range(4):
+    send_cot(0)
+    for w in (0, 2, 3):
         shard_loads[w].wait()
     finish_weight(0)
-    own_to_y(1).start()
-    own_to_y(2).start()
-    forward_weight(1, 1)
 
     @pl.loop(0, CHUNKS)
     def _(i):
@@ -311,13 +336,17 @@
 
         @pl.when(i == 2)
         def _():
-            forward_weight(1, 2)
-
-        @pl.when(i == 4)
-        def _():
+            own_to_y(2).start()
             forward_weight(2, 0)
 
-    finish_weight(1)
+        @pl.when(i == 5)
+        def _():
+            send_cot(1)
+
+        @pl.when(i == 6)
+        def _():
+            own_to_y(3).start()
+
 
     def attend(i):
         row_ids = lax.broadcasted_iota(jnp.int32, (128, chunk), 0)
@@ -348,26 +377,33 @@
                 lse[i, pl.ds(pair * 2 + h, 1), :] = peaks[h] + jnp.log2(total)
             out = jnp.concatenate(outs, axis=0).T
             mixf[i, :, lanes] = out
-            mixed[i, :, lanes] = out.astype(BF16)
-
-    def h1(i):
-        slot = i % 2
-        return remote(sb.at[slot, 1 - core], rb.at[i], h1_send.at[i], h1_recv.at[i], r, c_core)
-
-    def h2(i):
-        return remote(rb.at[i], xr.at[i], h2_send.at[i], h2_recv.at[i], r, c_x)
-
-    def h3(i, x, side):
-        block = hid.at[i, :, aligned(x * 2 + side, width)]
-        return remote(block, block, h3_send.at[i, x], h3_recv.at[i, x], r, c_core)
+            mixed[i, :, aligned(slab * 2 + pair, 128)] = out.astype(BF16)
+
+    def mixed_block(i, order):
+        return mixed.at[i, :, aligned(order, width)]
+
+    def mixed_x(i, order):
+        block = mixed_block(i, order)
+        return remote(block, block, mx_send.at[i], mx_recv.at[i], r, c_x)
+
+    def mixed_core(i, slot, order):
+        block = mixed_block(i, order)
+        return remote(block, block, mc_send.at[i, slot], mc_recv.at[i, slot], r, c_core)
 
     def expand(t):
-        for x in range(2):
-            h3(t, x, core).wait_send()
-            h3(t, x, 1 - core).wait_recv()
+        mixed_core(t, 0, (1 - core) * 2 + xx).wait_recv()
+        mixed_core(t, 1, (1 - core) * 2 + 1 - xx).wait_recv()
+
+        @pl.when(t >= 2)
+        def _():
+            keep_hid(t - 2).wait()
+
+        hid[t % 2] = tok_all[t].astype(F32) + (
+            jnp.dot(mixed[t], wo[...], preferred_element_type=F32) + vecs[2:3, :]
+        )
         for part in range(7):
             rows = pl.ds(part * (chunk // 7), chunk // 7)
-            units, _, inverse = row_norm(hid[t, rows, :])
+            units, _, inverse = row_norm(hid[t % 2, rows, :])
             unit[t, rows, :] = units.astype(BF16)
             inv[t, rows, :] = jnp.broadcast_to(inverse, (chunk // 7, 128))
             norm_two[t, rows, :] = (units * vecs[3:4, :] + vecs[4:5, :]).astype(BF16)
@@ -382,83 +418,87 @@
             copy.start()
         keep_hid(t).start()
 
-    def spread_hidden(t):
-        h2(t).wait()
-        for x in range(2):
-            lanes = aligned(x * 2 + core, width)
-            total = rb[t, x].astype(F32) + xr[t, x].astype(F32)
-            hid[t, :, lanes] = tok_all[t, :, lanes].astype(F32) + total + vecs[2:3, lanes]
-        for x in range(2):
-            h3(t, x, core).start()
+    def pass_mixed(t):
+        mixed_x(t, core * 2 + 1 - xx).wait_recv()
+        mixed_core(t, 1, core * 2 + 1 - xx).start()
+
+    def pass_on_cot(t):
+        for s in range(2):
+            cot_x(t, s, c_x).wait_recv()
+            half_load(cot, cot_all, cot_sem, t, s).wait()
+        cot_pass(t, c_x).start()
 
     @pl.loop(0, CHUNKS)
     def _(i):
         attend(i)
+        mixed_x(i, slab).start()
+        mixed_core(i, 0, slab).start()
         for copy in kept(i, 1):
             copy.start()
-        partial = jnp.dot(mixed[i], wo[...], preferred_element_type=F32)
-        for x in range(2):
-            for side in range(2):
-                block = x * 2 + side
-                sb[i % 2, side, x] = partial[:, block * width : (block + 1) * width].astype(BF16)
-        h1(i).start()
 
         @pl.when(i == 0)
         def _():
+            forward_weight(1, 0)
+
+        @pl.when(i == 1)
+        def _():
             forward_weight(2, 1)
 
-        @pl.when(i == 1)
+        @pl.when(i == 3)
+        def _():
+            start_weight(3)
+            forward_weight(1, 1)
+
+        @pl.when(i == 5)
         def _():
             forward_weight(2, 2)
-            start_weight(3)
-
-        @pl.when(i == 2)
-        def _():
-            own_to_y(3).start()
+
+        @pl.when(i == 6)
+        def _():
             forward_weight(3, 0)
 
-        @pl.when(i == 3)
-        def _():
+        @pl.when(i >= 1)
+        def _():
+            pass_mixed(i - 1)
+
+    pass_mixed(CHUNKS - 1)
+    forward_weight(1, 2)
+    finish_weight(1)
+    out_core(core).start()
+    send_cot(2)
+    pass_on_cot(0)
+    pass_on_cot(1)
+    out_core(core).wait_send()
+    out_core(1 - core).wait_recv()
+    finish_weight(2)
+
+    @pl.loop(0, CHUNKS)
+    def _(t):
+        expand(t)
+
+        @pl.when(t == 0)
+        def _():
+            send_cot(3)
             forward_weight(3, 1)
 
-        @pl.when(i == 4)
+        @pl.when(t == 1)
+        def _():
+            for n in range(4, CHUNKS):
+                send_cot(n)
+
+        @pl.when(t == 3)
         def _():
             forward_weight(3, 2)
 
-        @pl.when((i >= 1) & (i <= EARLY))
-        def _():
-            for s in range(2):
-                cot_x(i - 1, s, c_x).wait_recv()
-                half_load(cot, cot_all, cot_sem, i - 1, s).wait()
-            cot_pass(i - 1, c_x).start()
-
-        h1(i).wait()
-        for x in range(2):
-            rb[i, x] = (sb[i % 2, core, x].astype(F32) + rb[i, x].astype(F32)).astype(BF16)
-        h2(i).start()
-
-        @pl.when(i >= 1)
-        def _():
-            spread_hidden(i - 1)
-
-        @pl.when(i == 5)
-        def _():
-            finish_weight(2)
-
-        @pl.loop(jnp.maximum(2 * (i - 5), 0), jnp.maximum(2 * (i - 4), 0))
-        def _(t):
-            expand(t)
-
-    @pl.loop(4, CHUNKS)
-    def _(t):
-        @pl.when(t == CHUNKS - 1)
-        def _():
-            spread_hidden(CHUNKS - 1)
-
-        expand(t)
-
-    @pl.loop(0, EARLY)
+        @pl.when(t >= 2)
+        def _():
+            pass_on_cot(t)
+
+    @pl.loop(0, CHUNKS)
     def _(i):
+        mixed_x(i, slab).wait_send()
+        mixed_core(i, 0, slab).wait_send()
+        mixed_core(i, 1, core * 2 + 1 - xx).wait_send()
         for s in range(2):
             cot_x(i, s, c).wait_send()
             cot_core(i, s, c).wait_send()
@@ -478,22 +518,19 @@
     finish_weight(3)
     last = [
         keep(17, n, a, b)
-        for n, (a, b) in enumerate(((win, win_o), (wo, wo_o), (we, we_o), (wr, wr_o), (vecs, vec_o)))
+        for n, (a, b) in enumerate(((win, win_o), (wo.at[aligned(slab, width), :], wo_o), (we, we_o), (wr, wr_o), (vecs, vec_o)))
     ]
     for copy in last:
         copy.start()
 
     @pl.loop(0, CHUNKS)
     def _(i):
-        for stage in range(3):
+        for stage in range(4):
             for copy in kept(i, stage):
                 copy.wait()
-        keep_hid(i).wait()
-
-        @pl.when(i < EARLY)
-        def _():
-            for copy in kept(i, 3):
-                copy.wait()
+
+    for t in (CHUNKS - 2, CHUNKS - 1):
+        keep_hid(t).wait()
 
     for copy in last:
         copy.wait()
@@ -512,7 +549,7 @@
 
     outs = [
         sd((n, chunk, full), BF16),
-        sd((EARLY, chunk, full), BF16),
+        sd((n, chunk, full), BF16),
         sd((n, chunk, width), BF16),
         sd((n, width, chunk), BF16),
         sd((n, chunk, width), BF16),
@@ -537,22 +574,20 @@
     vm = pltpu.VMEM
     dma = pltpu.SemaphoreType.DMA
     scratch = [
-        vm((n, chunk, full), BF16), vm((EARLY, chunk, full), BF16), vm((n, chunk, full), BF16),
+        vm((n, chunk, full), BF16), vm((n, chunk, full), BF16), vm((n, chunk, full), BF16),
         vm((n, chunk, width), BF16), vm((n, width, chunk), BF16),
         vm((n, chunk, width), BF16), vm((n, width, chunk), BF16),
         vm((n, chunk, width), BF16), vm((n, width, chunk), BF16),
-        vm((n, chunk, width), BF16), vm((n, chunk, width), F32), vm((n, 8, chunk), F32),
-        vm((n, chunk, full), F32), vm((n, chunk, full), BF16), vm((n, chunk, 128), F32),
+        vm((n, chunk, full), BF16), vm((n, chunk, width), F32), vm((n, 8, chunk), F32),
+        vm((2, chunk, full), F32), vm((n, chunk, full), BF16), vm((n, chunk, 128), F32),
         vm((n, chunk, full), BF16), vm((n, chunk, hidden), BF16), vm((n, chunk, hidden), BF16),
-        vm((3, full, width), BF16), vm((width, full), BF16), vm((full, hidden), BF16), vm((hidden, full), BF16),
+        vm((3, full, width), BF16), vm((full, full), BF16), vm((full, hidden), BF16), vm((hidden, full), BF16),
         vm((8, full), F32), vm((n, chunk, 128), F32),
         vm((2, n, chunk, chunk), F32),
-        vm((2, 2, 2, chunk, width), BF16), vm((n, 2, chunk, width), BF16),
-        vm((n, 2, chunk, width), BF16),
-        dma((18, n)), dma((4,)), dma((n, 2)), dma((EARLY, 2)), dma((4, 2, 3)), dma((4, 2, 3)), dma((4, 4)), dma((4, 4)), dma((3,)), dma((3,)),
+        dma((18, n)), dma((4,)), dma((n, 2)), dma((n, 2)), dma((4, 2, 3)), dma((4, 2, 3)), dma((4, 4)), dma((4, 4)), dma((3,)), dma((3,)),
         dma((n, 2)), dma((n, 2)), dma((n, 2)), dma((n, 2)), dma((n,)), dma((n,)),
-        dma((EARLY, 2)), dma((EARLY, 2)), dma((EARLY, 2)), dma((EARLY, 2)), dma((EARLY,)), dma((EARLY,)),
-        dma((n,)), dma((n,)), dma((n,)), dma((n,)), dma((n, 2)), dma((n, 2)),
+        dma((n, 2)), dma((n, 2)), dma((n, 2)), dma((n, 2)), dma((n,)), dma((n,)),
+        dma((1,)), dma((1,)), dma((1,)), dma((1,)), dma((n,)), dma((n,)), dma((n, 2)), dma((n, 2)),
     ]
     return pl.pallas_call(
         forward_kernel,
@@ -570,16 +605,16 @@
 
 
 def backward_kernel(
-    tok_h, cot_h, cot_in, q_h, qt_h, k_h, kt_h, v_h, mixf_h, lse_h, hid_h, unit_h, inv_h,
+    tok_h, cot_h, q_h, qt_h, k_h, kt_h, v_h, mixf_h, lse_h, hid_h, unit_h, inv_h,
     normed_h, act_h, slope_h, win_h, wo_h, we_h, wr_h, vec_h, one_h, stat_h,
     out_o, tg_o, sums_o, gin_o, gout_o, gexp_o, gred_o,
-    cot, q, qt, k, kt, v, mixf, lse, hid, unit, inv, normed, act, slope, win, wo, we, wr, vecs, stat,
-    grad, dq, dk, dv, tg, out, sb_g, sb_o, rb_g, xr_g, rb_o, xr_o, xr_1, st, st_in,
-    col_sums, hid_sums, packet, packets,
+    cot, q, qt, k, kt, v, mixf, lse, hid, unit, inv, normed, act, slope, win, wo, we, wr, vecs,
+    grad, flat, dk, dv, tg, out, sb_g, sb_o, rb_g, xr_g, rb_o, xr_o, xr_1, st, st_in,
+    col_sums, packet, packets,
     ys_in, ys_out, ys_exp, ys_red, oh_in, oh_out, oh_exp, oh_red,
     yr_in, yr_out, yr_exp, yr_red, zr_in, zr_out, zr_exp, zr_red,
     gin, gout, gexp, gred,
-    load_sem, store_sem, hid_sem, cot_sem, cx_send, cx_recv, cc_send, cc_recv, cp_send, cp_recv, gy_send, gy_recv, gz_send, gz_recv,
+    load_sem, store_sem, hid_sem, gy_send, gy_recv, gz_send, gz_recv,
     h1g_send, h1g_recv, h2g_send, h2g_recv, h3g_send, h3g_recv,
     h1o_send, h1o_recv, h2o_send, h2o_recv, h1t_send, h1t_recv, h2t_send, h2t_recv,
     st_send, st_recv, pk_send, pk_recv,
@@ -589,7 +624,7 @@
     xx, core = c // 2, c % 2
     c_x, c_core, c_far = (c + 2) % 4, c + 1 - 2 * core, (c + 2) % 4 + 1 - 2 * core
     r_y = r + 1 - 2 * y
-    tok, one = act, normed
+    tok, one, stat = act, normed, inv
     chunk = q.shape[0] // CHUNKS
     half = chunk // 2
     width = q.shape[1]
@@ -606,70 +641,29 @@
 
     loads = {}
     order = (
-        ("wr", wr_h, wr), ("cot", cot_h, cot.at[pl.ds(0, EARLY * chunk), :]), ("slope", slope_h, slope), ("we", we_h, we), ("act", act_h, act),
+        ("wr", wr_h, wr), ("cot", cot_h, cot), ("slope", slope_h, slope), ("we", we_h, we), ("act", act_h, act),
         ("vec", vec_h, vecs), ("unit", unit_h, unit), ("inv", inv_h, inv), ("wo", wo_h, wo),
         ("normed", normed_h, normed), ("mixf", mixf_h, mixf), ("lse", lse_h, lse), ("qt", qt_h, qt), ("q", q_h, q),
-        ("k", k_h, k), ("v", v_h, v), ("kt", kt_h, kt), ("win", win_h, win), ("stat", stat_h, stat),
+        ("k", k_h, k), ("v", v_h, v), ("kt", kt_h, kt), ("stat", stat_h, stat),
         ("tok", tok_h, tok), ("one", one_h, one),
     )
     for n, (name, src, dst) in enumerate(order):
         loads[name] = pltpu.make_async_copy(src, dst, load_sem.at[n])
-    late = ("tok", "one")
-    for name, _, _ in order:
+    for n in range(3):
+        loads["win" + str(n)] = pltpu.make_async_copy(
+            win_h.at[n], win.at[:, pl.ds(n * width, width)], load_sem.at[len(order) + n]
+        )
+    late = ("tok", "one", "stat", "win0", "win1", "win2")
+    for name in loads:
         if name not in late:
             loads[name].start()
-    def cot_source(i, s):
-        return cot_in.at[pl.ds(pl.multiple_of(i * half, half), half), pl.ds(s * width, width)]
-
-    def cot_block(i, s, col):
-        return cot.at[pl.ds(pl.multiple_of(i * chunk + s * half, half), half), aligned(col, width)]
-
-    def cot_load(i, s):
-        return pltpu.make_async_copy(cot_source(i, s), cot_block(i, s, c), cot_sem.at[i, s])
-
-    for i in range(EARLY, CHUNKS):
-        for s in range(2):
-            cot_load(i, s).start()
     dk[...] = jnp.zeros_like(dk)
     dv[...] = jnp.zeros_like(dv)
     col_sums[...] = jnp.zeros_like(col_sums)
-    hid_sums[...] = jnp.zeros_like(hid_sums)
     pl.semaphore_wait(barrier, 10)
 
     def rows_of(i):
         return pl.ds(pl.multiple_of(i * chunk, chunk), chunk)
-
-    def cot_x(i, s, col):
-        return remote(cot_source(i, s), cot_block(i, s, col), cx_send.at[i, s], cx_recv.at[i, s], r, c_x)
-
-    def cot_core(i, s, col):
-        return remote(cot_source(i, s), cot_block(i, s, col), cc_send.at[i, s], cc_recv.at[i, s], r, c_core)
-
-    def cot_pass(i, col):
-        block = cot.at[rows_of(i), aligned(col, width)]
-        return remote(block, block, cp_send.at[i], cp_recv.at[i], r, c_core)
-
-    def send_cot(i):
-        for s in range(2):
-            cot_x(i, s, c).start()
-            cot_core(i, s, c).start()
-
-    def pass_cot(i):
-        for s in range(2):
-            cot_x(i, s, c_x).wait_recv()
-        cot_pass(i, c_x).start()
-
-    def finish_cot(i):
-        for s in range(2):
-            cot_load(i, s).wait()
-            cot_x(i, s, c).wait_send()
-            cot_core(i, s, c).wait_send()
-            cot_core(i, s, c_core).wait_recv()
-        cot_pass(i, c_x).wait_send()
-        cot_pass(i, c_far).wait_recv()
-
-    send_cot(EARLY)
-    send_cot(EARLY + 1)
 
     def h1(sb, rb, send, recv, i):
         return remote(sb.at[i % 2, 1 - core], rb.at[i], send.at[i], recv.at[i], r, c_core)
@@ -709,16 +703,20 @@
     def spread_grad(i):
         h2g(i).wait()
         if isinstance(i, int):
-            h2g(i + 2).start()
+            h2g(i + 4).start()
         else:
-            @pl.when(i + 2 < CHUNKS)
+            @pl.when(i + 4 < CHUNKS)
             def _():
-                h2g(i + 2).start()
+                h2g(i + 4).start()
 
         for x in range(2):
             grad[i % 4, :, aligned(x * 2 + core, width)] = rb_g[i, x].astype(F32) + xr_g[i, x].astype(F32)
         for x in range(2):
             h3g(i, x, core).start()
+
+    def column_sums(values):
+        ones = jnp.ones((8, values.shape[0]), BF16)
+        return jnp.dot(ones, values, preferred_element_type=F32)[0:1, :]
 
     ys = (ys_in, ys_out, ys_exp, ys_red)
     oh = (oh_in, oh_out, oh_exp, oh_red)
@@ -765,70 +763,67 @@
             total = total + zr[w][s].astype(F32)
         dst[...] = total
 
-    loads["wr"].wait()
-    loads["cot"].wait()
-    loads["slope"].wait()
-    loads["we"].wait()
-    loads["act"].wait()
-
-    @pl.loop(0, CHUNKS)
+    for name in ("wr", "cot", "slope", "we", "act"):
+        loads[name].wait()
+
+    @pl.loop(0, CHUNKS + 1)
     def _(i):
-        @pl.when(i >= EARLY)
-        def _():
-            finish_cot(i)
-
-        rows = rows_of(i)
-        for n in range(slope.shape[1] // 256):
-            lanes = slice(n * 256, (n + 1) * 256)
-            grad_act = lax.dot_general(cot[rows, :], wr[lanes, :], NT_DIMS, preferred_element_type=F32)
-            low = (slope[rows, lanes].astype(F32) * grad_act).astype(BF16)
-            slope[rows, lanes] = low
-            hid_sums[0:1, lanes] += jnp.sum(low.astype(F32), axis=0, keepdims=True)
-        fill(sb_g, i, lax.dot_general(slope[rows, :], we[...], NT_DIMS, preferred_element_type=F32))
-        h1g(i).start()
+        @pl.when(i < CHUNKS)
+        def _():
+            rows = rows_of(i)
+            for n in range(slope.shape[1] // 256):
+                lanes = slice(n * 256, (n + 1) * 256)
+                grad_act = lax.dot_general(cot[rows, :], wr[lanes, :], NT_DIMS, preferred_element_type=F32)
+                low = (slope[rows, lanes].astype(F32) * grad_act).astype(BF16)
+                slope[rows, lanes] = low
+            fill(sb_g, i, lax.dot_general(slope[rows, :], we[...], NT_DIMS, preferred_element_type=F32))
+            h1g(i).start()
 
         @pl.when(i >= 1)
         def _():
             h1o(i - 1).wait()
             merge(sb_o, rb_o, i - 1)
-
-        fill(sb_o, i, jnp.dot(act[rows, :], wr[...], preferred_element_type=F32))
-        h1o(i).start()
-        h1g(i).wait()
-        merge(sb_g, rb_g, i)
-
-        @pl.when((i >= 1) & (i + 2 < CHUNKS))
-        def _():
-            pass_cot(i + 2)
-
-            @pl.when(i + 4 < CHUNKS)
+            h1g(i - 1).wait()
+            merge(sb_g, rb_g, i - 1)
+
+        for at, n in ((1, 0), (2, 1), (4, 2), (6, 3)):
+            @pl.when(i == at)
             def _():
-                send_cot(i + 4)
-
-        @pl.when((i == 3) | (i == 4))
-        def _():
-            h2g(i - 3).start()
-
-        col_sums[0:1, :] += jnp.sum(cot[rows, :].astype(F32), axis=0, keepdims=True)
-
-    h1o(CHUNKS - 1).wait()
-    merge(sb_o, rb_o, CHUNKS - 1)
+                h2g(n).start()
+
+        @pl.when(i == 3)
+        def _():
+            grad_block(3, 0, act[...], cot)
+            gy(3, 0).start()
+
+        @pl.when(i == 5)
+        def _():
+            grad_block(3, 1, act[...], cot)
+            gy(3, 1).start()
+
+        @pl.when(i < CHUNKS)
+        def _():
+            fill(sb_o, i, jnp.dot(act[rows_of(i), :], wr[...], preferred_element_type=F32))
+            h1o(i).start()
+
+    for n in range(4):
+        packet[8 + n : 9 + n, :] = column_sums(slope[:, n * width : (n + 1) * width])
     loads["normed"].wait()
-    for s in range(3):
-        grad_block(3, s, act[...], cot)
-        if s < 2:
-            gy(3, s).start()
     spread_grad(0)
-    for s in range(3):
+    pass_on(3, 0)
+    grad_block(3, 2, act[...], cot)
+    gy(3, 2).start()
+    grad_block(3, 3, act[...], cot)
+    spread_grad(1)
+    grad_block(2, 0, normed, slope[...])
+    pass_on(3, 1)
+    gy(2, 0).start()
+    for s in range(1, 4):
         grad_block(2, s, normed, slope[...])
-    pass_on(3, 0)
-    gy(3, 2).start()
-    spread_grad(1)
-    grad_block(3, 3, act[...], cot)
-    grad_block(2, 3, normed, slope[...])
     for name in late:
-        loads[name].start()
-    for name in ("unit", "inv", "vec", "wo", "mixf", "lse", "qt", "q", "k", "v", "kt", "win", "stat"):
+        if name != "stat":
+            loads[name].start()
+    for name in ("unit", "inv", "vec", "wo", "mixf", "lse", "qt", "q", "k", "v", "kt"):
         loads[name].wait()
 
     def hid_load(i):
@@ -893,9 +888,15 @@
             for h in range(heads):
                 rows_h = slice(h * HEAD_DIM, (h + 1) * HEAD_DIM)
                 parts[h] = parts[h] + jnp.dot(kt[j, rows_h, :], grad_scores[h], preferred_element_type=F32)
-        dq[rows, :] = (jnp.concatenate(parts, axis=0).T * HEAD_DIM ** (-0.5)).astype(BF16)
+        flat[rows, 0:width] = (jnp.concatenate(parts, axis=0).T * HEAD_DIM ** (-0.5)).astype(BF16)
 
     def finish_out(i):
+        @pl.when(i >= 2)
+        def _():
+            for s in range(2):
+                out_store(i - 2, s).wait()
+
+        hid_load(i).start()
         h2o(i).wait()
         hid_load(i).wait()
         total = rb_o[i, xx].astype(F32) + xr_o[i].astype(F32)
@@ -905,9 +906,7 @@
         for s in range(2):
             out_store(i, s).start()
 
-    @pl.loop(0, CHUNKS)
-    def _(i):
-        hid_load(i).start()
+    def second_norm_back(i):
         for x in range(2):
             h3g(i, x, core).wait_send()
             h3g(i, x, 1 - core).wait_recv()
@@ -921,70 +920,104 @@
             plain = jnp.mean(scaled, axis=1, keepdims=True)
             cross = jnp.mean(scaled * units, axis=1, keepdims=True)
             total = cot[rows, :].astype(F32) + inv[rows, 0:1] * (scaled - plain - units * cross)
-            low = total.astype(BF16)
-            col_sums[1:2, :] += jnp.sum(incoming * units, axis=0, keepdims=True)
-            col_sums[2:3, :] += jnp.sum(incoming, axis=0, keepdims=True)
-            col_sums[3:4, :] += jnp.sum(low.astype(F32), axis=0, keepdims=True)
-            unit[rows, :] = low
+            mine = grad[i % 4, span, own]
+            col_sums[1:2, 0:width] += jnp.sum(mine * unit[rows, own].astype(F32), axis=0, keepdims=True)
+            col_sums[2:3, 0:width] += jnp.sum(mine, axis=0, keepdims=True)
+            unit[rows, :] = total.astype(BF16)
             grad[i % 4, span, :] = total
         for s in range(2):
             tg[i, s] = grad[i % 4, s * half : (s + 1) * half, own]
-        h2o(i).start()
-        attend_back(i)
-
-        @pl.when(i + 2 < CHUNKS)
+
+    @pl.loop(-1, CHUNKS)
+    def _(i):
+        @pl.when(i + 1 < CHUNKS)
+        def _():
+            second_norm_back(i + 1)
+
+        @pl.when((i >= 0) & (i + 2 < CHUNKS))
         def _():
             spread_grad(i + 2)
 
-        queue = ((3, 0), (3, 1), (3, 2), (2, 0), (2, 1), (2, 2), (3, 3), (2, 3))
-        for at in range(5):
-            @pl.when(i == at)
-            def _():
-                pass_on(*queue[at + 1])
-                gy(*queue[at + 3]).start()
-
-        @pl.when(i >= 1)
-        def _():
-            @pl.when(i >= 3)
-            def _():
-                for s in range(2):
-                    out_store(i - 3, s).wait()
-            finish_out(i - 1)
-
-    for s in range(2):
-        out_store(CHUNKS - 3, s).wait()
-    finish_out(CHUNKS - 1)
+        @pl.when(i == CHUNKS - 2)
+        def _():
+            for s in range(4):
+                grad_block(1, s, mixf[...].astype(BF16), unit)
+                gy(1, s).start()
+
+        @pl.when(i == CHUNKS - 1)
+        def _():
+            loads["stat"].start()
+
+        @pl.when(i >= 0)
+        def _():
+            attend_back(i)
+
+        @pl.when(i == -1)
+        def _():
+            pass_on(3, 2)
+            gy(2, 1).start()
+
+        @pl.when(i == 0)
+        def _():
+            pass_on(2, 0)
+            gy(2, 2).start()
+
+        @pl.when(i == 1)
+        def _():
+            pass_on(2, 1)
+            gy(3, 3).start()
+
+        @pl.when(i == 2)
+        def _():
+            pass_on(2, 2)
+            gy(2, 3).start()
+
+        @pl.when(i == CHUNKS - 2)
+        def _():
+            finish_grad(3, gred)
+
+        @pl.when(i == CHUNKS - 1)
+        def _():
+            for s in range(3):
+                pass_on(1, s)
+
+        @pl.when(i >= 3)
+        def _():
+            @pl.loop(2 * (i - 3), jnp.minimum(2 * (i - 3) + 2, CHUNKS))
+            def _(n):
+                h2o(n).start()
+
+        @pl.when(i >= 5)
+        def _():
+            @pl.loop(2 * (i - 5), 2 * (i - 5) + 2)
+            def _(n):
+                finish_out(n)
 
     for i in range(CHUNKS):
         rows = pl.ds(i * chunk, chunk)
-        k[rows, :] = (dk[rows, :] * HEAD_DIM ** (-0.5)).astype(BF16)
-        low = dv[rows, :].astype(BF16)
-        v[rows, :] = low
-        col_sums[4:5, 0:width] += jnp.sum(dq[rows, :].astype(F32), axis=0, keepdims=True)
-        col_sums[5:6, 0:width] += jnp.sum(low.astype(F32), axis=0, keepdims=True)
+        flat[rows, width : 2 * width] = (dk[rows, :] * HEAD_DIM ** (-0.5)).astype(BF16)
+        flat[rows, 2 * width : 3 * width] = dv[rows, :].astype(BF16)
     for name in late:
         loads[name].wait()
 
     def inward_block(s):
         zt = (z + 1 + s) % 4
         left = one[:, aligned(zt, 256)]
-        for n, right in enumerate((dq, k, v)):
-            block = lax.dot_general(left, right[...], TN_DIMS, preferred_element_type=F32).astype(BF16)
+        block = lax.dot_general(left, flat[...], TN_DIMS, preferred_element_type=F32).astype(BF16)
+        for n in range(3):
+            lanes = slice(n * width, (n + 1) * width)
 
             @pl.when(y == 0)
             def _():
-                oh_in[s, n] = block[0:128, :]
-                ys_in[s, n] = block[128:256, :]
+                oh_in[s, n] = block[0:128, lanes]
+                ys_in[s, n] = block[128:256, lanes]
 
             @pl.when(y == 1)
             def _():
-                oh_in[s, n] = block[128:256, :]
-                ys_in[s, n] = block[0:128, :]
+                oh_in[s, n] = block[128:256, lanes]
+                ys_in[s, n] = block[0:128, lanes]
 
         gy(0, s).start()
-
-    for s in range(3):
-        inward_block(s)
 
     def stat_copy(i, slot, target):
         return remote(st.at[i], st_in.at[i, slot], st_send.at[i, slot], st_recv.at[i, slot], r, target)
@@ -992,18 +1025,17 @@
     lane_ids = lax.broadcasted_iota(jnp.int32, (chunk, 128), 1)
     gain = vecs[0:1, :]
 
-    @pl.loop(0, CHUNKS + 2)
+    @pl.loop(0, CHUNKS + 3)
     def _(i):
+        for s in range(4):
+            @pl.when(i == s)
+            def _():
+                inward_block(s)
+
         @pl.when(i < CHUNKS)
         def _():
             rows = rows_of(i)
-            partial = lax.dot_general(dq[rows, :], win[0], NT_DIMS, preferred_element_type=F32)
-            partial = partial + lax.dot_general(
-                k[rows, :], win[1], NT_DIMS, preferred_element_type=F32
-            )
-            partial = partial + lax.dot_general(
-                v[rows, :], win[2], NT_DIMS, preferred_element_type=F32
-            )
+            partial = lax.dot_general(flat[rows, :], win[...], NT_DIMS, preferred_element_type=F32)
             fill(sb_g, i, partial)
             h1t(i).start()
             units = (tok[rows, :].astype(F32) - stat[rows, 0:1]) * stat[rows, 64:65]
@@ -1014,35 +1046,40 @@
             st[i] = both.T[0:8, :]
             for slot, target in enumerate((c_x, c_core, c_far)):
                 stat_copy(i, slot, target).start()
-            h1t(i).wait()
-            merge(sb_g, rb_g, i)
-            h2t(i).start()
+
+        @pl.when((i >= 4) & (i <= 6))
+        def _():
+            finish_out(i)
+
+        @pl.when((i >= 1) & (i <= CHUNKS))
+        def _():
+            h1t(i - 1).wait()
+            merge(sb_g, rb_g, i - 1)
+            h2t(i - 1).start()
 
         for s in range(3):
-            @pl.when(i == s + 1)
+            @pl.when(i == s + 2)
             def _():
                 pass_on(0, s)
 
-        @pl.when(i == 4)
-        def _():
-            for s in range(3):
-                grad_block(1, s, mixf[...].astype(BF16), unit)
-                gy(1, s).start()
-
         @pl.when(i == 5)
         def _():
-            inward_block(3)
-            grad_block(1, 3, mixf[...].astype(BF16), unit)
-            gy(1, 3).start()
+            packet[7:8, :] = column_sums(cot[:, own])
+            packet[4:5, :] = column_sums(unit[:, own])
 
         @pl.when(i == 6)
         def _():
-            for s in range(3):
-                pass_on(1, s)
-
-        @pl.when(i >= 2)
-        def _():
-            t = i - 2
+            packet[2:3, :] = column_sums(flat[:, 0:width])
+            packet[3:4, :] = column_sums(flat[:, 2 * width : 3 * width])
+            finish_grad(2, gexp)
+
+        @pl.when(i == 7)
+        def _():
+            finish_grad(1, gout)
+
+        @pl.when(i >= 3)
+        def _():
+            t = i - 3
             rows = rows_of(t)
             h2t(t).wait()
             total = st[t]
@@ -1065,22 +1102,14 @@
 
     packet[0:1, :] = col_sums[6:7, 0:width]
     packet[1:2, :] = col_sums[7:8, 0:width]
-    packet[2:4, :] = col_sums[4:6, 0:width]
-    packet[4:5, :] = col_sums[3:4, own]
-    packet[5:7, :] = col_sums[1:3, own]
-    packet[7:8, :] = col_sums[0:1, own]
-    for n in range(4):
-        packet[8 + n : 9 + n, :] = hid_sums[0:1, n * width : (n + 1) * width]
+    packet[5:7, :] = col_sums[1:3, 0:width]
 
     def packet_copy(step):
         return remote(packet, packets.at[step], pk_send.at[step], pk_recv.at[step], others[step], c)
 
     for step in range(7):
         packet_copy(step).start()
-    finish_grad(3, gred)
-    finish_grad(2, gexp)
     finish_grad(0, gin)
-    finish_grad(1, gout)
     stores = [
         pltpu.make_async_copy(src, dst, store_sem.at[2, n, 0])
         for n, (src, dst) in enumerate(((gin, gin_o), (gout, gout_o), (gexp, gexp_o), (gred, gred_o)))
@@ -1108,7 +1137,7 @@
 
 
 def backward_call(*arrays):
-    (tok, cot, cot_in, q, qt, k, kt, v, mixf, lse, hid, unit, inv, normed, act, slope, win, wo, we, wr, vec, one, stat) = arrays
+    (tok, cot, q, qt, k, kt, v, mixf, lse, hid, unit, inv, normed, act, slope, win, wo, we, wr, vec, one, stat) = arrays
     rows, width = q.shape
     full, hidden = we.shape
     n, chunk = CHUNKS, rows // CHUNKS
@@ -1138,18 +1167,17 @@
         vm((rows, full), BF16), like(q), like(qt), like(k), like(kt), like(v), like(mixf), like(lse),
         vm((2, chunk, width), F32),
         like(unit), like(inv), like(normed), like(act), like(slope),
-        like(win), like(wo), like(we), like(wr), like(vec), like(stat),
-        vm((4, chunk, full), F32), vm((rows, width), BF16), vm((rows, width), F32), vm((rows, width), F32),
+        vm((full, 3 * width), BF16), like(wo), like(we), like(wr), like(vec),
+        vm((4, chunk, full), F32), vm((rows, 3 * width), BF16), vm((rows, width), F32), vm((rows, width), F32),
         vm((n, 2, half, width), F32), vm((2, 2, half, width), BF16),
         vm((2, 2, 2, chunk, width), BF16), vm((2, 2, 2, chunk, width), BF16),
         vm((n, 2, chunk, width), BF16), vm((n, 2, chunk, width), BF16),
         vm((n, 2, chunk, width), BF16), vm((n, chunk, width), BF16), vm((n, chunk, width), BF16),
         vm((n, 8, chunk), F32), vm((n, 3, 8, chunk), F32),
-        vm((8, full), F32), vm((8, hidden), F32), vm((16, width), F32), vm((7, 16, width), F32),
+        vm((8, full), F32), vm((16, width), F32), vm((7, 16, width), F32),
         *shapes(4), *shapes(4), *shapes(4), *shapes(3),
         vm((3, 128, width), F32), vm((width, 128), F32), vm((128, hidden), F32), vm((hidden, 128), F32),
-        dma((21,)), dma((3, n, 2)), dma((n,)), dma((n, 2)), dma((n, 2)), dma((n, 2)), dma((n, 2)), dma((n, 2)), dma((n,)), dma((n,)),
-        dma((4, 4)), dma((4, 4)), dma((4, 3)), dma((4, 3)),
+        dma((23,)), dma((3, n, 2)), dma((n,)), dma((4, 4)), dma((4, 4)), dma((4, 3)), dma((4, 3)),
         dma((n,)), dma((n,)), dma((n,)), dma((n,)), dma((n, 2)), dma((n, 2)),
         dma((n,)), dma((n,)), dma((n,)), dma((n,)), dma((n,)), dma((n,)), dma((n,)), dma((n,)),
         dma((n, 3)), dma((n, 3)), dma((7,)), dma((7,)),
@@ -1623,7 +1651,7 @@
         return array.reshape(-1, array.shape[-1])
 
     outs = backward_call(
-        flat(tok), flat(cot), cotangent, flat(q), qt, flat(k), kt, flat(v), flat(mixf), lse, flat(hid), flat(unit),
+        flat(tok), flat(cot), flat(q), qt, flat(k), kt, flat(v), flat(mixf), lse, flat(hid), flat(unit),
         flat(inv), flat(normed), flat(act), flat(slope), win, wo, we, wr, vec, flat(one), flat(stat),
     )
     outs = finish_call(*outs)

time: 232 us -> 216 us (0.931)
  Pallas kernels: 231 us -> 215 us
    pallas_call x1, Pallas kernels: 102 us -> 93.5 us  [forward_call(): pl.pallas_call(forward_kernel, out_shape=outs, in_specs=[pl.BlockSpec(mem...]
    pallas_call x1, Pallas kernels: 124 us -> 117 us  [backward_call(): pl.pallas_call(backward_kernel, out_shape=outs, in_specs=[pl.BlockSpec(me...]
where the time goes in v3:
time: 216 us
  Pallas kernels  215 us (100%)
    pallas_call x1, Pallas kernels, backward_call(): pl.pallas_call(backward_kernel, out_shape=outs, in_specs=[pl.BlockSpec(me...  117 us
    pallas_call x1, Pallas kernels, forward_call(): pl.pallas_call(forward_kernel, out_shape=outs, in_specs=[pl.BlockSpec(mem...  93.5 us
    pallas_call x1, Pallas kernels, finish_call(): pl.pallas_call(finish_kernel, out_shape=big + small, in_specs=[hbm, hbm,...  4.85 us

profile of v3, /device:TPU:0, one launch (start us, length us, event | category | flops | bytes accessed | tf_op | source)
XLA Modules:
  0.0 216.0 jit_solution(2803952449993708186)
XLA Ops:
  0.7 93.5 %shard_map.245 = (bf16[7,224,1024]{2,1,0:T(8,128)(2,1)}, bf16[7,224,1024]{2,1,0:T(8,128)(2,1)}, bf16[7,224,256]{2,1,0:T(8,128)(2,1)}, bf16[7,256,224]{2,1,0:T(8,...) custom-call(bf16[784,512]{1,0:T(8,128)(2,1)} %tok.1, ...), custom_call_target="tpu_custom_call" | custom-call | tf_op jit(solution)/shard_map/pallas_call | solution.py:592
  94.1 116.8 %shard_map.246 = (bf16[784,512]{1,0:T(8,128)(2,1)}, f32[784,512]{1,0:T(8,128)}, f32[16,256]{1,0:T(8,128)}, f32[3,128,256]{2,1,0:T(8,128)}, f32[256,128]{1,0:T(8,...) custom-call(bf16[1568,1024]{1,0:T(8,128)(2,1)} %bitcast.30, bf16[1568,1024]{1,0:T(8,128)(2,1)} %bitcast.31, ...), custom_call_target="tpu_custom_call" | custom-call | tf_op jit(solution)/shard_map/pallas_call | solution.py:1185
  211.0 4.8 %shard_map.247 = (bf16[784,512]{1,0:T(8,128)(2,1)}, f32[784,512]{1,0:T(8,128)}, f32[3,128,256]{2,1,0:T(8,128)}, f32[256,128]{1,0:T(8,128)}, f32[128,1024]{1,0:T(...) custom-call(bf16[784,512]{1,0:T(8,128)(2,1)} %get-tuple-element.79.o, ...), custom_call_target="tpu_custom_call" | custom-call | tf_op jit(solution)/shard_map/pallas_call | solution.py:1229

commit v4 on v3

--- a/solution.py
+++ b/solution.py
@@ -115,15 +115,9 @@
 
     slab = core * 2 + xx
 
-    def out_piece(x, row):
-        return wo.at[aligned(core * 2 + x, width), aligned(row, 128)]
-
-    def out_x():
-        return remote(wo_s, out_piece(xx, r), wx_send.at[0], wx_recv.at[0], r, c_x)
-
-    def out_y(row):
-        block = wo.at[aligned(core, 2 * width), aligned(row, 128)]
-        return remote(block, block, wy_send.at[1, 0], wy_recv.at[1, 0], r_y, c)
+    def out_x(order):
+        block = wo.at[aligned(order, width), :]
+        return remote(block, block, wx_send.at[0], wx_recv.at[0], r, c_x)
 
     def out_core(side):
         block = wo.at[aligned(side, 2 * width), :]
@@ -131,14 +125,14 @@
 
     def weight_ref(w, zb, side):
         if w == 1:
-            return wo.at[aligned(core, 2 * width), aligned(zb, 256)]
+            return wo.at[aligned(slab, width), aligned(zb * 2 + side, 128)]
         return weight_blocks(fulls[w], WEIGHT_KINDS[w], zb * 2 + side)
 
     def line_copy(w, up, hop):
         zb = z - hop if up else z + hop
         block = weight_ref(w, zb, y)
         target = (z + 1 if up else z - 1) * 2 + y
-        source = shards[w] if hop == 0 and w != 1 else block
+        source = shards[w] if hop == 0 else block
         return remote(source, block, wz_send.at[w, up, hop], wz_recv.at[w, up, hop], target, c)
 
     def line_sends(up, hop):
@@ -167,8 +161,7 @@
                 zb = z - 1 - hop if up else z + 1 + hop
                 block = weight_ref(w, zb, y)
                 remote(block, block, wz_send.at[w, up, hop], wz_recv.at[w, up, hop], r_y, c).wait_recv()
-                if w != 1:
-                    y_copy(w, zb, y).start()
+                y_copy(w, zb, y).start()
 
             if hop < 2:
                 @pl.when(line_receives(up, hop) & line_sends(up, hop + 1))
@@ -181,10 +174,9 @@
                 @pl.when(line_sends(up, hop))
                 def _():
                     line_copy(w, up, hop).wait_send()
-        if w != 1:
-            for zb in range(4):
-                y_copy(w, zb, y).wait_send()
-                y_copy(w, zb, 1 - y).wait_recv()
+        for zb in range(4):
+            y_copy(w, zb, y).wait_send()
+            y_copy(w, zb, 1 - y).wait_recv()
 
     def vec_copy(slot, target, col):
         block = vecs.at[:, aligned(col, width)]
@@ -234,7 +226,6 @@
     own_to_y(0).start()
     for i in range(WINDOW):
         send_tok(i)
-    out_x().start()
     for slot, target in enumerate((c_x, c_core, c_far)):
         vec_copy(slot, target, c).start()
 
@@ -249,12 +240,22 @@
             pairs = ((mixf, mixf_o), (lse, lse_o))
             base = 8
         elif stage == 2:
-            pairs = ((unit, unit_o), (inv, inv_o), (norm_two, norm_o), (act, act_o), (slope, slope_o))
+            pairs = ((unit, unit_o), (inv, inv_o), (norm_two, norm_o))
             base = 10
+        elif stage == 4:
+            pairs = ((act, act_o), (slope, slope_o))
+            base = 13
         else:
             pairs = ((cot_all, cot_o),)
             base = 15
         return [keep(base + n, i, a.at[i], b.at[i]) for n, (a, b) in enumerate(pairs)]
+
+    last = [
+        keep(17, n, a, b)
+        for n, (a, b) in enumerate(
+            ((win, win_o), (wo.at[aligned(slab, width), :], wo_o), (we, we_o), (wr, wr_o), (vecs, vec_o))
+        )
+    ]
 
     def keep_hid(i):
         return keep(16, i, hid.at[i % 2, :, own], hid_o.at[i])
@@ -298,25 +299,31 @@
 
         @pl.when(g == 0)
         def _():
-            shard_loads[1].wait()
-            out_x().wait()
-            out_y(r).start()
+            start_weight(1)
+            own_to_y(1).start()
+
+        @pl.when(g == 1)
+        def _():
+            forward_weight(1, 0)
+
+        @pl.when(g == 3)
+        def _():
             start_weight(2)
-
-        @pl.when(g == 3)
-        def _():
-            out_y(r).wait_send()
-            out_y(r_y).wait_recv()
-            start_weight(1)
+            forward_weight(1, 1)
+            send_cot(0)
+            send_cot(1)
 
         @pl.loop(2 * g, jnp.minimum(2 * g + 2, CHUNKS))
         def _(i):
             first_norm(i)
 
-    send_cot(0)
-    for w in (0, 2, 3):
+    for w in range(4):
         shard_loads[w].wait()
+    own_to_y(3).start()
+    forward_weight(1, 2)
     finish_weight(0)
+    last[0].start()
+    last[4].start()
 
     @pl.loop(0, CHUNKS)
     def _(i):
@@ -334,50 +341,55 @@
         for copy in kept(i, 0):
             copy.start()
 
-        @pl.when(i == 2)
+        @pl.when(i == 0)
         def _():
             own_to_y(2).start()
+            finish_weight(1)
+            out_x(slab).start()
+
+        @pl.when(i == 4)
+        def _():
             forward_weight(2, 0)
 
-        @pl.when(i == 5)
-        def _():
-            send_cot(1)
-
         @pl.when(i == 6)
         def _():
-            own_to_y(3).start()
-
+            forward_weight(2, 1)
 
     def attend(i):
         row_ids = lax.broadcasted_iota(jnp.int32, (128, chunk), 0)
-
-        @pl.loop(0, width // 128)
-        def _(pair):
-            lanes = aligned(pair, 128)
-            peaks = []
-            for h in range(2):
-                query = qt[i, lanes, :]
-                query = jnp.where(row_ids // HEAD_DIM == h, query, jnp.zeros_like(query))
-                peak = jnp.full((1, chunk), -jnp.inf, F32)
-                for j in range(CHUNKS):
-                    block = jnp.dot(k[j, :, lanes], query, preferred_element_type=F32)
-                    scores[h, j] = block
-                    peak = jnp.maximum(peak, jnp.max(block, axis=0, keepdims=True))
-                peaks.append(peak * scale)
-            outs = []
-            for h in range(2):
-                total = jnp.zeros((1, chunk), F32)
-                acc = jnp.zeros((HEAD_DIM, chunk), F32)
-                rows = pl.ds(pl.multiple_of(pair * 128 + h * HEAD_DIM, HEAD_DIM), HEAD_DIM)
-                for j in range(CHUNKS):
-                    weights = jnp.exp2(scores[h, j] * scale - peaks[h])
-                    total = total + jnp.sum(weights, axis=0, keepdims=True)
-                    acc = acc + jnp.dot(vt[j, rows, :], weights.astype(BF16), preferred_element_type=F32)
-                outs.append(acc / total)
-                lse[i, pl.ds(pair * 2 + h, 1), :] = peaks[h] + jnp.log2(total)
-            out = jnp.concatenate(outs, axis=0).T
-            mixf[i, :, lanes] = out
-            mixed[i, :, aligned(slab * 2 + pair, 128)] = out.astype(BF16)
+        heads = width // HEAD_DIM
+
+        def score(h):
+            lanes = slice(h // 2 * 128, h // 2 * 128 + 128)
+            query = qt[i, lanes, :]
+            query = jnp.where(row_ids // HEAD_DIM == h % 2, query, jnp.zeros_like(query))
+            peak = jnp.full((1, chunk), -jnp.inf, F32)
+            for j in range(CHUNKS):
+                block = jnp.dot(k[j, :, lanes], query, preferred_element_type=F32)
+                scores[h % 2, j] = block
+                peak = jnp.maximum(peak, jnp.max(block, axis=0, keepdims=True))
+            return peak * scale
+
+        def mix(h, peak):
+            total = jnp.zeros((1, chunk), F32)
+            acc = jnp.zeros((HEAD_DIM, chunk), F32)
+            for j in range(CHUNKS):
+                weights = jnp.exp2(scores[h % 2, j] * scale - peak)
+                total = total + jnp.sum(weights, axis=0, keepdims=True)
+                rows = slice(h * HEAD_DIM, (h + 1) * HEAD_DIM)
+                acc = acc + jnp.dot(vt[j, rows, :], weights.astype(BF16), preferred_element_type=F32)
+            lse[i, h : h + 1, :] = peak + jnp.log2(total)
+            return acc / total
+
+        outs = []
+        peak = score(0)
+        for h in range(heads):
+            following = score(h + 1) if h + 1 < heads else None
+            outs.append(mix(h, peak))
+            peak = following
+        out = jnp.concatenate(outs, axis=0).T
+        mixf[i] = out
+        mixed[i, :, aligned(slab, width)] = out.astype(BF16)
 
     def mixed_block(i, order):
         return mixed.at[i, :, aligned(order, width)]
@@ -390,7 +402,7 @@
         block = mixed_block(i, order)
         return remote(block, block, mc_send.at[i, slot], mc_recv.at[i, slot], r, c_core)
 
-    def expand(t):
+    def second_norm(t):
         mixed_core(t, 0, (1 - core) * 2 + xx).wait_recv()
         mixed_core(t, 1, (1 - core) * 2 + 1 - xx).wait_recv()
 
@@ -407,6 +419,11 @@
             unit[t, rows, :] = units.astype(BF16)
             inv[t, rows, :] = jnp.broadcast_to(inverse, (chunk // 7, 128))
             norm_two[t, rows, :] = (units * vecs[3:4, :] + vecs[4:5, :]).astype(BF16)
+        for copy in kept(t, 2):
+            copy.start()
+        keep_hid(t).start()
+
+    def expand(t):
         for n in range(we.shape[1] // 256):
             lanes = slice(n * 256, (n + 1) * 256)
             expanded = jnp.dot(norm_two[t], we[:, lanes], preferred_element_type=F32) + exp_bias[:, lanes]
@@ -414,9 +431,8 @@
             act[t, :, lanes] = (expanded * gate).astype(BF16)
             bell = jnp.exp2(expanded * expanded * (-0.5 * LOG2E)) * 0.3989422804014327
             slope[t, :, lanes] = (gate + expanded * bell).astype(BF16)
-        for copy in kept(t, 2):
+        for copy in kept(t, 4):
             copy.start()
-        keep_hid(t).start()
 
     def pass_mixed(t):
         mixed_x(t, core * 2 + 1 - xx).wait_recv()
@@ -438,39 +454,45 @@
 
         @pl.when(i == 0)
         def _():
-            forward_weight(1, 0)
-
-        @pl.when(i == 1)
-        def _():
-            forward_weight(2, 1)
+            start_weight(3)
+
+        @pl.when(i == 2)
+        def _():
+            forward_weight(2, 2)
 
         @pl.when(i == 3)
         def _():
-            start_weight(3)
-            forward_weight(1, 1)
+            out_x(slab).wait_send()
+            out_x(core * 2 + 1 - xx).wait_recv()
+            out_core(core).start()
+
+        @pl.when(i == 4)
+        def _():
+            forward_weight(3, 0)
+            send_cot(2)
+            pass_mixed(0)
+            pass_mixed(1)
+            out_core(core).wait_send()
+            out_core(1 - core).wait_recv()
+
+        @pl.when(i == 6)
+        def _():
+            forward_weight(3, 1)
+            send_cot(3)
+
+        @pl.when(i >= 5)
+        def _():
+            @pl.loop(2 * (i - 5), i - 3)
+            def _(t):
+                second_norm(t)
 
         @pl.when(i == 5)
         def _():
-            forward_weight(2, 2)
-
-        @pl.when(i == 6)
-        def _():
-            forward_weight(3, 0)
-
-        @pl.when(i >= 1)
-        def _():
-            pass_mixed(i - 1)
-
-    pass_mixed(CHUNKS - 1)
-    forward_weight(1, 2)
-    finish_weight(1)
-    out_core(core).start()
-    send_cot(2)
-    pass_on_cot(0)
-    pass_on_cot(1)
-    out_core(core).wait_send()
-    out_core(1 - core).wait_recv()
+            pass_mixed(2)
+
     finish_weight(2)
+    last[1].start()
+    last[2].start()
 
     @pl.loop(0, CHUNKS)
     def _(t):
@@ -478,21 +500,31 @@
 
         @pl.when(t == 0)
         def _():
-            send_cot(3)
-            forward_weight(3, 1)
+            send_cot(4)
 
         @pl.when(t == 1)
         def _():
-            for n in range(4, CHUNKS):
-                send_cot(n)
+            send_cot(5)
+            send_cot(6)
 
         @pl.when(t == 3)
         def _():
             forward_weight(3, 2)
 
-        @pl.when(t >= 2)
-        def _():
-            pass_on_cot(t)
+        @pl.when((t >= 2) & (t <= 5))
+        def _():
+            second_norm(t + 1)
+
+        @pl.when((t >= 1) & (t <= 4))
+        def _():
+            pass_mixed(t + 2)
+
+        @pl.when(t >= 3)
+        def _():
+            pass_on_cot(t - 3)
+
+    for n in range(4, CHUNKS):
+        pass_on_cot(n)
 
     @pl.loop(0, CHUNKS)
     def _(i):
@@ -516,16 +548,11 @@
         tok_pass(i, c_x).wait_send()
 
     finish_weight(3)
-    last = [
-        keep(17, n, a, b)
-        for n, (a, b) in enumerate(((win, win_o), (wo.at[aligned(slab, width), :], wo_o), (we, we_o), (wr, wr_o), (vecs, vec_o)))
-    ]
-    for copy in last:
-        copy.start()
+    last[3].start()
 
     @pl.loop(0, CHUNKS)
     def _(i):
-        for stage in range(4):
+        for stage in range(5):
             for copy in kept(i, stage):
                 copy.wait()
 
@@ -614,7 +641,7 @@
     ys_in, ys_out, ys_exp, ys_red, oh_in, oh_out, oh_exp, oh_red,
     yr_in, yr_out, yr_exp, yr_red, zr_in, zr_out, zr_exp, zr_red,
     gin, gout, gexp, gred,
-    load_sem, store_sem, hid_sem, gy_send, gy_recv, gz_send, gz_recv,
+    load_sem, chunk_sem, store_sem, hid_sem, gy_send, gy_recv, gz_send, gz_recv,
     h1g_send, h1g_recv, h2g_send, h2g_recv, h3g_send, h3g_recv,
     h1o_send, h1o_recv, h2o_send, h2o_recv, h1t_send, h1t_recv, h2t_send, h2t_recv,
     st_send, st_recv, pk_send, pk_recv,
@@ -639,9 +666,12 @@
     for row in others:
         pl.semaphore_signal(barrier, inc=1, device_id=(row, c), device_id_type=MESH)
 
+    def rows_of(i):
+        return pl.ds(pl.multiple_of(i * chunk, chunk), chunk)
+
     loads = {}
     order = (
-        ("wr", wr_h, wr), ("cot", cot_h, cot), ("slope", slope_h, slope), ("we", we_h, we), ("act", act_h, act),
+        ("wr", wr_h, wr), ("we", we_h, we),
         ("vec", vec_h, vecs), ("unit", unit_h, unit), ("inv", inv_h, inv), ("wo", wo_h, wo),
         ("normed", normed_h, normed), ("mixf", mixf_h, mixf), ("lse", lse_h, lse), ("qt", qt_h, qt), ("q", q_h, q),
         ("k", k_h, k), ("v", v_h, v), ("kt", kt_h, kt), ("stat", stat_h, stat),
@@ -653,7 +683,19 @@
         loads["win" + str(n)] = pltpu.make_async_copy(
             win_h.at[n], win.at[:, pl.ds(n * width, width)], load_sem.at[len(order) + n]
         )
-    late = ("tok", "one", "stat", "win0", "win1", "win2")
+    def chunk_loads(i):
+        rows = rows_of(i)
+        return [
+            pltpu.make_async_copy(a.at[rows, :], b.at[rows, :], chunk_sem.at[n, i])
+            for n, (a, b) in enumerate(((cot_h, cot), (slope_h, slope), (act_h, act)))
+        ]
+
+    loads["wr"].start()
+    loads["we"].start()
+    for i in range(CHUNKS):
+        for copy in chunk_loads(i):
+            copy.start()
+    late = ("wr", "we", "tok", "one", "stat", "win0", "win1", "win2")
     for name in loads:
         if name not in late:
             loads[name].start()
@@ -661,9 +703,6 @@
     dv[...] = jnp.zeros_like(dv)
     col_sums[...] = jnp.zeros_like(col_sums)
     pl.semaphore_wait(barrier, 10)
-
-    def rows_of(i):
-        return pl.ds(pl.multiple_of(i * chunk, chunk), chunk)
 
     def h1(sb, rb, send, recv, i):
         return remote(sb.at[i % 2, 1 - core], rb.at[i], send.at[i], recv.at[i], r, c_core)
@@ -763,13 +802,24 @@
             total = total + zr[w][s].astype(F32)
         dst[...] = total
 
-    for name in ("wr", "cot", "slope", "we", "act"):
-        loads[name].wait()
+    loads["wr"].wait()
+    loads["we"].wait()
 
     @pl.loop(0, CHUNKS + 1)
     def _(i):
         @pl.when(i < CHUNKS)
         def _():
+            @pl.when(i < 3)
+            def _():
+                for copy in chunk_loads(i):
+                    copy.wait()
+
+            @pl.when(i == 3)
+            def _():
+                for n in range(3, CHUNKS):
+                    for copy in chunk_loads(n):
+                        copy.wait()
+
             rows = rows_of(i)
             for n in range(slope.shape[1] // 256):
                 lanes = slice(n * 256, (n + 1) * 256)
@@ -820,14 +870,14 @@
     gy(2, 0).start()
     for s in range(1, 4):
         grad_block(2, s, normed, slope[...])
-    for name in late:
+    for name in late[2:]:
         if name != "stat":
             loads[name].start()
     for name in ("unit", "inv", "vec", "wo", "mixf", "lse", "qt", "q", "k", "v", "kt"):
         loads[name].wait()
 
     def hid_load(i):
-        return pltpu.make_async_copy(hid_h.at[rows_of(i), :], hid.at[i % 2], hid_sem.at[i])
+        return pltpu.make_async_copy(hid_h.at[rows_of(i), :], hid, hid_sem.at[i])
 
     def out_store(i, s):
         return pltpu.make_async_copy(
@@ -900,7 +950,7 @@
         h2o(i).wait()
         hid_load(i).wait()
         total = rb_o[i, xx].astype(F32) + xr_o[i].astype(F32)
-        value = (hid[i % 2] + total + vecs[5:6, own]).astype(BF16)
+        value = (hid[...] + total + vecs[5:6, own]).astype(BF16)
         for s in range(2):
             out[i % 2, s] = value[s * half : (s + 1) * half, :]
         for s in range(2):
@@ -997,7 +1047,7 @@
         rows = pl.ds(i * chunk, chunk)
         flat[rows, width : 2 * width] = (dk[rows, :] * HEAD_DIM ** (-0.5)).astype(BF16)
         flat[rows, 2 * width : 3 * width] = dv[rows, :].astype(BF16)
-    for name in late:
+    for name in late[2:]:
         loads[name].wait()
 
     def inward_block(s):
@@ -1165,7 +1215,7 @@
 
     scratch = [
         vm((rows, full), BF16), like(q), like(qt), like(k), like(kt), like(v), like(mixf), like(lse),
-        vm((2, chunk, width), F32),
+        vm((chunk, width), F32),
         like(unit), like(inv), like(normed), like(act), like(slope),
         vm((full, 3 * width), BF16), like(wo), like(we), like(wr), like(vec),
         vm((4, chunk, full), F32), vm((rows, 3 * width), BF16), vm((rows, width), F32), vm((rows, width), F32),
@@ -1177,7 +1227,7 @@
         vm((8, full), F32), vm((16, width), F32), vm((7, 16, width), F32),
         *shapes(4), *shapes(4), *shapes(4), *shapes(3),
         vm((3, 128, width), F32), vm((width, 128), F32), vm((128, hidden), F32), vm((hidden, 128), F32),
-        dma((23,)), dma((3, n, 2)), dma((n,)), dma((4, 4)), dma((4, 4)), dma((4, 3)), dma((4, 3)),
+        dma((23,)), dma((3, n)), dma((3, n, 2)), dma((n,)), dma((4, 4)), dma((4, 4)), dma((4, 3)), dma((4, 3)),
         dma((n,)), dma((n,)), dma((n,)), dma((n,)), dma((n, 2)), dma((n, 2)),
         dma((n,)), dma((n,)), dma((n,)), dma((n,)), dma((n,)), dma((n,)), dma((n,)), dma((n,)),
         dma((n, 3)), dma((n, 3)), dma((7,)), dma((7,)),

time: 216 us -> 208 us (0.963)
  Pallas kernels: 215 us -> 207 us
    pallas_call x1, Pallas kernels: 93.5 us -> 86.5 us  [forward_call(): pl.pallas_call(forward_kernel, out_shape=outs, in_specs=[pl.BlockSpec(mem...]
where the time goes in v4:
time: 208 us
  Pallas kernels  207 us (100%)
    pallas_call x1, Pallas kernels, backward_call(): pl.pallas_call(backward_kernel, out_shape=outs, in_specs=[pl.BlockSpec(me...  116 us
    pallas_call x1, Pallas kernels, forward_call(): pl.pallas_call(forward_kernel, out_shape=outs, in_specs=[pl.BlockSpec(mem...  86.5 us
    pallas_call x1, Pallas kernels, finish_call(): pl.pallas_call(finish_kernel, out_shape=big + small, in_specs=[hbm, hbm,...  4.85 us

profile of v4, /device:TPU:0, one launch (start us, length us, event | category | flops | bytes accessed | tf_op | source)
XLA Modules:
  0.0 207.8 jit_solution(16713459997524402210)
XLA Ops:
  0.7 86.5 %shard_map.245 = (bf16[7,224,1024]{2,1,0:T(8,128)(2,1)}, bf16[7,224,1024]{2,1,0:T(8,128)(2,1)}, bf16[7,224,256]{2,1,0:T(8,128)(2,1)}, bf16[7,256,224]{2,1,0:T(8,...) custom-call(bf16[784,512]{1,0:T(8,128)(2,1)} %tok.1, ...), custom_call_target="tpu_custom_call" | custom-call | tf_op jit(solution)/shard_map/pallas_call | solution.py:619
  87.1 115.6 %shard_map.246 = (bf16[784,512]{1,0:T(8,128)(2,1)}, f32[784,512]{1,0:T(8,128)}, f32[16,256]{1,0:T(8,128)}, f32[3,128,256]{2,1,0:T(8,128)}, f32[256,128]{1,0:T(8,...) custom-call(bf16[1568,1024]{1,0:T(8,128)(2,1)} %bitcast.30, bf16[1568,1024]{1,0:T(8,128)(2,1)} %bitcast.31, ...), custom_call_target="tpu_custom_call" | custom-call | tf_op jit(solution)/shard_map/pallas_call | solution.py:1235
  202.8 4.8 %shard_map.247 = (bf16[784,512]{1,0:T(8,128)(2,1)}, f32[784,512]{1,0:T(8,128)}, f32[3,128,256]{2,1,0:T(8,128)}, f32[256,128]{1,0:T(8,128)}, f32[128,1024]{1,0:T(...) custom-call(bf16[784,512]{1,0:T(8,128)(2,1)} %get-tuple-element.79.o, ...), custom_call_target="tpu_custom_call" | custom-call | tf_op jit(solution)/shard_map/pallas_call | solution.py:1279

commit v5 on v4

--- a/solution.py
+++ b/solution.py
@@ -1077,11 +1077,6 @@
 
     @pl.loop(0, CHUNKS + 3)
     def _(i):
-        for s in range(4):
-            @pl.when(i == s)
-            def _():
-                inward_block(s)
-
         @pl.when(i < CHUNKS)
         def _():
             rows = rows_of(i)
@@ -1097,6 +1092,11 @@
             for slot, target in enumerate((c_x, c_core, c_far)):
                 stat_copy(i, slot, target).start()
 
+        for at, s in ((0, 1), (2, 0), (3, 2), (4, 3)):
+            @pl.when(i == at)
+            def _():
+                inward_block(s)
+
         @pl.when((i >= 4) & (i <= 6))
         def _():
             finish_out(i)
@@ -1107,8 +1107,8 @@
             merge(sb_g, rb_g, i - 1)
             h2t(i - 1).start()
 
-        for s in range(3):
-            @pl.when(i == s + 2)
+        for at, s in ((3, 1), (5, 0), (6, 2)):
+            @pl.when(i == at)
             def _():
                 pass_on(0, s)
 

time: 208 us -> 205 us (0.986)
  Pallas kernels: 207 us -> 204 us
    pallas_call x1, Pallas kernels: 116 us -> 112 us  [backward_call(): pl.pallas_call(backward_kernel, out_shape=outs, in_specs=[pl.BlockSpec(me...]
where the time goes in v5:
time: 205 us
  Pallas kernels  204 us (100%)
    pallas_call x1, Pallas kernels, backward_call(): pl.pallas_call(backward_kernel, out_shape=outs, in_specs=[pl.BlockSpec(me...  112 us
    pallas_call x1, Pallas kernels, forward_call(): pl.pallas_call(forward_kernel, out_shape=outs, in_specs=[pl.BlockSpec(mem...  86.5 us
    pallas_call x1, Pallas kernels, finish_call(): pl.pallas_call(finish_kernel, out_shape=big + small, in_specs=[hbm, hbm,...  4.85 us

profile of v5, /device:TPU:0, one launch (start us, length us, event | category | flops | bytes accessed | tf_op | source)
XLA Modules:
  0.0 204.6 jit_solution(12905070247241806534)
XLA Ops:
  0.7 86.5 %shard_map.245 = (bf16[7,224,1024]{2,1,0:T(8,128)(2,1)}, bf16[7,224,1024]{2,1,0:T(8,128)(2,1)}, bf16[7,224,256]{2,1,0:T(8,128)(2,1)}, bf16[7,256,224]{2,1,0:T(8,...) custom-call(bf16[784,512]{1,0:T(8,128)(2,1)} %tok.1, ...), custom_call_target="tpu_custom_call" | custom-call | tf_op jit(solution)/shard_map/pallas_call | solution.py:619
  87.1 112.4 %shard_map.246 = (bf16[784,512]{1,0:T(8,128)(2,1)}, f32[784,512]{1,0:T(8,128)}, f32[16,256]{1,0:T(8,128)}, f32[3,128,256]{2,1,0:T(8,128)}, f32[256,128]{1,0:T(8,...) custom-call(bf16[1568,1024]{1,0:T(8,128)(2,1)} %bitcast.30, bf16[1568,1024]{1,0:T(8,128)(2,1)} %bitcast.31, ...), custom_call_target="tpu_custom_call" | custom-call | tf_op jit(solution)/shard_map/pallas_call | solution.py:1235
  199.6 4.8 %shard_map.247 = (bf16[784,512]{1,0:T(8,128)(2,1)}, f32[784,512]{1,0:T(8,128)}, f32[3,128,256]{2,1,0:T(8,128)}, f32[256,128]{1,0:T(8,128)}, f32[128,1024]{1,0:T(...) custom-call(bf16[784,512]{1,0:T(8,128)(2,1)} %get-tuple-element.79.o, ...), custom_call_target="tpu_custom_call" | custom-call | tf_op jit(solution)/shard_map/pallas_call | solution.py:1279

commit v6 on v5

--- a/solution.py
+++ b/solution.py
@@ -308,7 +308,6 @@
 
         @pl.when(g == 3)
         def _():
-            start_weight(2)
             forward_weight(1, 1)
             send_cot(0)
             send_cot(1)
@@ -319,8 +318,8 @@
 
     for w in range(4):
         shard_loads[w].wait()
-    own_to_y(3).start()
     forward_weight(1, 2)
+    start_weight(2)
     finish_weight(0)
     last[0].start()
     last[4].start()
@@ -346,6 +345,10 @@
             own_to_y(2).start()
             finish_weight(1)
             out_x(slab).start()
+
+        @pl.when(i == 2)
+        def _():
+            own_to_y(3).start()
 
         @pl.when(i == 4)
         def _():
@@ -794,6 +797,11 @@
         oh[w][s] = (oh[w][s].astype(F32) + yr[w][s].astype(F32)).astype(BF16)
         gz(w, s).start()
 
+    stores = [
+        pltpu.make_async_copy(src, dst, store_sem.at[2, n, 0])
+        for n, (src, dst) in enumerate(((gin, gin_o), (gout, gout_o), (gexp, gexp_o), (gred, gred_o)))
+    ]
+
     def finish_grad(w, dst):
         gy(w, 3).wait()
         total = oh[w][3].astype(F32) + yr[w][3].astype(F32)
@@ -801,6 +809,7 @@
             gz(w, s).wait()
             total = total + zr[w][s].astype(F32)
         dst[...] = total
+        stores[w].start()
 
     loads["wr"].wait()
     loads["we"].wait()
@@ -1160,12 +1169,6 @@
     for step in range(7):
         packet_copy(step).start()
     finish_grad(0, gin)
-    stores = [
-        pltpu.make_async_copy(src, dst, store_sem.at[2, n, 0])
-        for n, (src, dst) in enumerate(((gin, gin_o), (gout, gout_o), (gexp, gexp_o), (gred, gred_o)))
-    ]
-    for copy in stores:
-        copy.start()
     total = packet[...]
     for step in range(7):
         packet_copy(step).wait()
@@ -1248,11 +1251,16 @@
     outs, vector_o, buffers = refs[:6], refs[6:14], refs[14:20]
     load_sem, store_sem = refs[20:]
     ins = (out_i, tg_i, gin_i, gout_i, gexp_i, gred_i)
-    loads = [pltpu.make_async_copy(a, b, load_sem.at[n]) for n, (a, b) in enumerate(zip(ins, buffers))]
-    stores = [pltpu.make_async_copy(a, b, store_sem.at[n]) for n, (a, b) in enumerate(zip(buffers, outs))]
-    order = (0, 2, 3, 4, 5, 1)
-    for n in order:
-        loads[n].start()
+    loads, stores = [], []
+    for n, parts in ((1, 2), (0, 1), (4, 1), (5, 1), (2, 1), (3, 1)):
+        size = ins[n].shape[0] // parts
+        for part in range(parts):
+            span = pl.ds(part * size, size)
+            slot = len(loads)
+            loads.append(pltpu.make_async_copy(ins[n].at[span], buffers[n].at[span], load_sem.at[slot]))
+            stores.append(pltpu.make_async_copy(buffers[n].at[span], outs[n].at[span], store_sem.at[slot]))
+    for copy in loads:
+        copy.start()
     first_gain, first_shift, attn, b_out, g_two, s_two, b_red, b_exp = vector_o
     first_gain[...] = sums_i[0:1, :]
     first_shift[...] = sums_i[1:2, :]
@@ -1264,11 +1272,11 @@
     for n in range(4):
         width = sums_i.shape[1]
         b_exp[:, n * width : (n + 1) * width] = sums_i[8 + n : 9 + n, :]
-    for n in order:
-        loads[n].wait()
-        stores[n].start()
-    for n in order:
-        stores[n].wait()
+    for load, store in zip(loads, stores):
+        load.wait()
+        store.start()
+    for store in stores:
+        store.wait()
 
 
 def finish_call(out, tg, sums, gin, gout, gexp, gred):
@@ -1281,7 +1289,7 @@
         out_shape=big + small,
         in_specs=[hbm, hbm, vm, hbm, hbm, hbm, hbm],
         out_specs=[hbm] * 6 + [vm] * 8,
-        scratch_shapes=[pltpu.VMEM(a.shape, a.dtype) for a in big] + [pltpu.SemaphoreType.DMA((6,))] * 2,
+        scratch_shapes=[pltpu.VMEM(a.shape, a.dtype) for a in big] + [pltpu.SemaphoreType.DMA((7,))] * 2,
     )(out, tg, sums, gin, gout, gexp, gred)
 
 

time: 205 us -> 203 us (level)
    pallas_call x1, Pallas kernels: 86.5 us -> 83.8 us  [forward_call(): pl.pallas_call(forward_kernel, out_shape=outs, in_specs=[pl.BlockSpec(mem...]
where the time goes in v6:
time: 203 us
  Pallas kernels  202 us (100%)
    pallas_call x1, Pallas kernels, backward_call(): pl.pallas_call(backward_kernel, out_shape=outs, in_specs=[pl.BlockSpec(me...  114 us
    pallas_call x1, Pallas kernels, forward_call(): pl.pallas_call(forward_kernel, out_shape=outs, in_specs=[pl.BlockSpec(mem...  83.8 us
    pallas_call x1, Pallas kernels, finish_call(): pl.pallas_call(finish_kernel, out_shape=big + small, in_specs=[hbm, hbm,...  4.53 us

profile of v6, /device:TPU:0, one launch (start us, length us, event | category | flops | bytes accessed | tf_op | source)
XLA Modules:
  0.0 203.0 jit_solution(11391686767156045574)
XLA Ops:
  0.7 83.8 %shard_map.245 = (bf16[7,224,1024]{2,1,0:T(8,128)(2,1)}, bf16[7,224,1024]{2,1,0:T(8,128)(2,1)}, bf16[7,224,256]{2,1,0:T(8,128)(2,1)}, bf16[7,256,224]{2,1,0:T(8,...) custom-call(bf16[784,512]{1,0:T(8,128)(2,1)} %tok.1, ...), custom_call_target="tpu_custom_call" | custom-call | tf_op jit(solution)/shard_map/pallas_call | solution.py:622
  84.4 113.8 %shard_map.246 = (bf16[784,512]{1,0:T(8,128)(2,1)}, f32[784,512]{1,0:T(8,128)}, f32[16,256]{1,0:T(8,128)}, f32[3,128,256]{2,1,0:T(8,128)}, f32[256,128]{1,0:T(8,...) custom-call(bf16[1568,1024]{1,0:T(8,128)(2,1)} %bitcast.30, bf16[1568,1024]{1,0:T(8,128)(2,1)} %bitcast.31, ...), custom_call_target="tpu_custom_call" | custom-call | tf_op jit(solution)/shard_map/pallas_call | solution.py:1238
  198.2 4.5 %shard_map.247 = (bf16[784,512]{1,0:T(8,128)(2,1)}, f32[784,512]{1,0:T(8,128)}, f32[3,128,256]{2,1,0:T(8,128)}, f32[256,128]{1,0:T(8,128)}, f32[128,1024]{1,0:T(...) custom-call(bf16[784,512]{1,0:T(8,128)(2,1)} %get-tuple-element.79.o, ...), custom_call_target="tpu_custom_call" | custom-call | tf_op jit(solution)/shard_map/pallas_call | solution.py:1287
